TPU v7x, 128 devices: a whole 4x4x4 slice. The times are simulated.
128 devices in a mesh: tm: 2 (over x_lo), gz: 8 (over y, x_hi), view: 8 (over z, core).
Axes of the slice: x: 4 (x_hi: 2, x_lo: 2; x = x_hi * 2 + x_lo), y: 4, z: 4, core: 2. Of those that a mesh axis runs over, the one named last changes fastest.
Arguments:
- sinogram: bfloat16 [2, 16, 1024, 2560], P(None, 'view', ('tm', 'gz')), may hold values from 102 to 358
- projector: bfloat16 [16, 1024, 2560], P('view'), may hold values from 0.0099487305 to 1
- warm_volume: float32 [1024, 1024], P(('tm', 'gz')), may hold values from 0.2 to 2.5, as said below
- view_order: int32 [2], replicated, may hold values from 0 to 1, each once
Outputs:
- volumes: float32 [2, 1024, 1024], P(None, ('tm', 'gz'))
Inputs may be any that keep to these rules, and one draw needn't show every extreme that they name: `view_order`: each local view number appears once. `warm_volume`: positive attenuation values.
All inputs are finite; a program needn't handle non-finite values.
Results may differ from a plain program's by a relative error of at most 0.0003.
Values may be sent and summed in bfloat16 or wider, within the bound.
No kernel may reach another device: no remote copies, remote signals or barrier semaphores. Data moves between devices by JAX's collectives and lax.ppermute only.
A program may use at most 64 MiB of HBM per device.

v0:
```python
import jax
import jax.numpy as jnp
from jax import lax
from jax.sharding import PartitionSpec as P

RY = 128
FRAMES = 2
SWEEPS = 3
TV_STEPS = 2


RELAXATION = 0.9
STEP_SCALE = 0.3
STEP_DECAY = 0.7
SMOOTHING = 0.01
NORM_GUARD = 1e-06


def copy_for_each(array, axis):
    devices = lax.axis_size(axis)
    return lax.all_to_all(
        jnp.broadcast_to(array[None], (devices, *array.shape)), axis, 0, 0, tiled=True
    )


def of_everyone(array, axis):
    everything = copy_for_each(array, axis)
    return jnp.sum(everything, axis=0)


def with_halo(array, sides, width):
    edges = {}
    for axis, dim in sides:
        devices, length = (lax.axis_size(axis), array.shape[dim])
        up = [(i, (i + 1) % devices) for i in range(devices - 1)]
        last = lax.slice_in_dim(array, length - width, length, axis=dim)
        initial = lax.slice_in_dim(array, 0, width, axis=dim)
        edges[dim] = (
            lax.ppermute(last, axis, up),
            lax.ppermute(initial, axis, [(b, a) for a, b in up]),
        )
    done = []
    for _, dim in sides:
        low, high = edges[dim]
        around = [(width, width) if d in done else (0, 0) for d in range(array.ndim)]
        array = jnp.concatenate([jnp.pad(low, around), array, jnp.pad(high, around)], axis=dim)
        done.append(dim)
    return array


def total_of_pieces(array, axis):
    return lax.all_gather(array, axis).sum(0)


def tv_gradient(volume, first_z, depth_total):
    row_count = volume.shape[0]
    pixels = volume.shape[1]
    zero_row = jnp.zeros((1, pixels), jnp.float32)
    zero_band = jnp.zeros((row_count, RY), jnp.float32)
    zero_col = jnp.zeros((row_count, 1), jnp.float32)
    zindex = first_z + jnp.arange(row_count, dtype=jnp.int32)
    inside = ((zindex >= 0) & (zindex < depth_total - 1)).astype(jnp.float32)
    diff_z = jnp.concatenate([volume[1:] - volume[:-1], zero_row], axis=0) * inside[:, None]
    diff_i = jnp.concatenate([volume[:, RY:] - volume[:, :-RY], zero_band], axis=1)
    column = jnp.arange(pixels, dtype=jnp.int32) % RY
    diff_j = jnp.concatenate([volume[:, 1:] - volume[:, :-1], zero_col], axis=1)
    diff_j = diff_j * (column < RY - 1).astype(jnp.float32)[None, :]
    magnitude = jnp.sqrt(diff_z * diff_z + diff_i * diff_i + diff_j * diff_j + SMOOTHING)
    flux_z = diff_z / magnitude
    flux_i = diff_i / magnitude
    flux_j = diff_j / magnitude
    gradient = jnp.concatenate([zero_row, flux_z[:-1]], axis=0) - flux_z
    gradient = gradient + (jnp.concatenate([zero_band, flux_i[:, :-RY]], axis=1) - flux_i)
    gradient = gradient + (jnp.concatenate([zero_col, flux_j[:, :-1]], axis=1) - flux_j)
    return gradient


def body(sinogram, projector, warm_volume, view_order):
    slices = warm_volume.shape[0]
    pixels = warm_volume.shape[1]
    per_view = projector.shape[0]
    ray_sums = jnp.sum(projector, axis=1, dtype=jnp.float32)
    coverage = of_everyone(jnp.sum(projector, axis=2, dtype=jnp.float32), "view")
    slab_count = lax.axis_size("tm") * lax.axis_size("gz")
    slab_index = lax.axis_index("tm") * lax.axis_size("gz") + lax.axis_index("gz")
    depth_total = slices * slab_count
    cell_count = depth_total * pixels
    rim_width = TV_STEPS

    def make_project(measured, slot_index):
        ray_tile = lax.dynamic_index_in_dim(projector, slot_index, 0, keepdims=False)
        ray_total = lax.dynamic_index_in_dim(ray_sums, slot_index, 0, keepdims=False)
        observed = lax.dynamic_index_in_dim(measured, slot_index, 0, keepdims=False)

        def project(piece_rows, first_row):
            forward = jnp.dot(piece_rows, ray_tile, preferred_element_type=jnp.float32)
            mismatch = ((observed.astype(jnp.float32) - forward) / ray_total[None, :]).astype(
                jnp.bfloat16
            )
            return lax.dot_general(
                mismatch, ray_tile, (((1,), (1,)), ((), ())), preferred_element_type=jnp.float32
            )

        return project

    first_slice = slab_index * slices
    current = warm_volume
    finished = []
    for frame_no in range(FRAMES):
        reconstruct_current = current
        reconstruct_measured = sinogram[frame_no]
        for sweep_no in range(SWEEPS):
            first_step = sweep_no * TV_STEPS
            row_count = reconstruct_current.shape[0]
            extended = with_halo(reconstruct_current, ((("tm", "gz"), 0),), rim_width)
            for step_no in range(TV_STEPS):
                gradient = tv_gradient(extended, first_slice - rim_width, depth_total)
                interior = lax.slice_in_dim(gradient, rim_width, rim_width + row_count, axis=0)
                spread = jnp.sqrt(
                    of_everyone(jnp.sum(interior * interior), ("tm", "gz")) / cell_count
                    + NORM_GUARD
                )
                extended = (
                    extended - STEP_SCALE * STEP_DECAY ** (first_step + step_no) * gradient / spread
                )
            reconstruct_current = lax.slice_in_dim(
                extended, rim_width, rim_width + row_count, axis=0
            )
            for subset in range(per_view):
                reconstruct_slot_index = view_order[subset]
                reconstruct_project = make_project(reconstruct_measured, reconstruct_slot_index)
                partial_back = reconstruct_project(reconstruct_current.astype(jnp.bfloat16), 0)
                summed = total_of_pieces(partial_back, "view")
                weight = lax.dynamic_index_in_dim(
                    coverage, reconstruct_slot_index, 0, keepdims=False
                )
                reconstruct_current = jnp.maximum(
                    reconstruct_current + RELAXATION * summed / weight[None, :], 0.0
                )
        current = reconstruct_current
        finished.append(current)
    volumes = jnp.stack(finished, axis=0)
    return volumes


def solution(mesh):
    return jax.shard_map(
        body,
        mesh=mesh,
        in_specs=(
            P(None, "view", ("tm", "gz"), None),
            P("view", None, None),
            P(("tm", "gz"), None),
            P(),
        ),
        out_specs=P(None, ("tm", "gz"), None),
        check_vma=False,
    )
```

profile of v0, /device:TPU:0, one launch (start us, length us, event | category | flops | bytes accessed | tf_op | source)
XLA Modules:
  0.0 688.0 jit_solution(16918986917550199975)
XLA Ops:
  15.0 7.6 %convert_reduce_fusion = (f32[2,1024]{1,0:T(2,128)S(1)}, f32[2,2560]{1,0:T(2,128)S(1)}) fusion(bf16[2,1024,2560]{2,1,0:T(8,128)(2,1)} %param.5), kind=kLoop, calls=%fused_computation | loop fusion | flops 15721472 | bytes 10514432 | tf_op jit(solution)/shard_map/reduce_sum | solution.py:83
  28.6 8.2 %all-to-all-start = ((f32[16,1,1]{2,1,0:T(1,128)}), f32[16,1,1]{2,1,0:T(1,128)S(1)}, u32[]{:S(2)}, u32[]{:S(2)}) async-start(f32[16,1,1]{2,1,0:T(1,128)} %broadcast_in_dim.26), calls=%async_computation | async-start | bytes 16384 | tf_op jit(solution)/shard_map/all_to_all | solution.py:21
  68.2 10.7 %all_to_all.77 = f32[8,2,1024]{2,1,0:T(2,128)S(1)} all-to-all(f32[8,2,1024]{2,1,0:T(2,128)S(1)} %broadcast_in_dim.28), channel_id=1, replica_groups=mesh['tm'=2,'gz'=8,'view'=8] {'view'}, dimensions={0} | all-to-all | bytes 131072 | tf_op jit(solution)/shard_map/all_to_all | solution.py:21
  79.0 13.4 %all-gather.25.cloned.1.call-done = f32[512,1024]{1,0:T(8,128)} async-done(((f32[64,1024]{1,0:T(8,128)}), f32[512,1024]{1,0:T(8,128)}) %all-gather.25.cloned.1.call-update) | async-done | bytes 2097168 | tf_op jit(solution)/shard_map/all_gather | solution.py:52
  94.2 7.4 %fusion.20 = f32[64,1024]{1,0:T(8,128)} fusion(bf16[2,1024,2560]{2,1,0:T(8,128)(2,1)} %param.5, s32[]{:T(128)S(6)} %select_n.113, f32[2560]{0:T(1024)S(1)} %get-tuple-element.8, bf16[1,2,64,2560]{3,2,1,0:T(8,128)(2,1)S(1)} %get-tuple-element.9, f32[64,1024]{1,0:T(8,128)S(1)} %slice_subtract_fusion.29, f32[64,1024]{1,0:T(8,128)S(1)} %reduce_sum.356, ...), kind=kOutput, calls=%fused_computation.22 | convolution fusion | flops 672071680 | bytes 11617792 | tf_op jit(solution)/shard_map/dot_general | solution.py:100
  101.7 25.9 %all-gather.27.cloned.1.call-done = f32[512,1024]{1,0:T(8,128)} async-done(((f32[64,1024]{1,0:T(8,128)}), f32[512,1024]{1,0:T(8,128)}) %all-gather.27.cloned.1.call-update) | async-done | bytes 2097168 | tf_op jit(solution)/shard_map/all_gather | solution.py:52
  143.4 13.9 %all_to_all.78 = f32[16,1,1]{2,1,0:T(1,128)S(1)} all-to-all(f32[16,1,1]{2,1,0:T(1,128)S(1)} %broadcast_in_dim.29), channel_id=1, replica_groups=mesh['tm'=2,'gz'=8,'view'=8] {'tm','gz'}, dimensions={0} | all-to-all | bytes 128 | tf_op jit(solution)/shard_map/all_to_all | solution.py:21
  160.7 10.8 %all_to_all.79 = f32[16,1,1]{2,1,0:T(1,128)S(1)} all-to-all(f32[16,1,1]{2,1,0:T(1,128)S(1)} %broadcast_in_dim.30), channel_id=1, replica_groups=mesh['tm'=2,'gz'=8,'view'=8] {'tm','gz'}, dimensions={0} | all-to-all | bytes 128 | tf_op jit(solution)/shard_map/all_to_all | solution.py:21
  172.9 7.4 %fusion.40 = f32[64,1024]{1,0:T(8,128)} fusion(bf16[2,1024,2560]{2,1,0:T(8,128)(2,1)} %param.5, s32[]{:T(128)S(6)} %select_n.112, f32[2560]{0:T(1024)S(1)} %get-tuple-element.7, bf16[1,2,64,2560]{3,2,1,0:T(8,128)(2,1)S(1)} %get-tuple-element.9, f32[64,1024]{1,0:T(8,128)S(1)} %slice_subtract_fusion.28), kind=kOutput, calls=%fused_computation.42 | convolution fusion | flops 671809536 | bytes 11351552 | tf_op jit(solution)/shard_map/dot_general | solution.py:100
  180.3 22.2 %all-gather.29.cloned.1.call-done = f32[512,1024]{1,0:T(8,128)} async-done(((f32[64,1024]{1,0:T(8,128)}), f32[512,1024]{1,0:T(8,128)}) %all-gather.29.cloned.1.call-update) | async-done | bytes 2097168 | tf_op jit(solution)/shard_map/all_gather | solution.py:52
  204.3 7.4 %fusion.16 = f32[64,1024]{1,0:T(8,128)} fusion(bf16[2,1024,2560]{2,1,0:T(8,128)(2,1)} %param.5, s32[]{:T(128)S(6)} %select_n.113, f32[2560]{0:T(1024)S(1)} %get-tuple-element.8, bf16[1,2,64,2560]{3,2,1,0:T(8,128)(2,1)S(1)} %get-tuple-element.9, f32[64,1024]{1,0:T(8,128)S(1)} %slice_subtract_fusion.28, f32[64,1024]{1,0:T(8,128)S(1)} %reduce_sum.364, ...), kind=kOutput, calls=%fused_computation.18 | convolution fusion | flops 672071680 | bytes 11617792 | tf_op jit(solution)/shard_map/dot_general | solution.py:100
  211.8 25.9 %all-gather.31.cloned.1.call-done = f32[512,1024]{1,0:T(8,128)} async-done(((f32[64,1024]{1,0:T(8,128)}), f32[512,1024]{1,0:T(8,128)}) %all-gather.31.cloned.1.call-update) | async-done | bytes 2097168 | tf_op jit(solution)/shard_map/all_gather | solution.py:52
  253.5 13.9 %all_to_all.80 = f32[16,1,1]{2,1,0:T(1,128)S(1)} all-to-all(f32[16,1,1]{2,1,0:T(1,128)S(1)} %broadcast_in_dim.31), channel_id=1, replica_groups=mesh['tm'=2,'gz'=8,'view'=8] {'tm','gz'}, dimensions={0} | all-to-all | bytes 128 | tf_op jit(solution)/shard_map/all_to_all | solution.py:21
  270.9 10.6 %all_to_all.81 = f32[16,1,1]{2,1,0:T(1,128)S(1)} all-to-all(f32[16,1,1]{2,1,0:T(1,128)S(1)} %broadcast_in_dim.32), channel_id=1, replica_groups=mesh['tm'=2,'gz'=8,'view'=8] {'tm','gz'}, dimensions={0} | all-to-all | bytes 128 | tf_op jit(solution)/shard_map/all_to_all | solution.py:21
  290.3 22.2 %all-gather.33.cloned.1.call-done = f32[512,1024]{1,0:T(8,128)} async-done(((f32[64,1024]{1,0:T(8,128)}), f32[512,1024]{1,0:T(8,128)}) %all-gather.33.cloned.1.call-update) | async-done | bytes 2097168 | tf_op jit(solution)/shard_map/all_gather | solution.py:52
  314.3 7.4 %fusion.12 = f32[64,1024]{1,0:T(8,128)} fusion(bf16[2,1024,2560]{2,1,0:T(8,128)(2,1)} %param.5, s32[]{:T(128)S(6)} %select_n.113, f32[2560]{0:T(1024)S(1)} %get-tuple-element.8, bf16[1,2,64,2560]{3,2,1,0:T(8,128)(2,1)S(1)} %get-tuple-element.9, f32[64,1024]{1,0:T(8,128)S(1)} %slice_subtract_fusion.27, f32[64,1024]{1,0:T(8,128)S(1)} %reduce_sum.370, ...), kind=kOutput, calls=%fused_computation.14 | convolution fusion | flops 672071680 | bytes 11617792 | tf_op jit(solution)/shard_map/dot_general | solution.py:100
  321.8 25.9 %all-gather.35.cloned.1.call-done = f32[512,1024]{1,0:T(8,128)} async-done(((f32[64,1024]{1,0:T(8,128)}), f32[512,1024]{1,0:T(8,128)}) %all-gather.35.cloned.1.call-update) | async-done | bytes 2097168 | tf_op jit(solution)/shard_map/all_gather | solution.py:52
  363.5 13.9 %all_to_all.82 = f32[16,1,1]{2,1,0:T(1,128)S(1)} all-to-all(f32[16,1,1]{2,1,0:T(1,128)S(1)} %broadcast_in_dim.33), channel_id=1, replica_groups=mesh['tm'=2,'gz'=8,'view'=8] {'tm','gz'}, dimensions={0} | all-to-all | bytes 128 | tf_op jit(solution)/shard_map/all_to_all | solution.py:21
  380.8 10.8 %all_to_all.83 = f32[16,1,1]{2,1,0:T(1,128)S(1)} all-to-all(f32[16,1,1]{2,1,0:T(1,128)S(1)} %broadcast_in_dim.34), channel_id=1, replica_groups=mesh['tm'=2,'gz'=8,'view'=8] {'tm','gz'}, dimensions={0} | all-to-all | bytes 128 | tf_op jit(solution)/shard_map/all_to_all | solution.py:21
  400.5 22.2 %all-gather.37.cloned.1.call-done = f32[512,1024]{1,0:T(8,128)} async-done(((f32[64,1024]{1,0:T(8,128)}), f32[512,1024]{1,0:T(8,128)}) %all-gather.37.cloned.1.call-update) | async-done | bytes 2097168 | tf_op jit(solution)/shard_map/all_gather | solution.py:52
  424.5 7.4 %fusion.8 = f32[64,1024]{1,0:T(8,128)} fusion(bf16[2,1024,2560]{2,1,0:T(8,128)(2,1)} %param.5, s32[]{:T(128)S(6)} %select_n.113, f32[2560]{0:T(1024)S(1)} %get-tuple-element.8, bf16[1,2,64,2560]{3,2,1,0:T(8,128)(2,1)S(1)} %get-tuple-element.10, f32[64,1024]{1,0:T(8,128)S(1)} %slice_subtract_fusion.26, f32[64,1024]{1,0:T(8,128)S(1)} %reduce_sum.376, ...), kind=kOutput, calls=%fused_computation.10 | convolution fusion | flops 672071680 | bytes 11617792 | tf_op jit(solution)/shard_map/dot_general | solution.py:100
  432.0 25.9 %all-gather.39.cloned.1.call-done = f32[512,1024]{1,0:T(8,128)} async-done(((f32[64,1024]{1,0:T(8,128)}), f32[512,1024]{1,0:T(8,128)}) %all-gather.39.cloned.1.call-update) | async-done | bytes 2097168 | tf_op jit(solution)/shard_map/all_gather | solution.py:52
  473.7 13.9 %all_to_all.84 = f32[16,1,1]{2,1,0:T(1,128)S(1)} all-to-all(f32[16,1,1]{2,1,0:T(1,128)S(1)} %broadcast_in_dim.35), channel_id=1, replica_groups=mesh['tm'=2,'gz'=8,'view'=8] {'tm','gz'}, dimensions={0} | all-to-all | bytes 128 | tf_op jit(solution)/shard_map/all_to_all | solution.py:21
  491.0 10.6 %all_to_all.85 = f32[16,1,1]{2,1,0:T(1,128)S(1)} all-to-all(f32[16,1,1]{2,1,0:T(1,128)S(1)} %broadcast_in_dim.36), channel_id=1, replica_groups=mesh['tm'=2,'gz'=8,'view'=8] {'tm','gz'}, dimensions={0} | all-to-all | bytes 128 | tf_op jit(solution)/shard_map/all_to_all | solution.py:21
  510.4 22.2 %all-gather.41.cloned.1.call-done = f32[512,1024]{1,0:T(8,128)} async-done(((f32[64,1024]{1,0:T(8,128)}), f32[512,1024]{1,0:T(8,128)}) %all-gather.41.cloned.1.call-update) | async-done | bytes 2097168 | tf_op jit(solution)/shard_map/all_gather | solution.py:52
  534.4 7.4 %fusion.4 = f32[64,1024]{1,0:T(8,128)} fusion(bf16[2,1024,2560]{2,1,0:T(8,128)(2,1)} %param.5, s32[]{:T(128)S(6)} %select_n.113, f32[2560]{0:T(1024)S(1)} %get-tuple-element.8, bf16[1,2,64,2560]{3,2,1,0:T(8,128)(2,1)S(1)} %get-tuple-element.10, f32[64,1024]{1,0:T(8,128)S(1)} %slice_subtract_fusion.25, f32[64,1024]{1,0:T(8,128)S(1)} %reduce_sum.382, ...), kind=kOutput, calls=%fused_computation.6 | convolution fusion | flops 672071680 | bytes 11617792 | tf_op jit(solution)/shard_map/dot_general | solution.py:100
  541.9 25.9 %all-gather.43.cloned.1.call-done = f32[512,1024]{1,0:T(8,128)} async-done(((f32[64,1024]{1,0:T(8,128)}), f32[512,1024]{1,0:T(8,128)}) %all-gather.43.cloned.1.call-update) | async-done | bytes 2097168 | tf_op jit(solution)/shard_map/all_gather | solution.py:52
  583.6 13.9 %all_to_all.86 = f32[16,1,1]{2,1,0:T(1,128)S(1)} all-to-all(f32[16,1,1]{2,1,0:T(1,128)S(1)} %broadcast_in_dim.37), channel_id=1, replica_groups=mesh['tm'=2,'gz'=8,'view'=8] {'tm','gz'}, dimensions={0} | all-to-all | bytes 128 | tf_op jit(solution)/shard_map/all_to_all | solution.py:21
  601.0 10.9 %all_to_all.87 = f32[16,1,1]{2,1,0:T(1,128)S(1)} all-to-all(f32[16,1,1]{2,1,0:T(1,128)S(1)} %broadcast_in_dim.38), channel_id=1, replica_groups=mesh['tm'=2,'gz'=8,'view'=8] {'tm','gz'}, dimensions={0} | all-to-all | bytes 128 | tf_op jit(solution)/shard_map/all_to_all | solution.py:21
  620.7 22.2 %all-gather.45.cloned.1.call-done = f32[512,1024]{1,0:T(8,128)} async-done(((f32[64,1024]{1,0:T(8,128)}), f32[512,1024]{1,0:T(8,128)}) %all-gather.45.cloned.1.call-update) | async-done | bytes 2097168 | tf_op jit(solution)/shard_map/all_gather | solution.py:52
  644.6 7.4 %fusion = f32[64,1024]{1,0:T(8,128)} fusion(bf16[2,1024,2560]{2,1,0:T(8,128)(2,1)} %param.5, s32[]{:T(128)S(6)} %select_n.113, f32[2560]{0:T(1024)S(1)} %get-tuple-element.8, bf16[1,2,64,2560]{3,2,1,0:T(8,128)(2,1)S(1)} %get-tuple-element.10, f32[64,1024]{1,0:T(8,128)S(1)} %slice_subtract_fusion.24, f32[64,1024]{1,0:T(8,128)S(1)} %reduce_sum.388, ...), kind=kOutput, calls=%fused_computation.2 | convolution fusion | flops 672071680 | bytes 11617792 | tf_op jit(solution)/shard_map/dot_general | solution.py:100
  652.1 25.9 %all-gather.47.cloned.1.call-done = f32[512,1024]{1,0:T(8,128)} async-done(((f32[64,1024]{1,0:T(8,128)}), f32[512,1024]{1,0:T(8,128)}) %all-gather.47.cloned.1.call-update) | async-done | bytes 2097168 | tf_op jit(solution)/shard_map/all_gather | solution.py:52
  (219 shorter events, 179.1 us)
Async XLA Ops:
  7.3 18.7 %collective-permute-start = (f32[2,1024]{1,0:T(2,128)S(1)}, f32[2,1024]{1,0:T(2,128)S(1)}, u32[]{:S(2)}, u32[]{:S(2)}) collective-permute-start(f32[2,1024]{1,0:T(2,128)S(1)} %get-tuple-element.57), channel_id=1, source_target_pairs={{0,8},{8,16},{16,24},{24,32},{32,40},{40,48},{48,56},{56,64},{64,7... | collective-permute-start | bytes 24584 | tf_op jit(solution)/shard_map/ppermute | solution.py:39
  12.4 13.7 %collective-permute-start.1 = (f32[2,1024]{1,0:T(2,128)S(1)}, f32[2,1024]{1,0:T(2,128)S(1)}, u32[]{:S(2)}, u32[]{:S(2)}) collective-permute-start(f32[2,1024]{1,0:T(2,128)S(1)} %get-tuple-element.58), channel_id=1, source_target_pairs={{8,0},{16,8},{24,16},{32,24},{40,32},{48,40},{56,48},{64,56},{72,6... | collective-permute-start | bytes 24584 | tf_op jit(solution)/shard_map/ppermute | solution.py:40
  15.0 7.6 %copy-start = (bf16[2,2,64,2560]{3,2,1,0:T(8,128)(2,1)S(1)}, bf16[2,2,64,2560]{3,2,1,0:T(8,128)(2,1)}, u32[]{:S(2)}) copy-start(bf16[2,2,64,2560]{3,2,1,0:T(8,128)(2,1)} %param.4) | copy-start | bytes 3932164
  15.0 11.1 %copy-start.1 = (f32[64,1024]{1,0:T(8,128)S(1)}, f32[64,1024]{1,0:T(8,128)}, u32[]{:S(2)}) copy-start(f32[64,1024]{1,0:T(8,128)} %param.6) | copy-start | bytes 786436
  28.6 15.7 %all-to-all-start = ((f32[16,1,1]{2,1,0:T(1,128)}), f32[16,1,1]{2,1,0:T(1,128)S(1)}, u32[]{:S(2)}, u32[]{:S(2)}) async-start(f32[16,1,1]{2,1,0:T(1,128)} %broadcast_in_dim.26), calls=%async_computation | async-start | bytes 16384 | tf_op jit(solution)/shard_map/all_to_all | solution.py:21
  48.5 10.9 %all-to-all-start.1 = ((f32[16,1,1]{2,1,0:T(1,128)}), f32[16,1,1]{2,1,0:T(1,128)S(1)}, u32[]{:S(2)}, u32[]{:S(2)}) async-start(f32[16,1,1]{2,1,0:T(1,128)} %broadcast_in_dim.27), calls=%async_computation.1 | async-start | bytes 16384 | tf_op jit(solution)/shard_map/all_to_all | solution.py:21
  51.9 40.5 %all-gather.25.cloned.1.call-start = ((), (), s32[]{:S(2)}) async-start(), calls=%async_computation.13 | async-start | bytes 2359296 | tf_op jit(solution)/shard_map/all_gather | solution.py:52
  68.2 59.4 %all-gather.27.cloned.1.call-start = ((), (), s32[]{:S(2)}) async-start(), calls=%async_computation.14 | async-start | bytes 2359296 | tf_op jit(solution)/shard_map/all_gather | solution.py:52
  101.6 101.0 %all-gather.29.cloned.1.call-start = ((), (), s32[]{:S(2)}) async-start(), calls=%async_computation.15 | async-start | bytes 2359296 | tf_op jit(solution)/shard_map/all_gather | solution.py:52
  129.4 6.2 collective-permute-start.2
  134.3 7.0 %collective-permute-start.3 = (f32[2,1024]{1,0:T(2,128)S(1)}, f32[2,1024]{1,0:T(2,128)S(1)}, u32[]{:S(2)}, u32[]{:S(2)}) collective-permute-start(f32[2,1024]{1,0:T(2,128)S(1)} %get-tuple-element.56), channel_id=1, source_target_pairs={{8,0},{16,8},{24,16},{32,24},{40,32},{48,40},{56,48},{64,56},{72,6... | collective-permute-start | bytes 24584 | tf_op jit(solution)/shard_map/ppermute | solution.py:40
  180.3 57.4 %all-gather.31.cloned.1.call-start = ((), (), s32[]{:S(2)}) async-start(), calls=%async_computation.16 | async-start | bytes 2359296 | tf_op jit(solution)/shard_map/all_gather | solution.py:52
  211.8 100.7 %all-gather.33.cloned.1.call-start = ((), (), s32[]{:S(2)}) async-start(), calls=%async_computation.17 | async-start | bytes 2359296 | tf_op jit(solution)/shard_map/all_gather | solution.py:52
  239.5 6.2 collective-permute-start.4
  244.4 7.0 %collective-permute-start.5 = (f32[2,1024]{1,0:T(2,128)S(1)}, f32[2,1024]{1,0:T(2,128)S(1)}, u32[]{:S(2)}, u32[]{:S(2)}) collective-permute-start(f32[2,1024]{1,0:T(2,128)S(1)} %get-tuple-element.54), channel_id=1, source_target_pairs={{8,0},{16,8},{24,16},{32,24},{40,32},{48,40},{56,48},{64,56},{72,6... | collective-permute-start | bytes 24584 | tf_op jit(solution)/shard_map/ppermute | solution.py:40
  290.2 57.4 %all-gather.35.cloned.1.call-start = ((), (), s32[]{:S(2)}) async-start(), calls=%async_computation.18 | async-start | bytes 2359296 | tf_op jit(solution)/shard_map/all_gather | solution.py:52
  321.7 101.0 %all-gather.37.cloned.1.call-start = ((), (), s32[]{:S(2)}) async-start(), calls=%async_computation.19 | async-start | bytes 2359296 | tf_op jit(solution)/shard_map/all_gather | solution.py:52
  349.5 6.2 collective-permute-start.6
  354.4 7.0 %collective-permute-start.7 = (f32[2,1024]{1,0:T(2,128)S(1)}, f32[2,1024]{1,0:T(2,128)S(1)}, u32[]{:S(2)}, u32[]{:S(2)}) collective-permute-start(f32[2,1024]{1,0:T(2,128)S(1)} %get-tuple-element.52), channel_id=1, source_target_pairs={{8,0},{16,8},{24,16},{32,24},{40,32},{48,40},{56,48},{64,56},{72,6... | collective-permute-start | bytes 24584 | tf_op jit(solution)/shard_map/ppermute | solution.py:40
  400.4 57.4 %all-gather.39.cloned.1.call-start = ((), (), s32[]{:S(2)}) async-start(), calls=%async_computation.20 | async-start | bytes 2359296 | tf_op jit(solution)/shard_map/all_gather | solution.py:52
  431.9 100.7 %all-gather.41.cloned.1.call-start = ((), (), s32[]{:S(2)}) async-start(), calls=%async_computation.21 | async-start | bytes 2359296 | tf_op jit(solution)/shard_map/all_gather | solution.py:52
  459.7 6.2 collective-permute-start.8
  464.6 7.0 %collective-permute-start.9 = (f32[2,1024]{1,0:T(2,128)S(1)}, f32[2,1024]{1,0:T(2,128)S(1)}, u32[]{:S(2)}, u32[]{:S(2)}) collective-permute-start(f32[2,1024]{1,0:T(2,128)S(1)} %get-tuple-element.50), channel_id=1, source_target_pairs={{8,0},{16,8},{24,16},{32,24},{40,32},{48,40},{56,48},{64,56},{72,6... | collective-permute-start | bytes 24584 | tf_op jit(solution)/shard_map/ppermute | solution.py:40
  510.4 57.4 %all-gather.43.cloned.1.call-start = ((), (), s32[]{:S(2)}) async-start(), calls=%async_computation.22 | async-start | bytes 2359296 | tf_op jit(solution)/shard_map/all_gather | solution.py:52
  541.9 101.0 %all-gather.45.cloned.1.call-start = ((), (), s32[]{:S(2)}) async-start(), calls=%async_computation.23 | async-start | bytes 2359296 | tf_op jit(solution)/shard_map/all_gather | solution.py:52
  569.6 6.2 collective-permute-start.10
  574.5 7.0 %collective-permute-start.11 = (f32[2,1024]{1,0:T(2,128)S(1)}, f32[2,1024]{1,0:T(2,128)S(1)}, u32[]{:S(2)}, u32[]{:S(2)}) collective-permute-start(f32[2,1024]{1,0:T(2,128)S(1)} %get-tuple-element.48), channel_id=1, source_target_pairs={{8,0},{16,8},{24,16},{32,24},{40,32},{48,40},{56,48},{64,56},{72,6... | collective-permute-start | bytes 24584 | tf_op jit(solution)/shard_map/ppermute | solution.py:40
  620.6 57.4 %all-gather.47.cloned.1.call-start = ((), (), s32[]{:S(2)}) async-start(), calls=%async_computation.24 | async-start | bytes 2359296 | tf_op jit(solution)/shard_map/all_gather | solution.py:52
Sparse Core Ops, SparseCore 0:
  68.3 24.0 all-gather.24
  101.7 25.7 all-gather.26
  180.4 22.1 all-gather.28
  211.9 25.7 all-gather.30
  290.4 22.0 all-gather.32
  321.8 25.7 all-gather.34
  400.6 22.1 all-gather.36
  432.0 25.7 all-gather.38
  510.5 22.0 all-gather.40
  542.0 25.7 all-gather.42
  620.7 22.1 all-gather.44
  652.2 25.7 all-gather.46
where the time goes:
time: 699 us; the launch traced here: 688 us
  waiting for transfers between devices  323 us (46%)
  blocking collectives  134 us (19%)
  matrix products  88.9 us (13%)
  other arithmetic  54 us (8%)
  starting transfers between devices  49.3 us (7%)
  between operations  27.5 us (4%)
  local copies, waits for them, and re-layouts  11.5 us (2%)
    all_gather x12, waiting for transfers between devices, total_of_pieces(): return lax.all_gather(array, axis).sum(0)  280 us
    all_to_all x11, blocking collectives, copy_for_each(): lax.all_to_all(jnp.broadcast_to(array[None], (devices, *array.shape)), ax...  134 us
    dot_general x12, matrix products, project(): lax.dot_general(mismatch, ray_tile, (((1,), (1,)), ((), ())), preferred_e...  88.9 us
    ppermute x6, starting transfers between devices, with_halo(): lax.ppermute(last, axis, up)  29.4 us
    ppermute x6, waiting for transfers between devices, with_halo(): lax.ppermute(initial, axis, [(b, a) for a, b in up])  28.5 us
    reduce_sum x12, other arithmetic, total_of_pieces(): return lax.all_gather(array, axis).sum(0)  20.9 us
    all_to_all x2, waiting for transfers between devices, copy_for_each(): lax.all_to_all(jnp.broadcast_to(array[None], (devices, *array.shape)), ax...  14.2 us
  transfers between devices with their start and end apart: 26, of which 19 were waited for; matrix products, arithmetic and copies ran while one was open for 1% of the time, Pallas kernels for 0%

commit v1 on v0

v1 whole, which is shorter than its diff:
```python
import functools

import jax
import jax.numpy as jnp
from jax import lax
from jax.experimental import pallas as pl
from jax.experimental.pallas import tpu as pltpu
from jax.sharding import PartitionSpec as P

RY = 128
FRAMES = 2
SWEEPS = 3
TV_STEPS = 2
VIEW = 8
HALO = 16
CHUNK = 256

RELAXATION = 0.9
STEP_SCALE = 0.3
STEP_DECAY = 0.7
SMOOTHING = 0.01
NORM_GUARD = 1e-06

F32 = jnp.float32
BF16 = jnp.bfloat16
VMEM = pl.BlockSpec(memory_space=pltpu.VMEM)
SMEM = pl.BlockSpec(memory_space=pltpu.SMEM)


def params(**kw):
    return pltpu.CompilerParams(vmem_limit_bytes=56 * 1024 * 1024, **kw)


def gram_kernel(order_ref, slab_ref, a_ref, s0_ref, s1_ref, out_ref, acc):
    n = pl.program_id(0)
    d = pl.program_id(1)
    rows = s0_ref.shape[0]
    part = rows // VIEW
    tile = a_ref[...]
    ray = jnp.sum(tile.astype(F32), axis=0, keepdims=True)
    inverse = 1.0 / ray
    lhs = []
    low = []
    for ref in (s0_ref, s1_ref):
        scaled = ref[...].astype(F32) * inverse
        high = scaled.astype(BF16)
        lhs.append(high)
        low.append((scaled - high.astype(F32)).astype(BF16))
    mine = a_ref[pl.ds(pl.multiple_of(slab_ref[0] * rows, rows), rows), :]
    lhs.append((mine.astype(F32) * inverse).astype(BF16))
    lhs.append(jnp.ones((16, CHUNK), BF16))
    stack = jnp.concatenate(lhs + low, axis=0)
    product = lax.dot_general(stack, tile, (((1,), (1,)), ((), ())), preferred_element_type=F32)
    top = 3 * rows + 16

    @pl.when(d == 0)
    def _():
        acc[...] = product

    @pl.when(d > 0)
    def _():
        acc[...] += product

    @pl.when(d == pl.num_programs(1) - 1)
    def _():
        b0 = acc[0:rows] + acc[top : top + rows]
        b1 = acc[rows : 2 * rows] + acc[top + rows : top + 2 * rows]
        for v in range(VIEW):
            where = pl.ds(v * part, part)
            out_ref[v, pl.ds(pl.multiple_of(n * part, part), part), :] = b0[v * part : (v + 1) * part]
            out_ref[v, pl.ds(pl.multiple_of((2 + n) * part, part), part), :] = b1[
                v * part : (v + 1) * part
            ]

        wide = 2 * part
        for quarter in range(VIEW // 2):
            for half in range(2):
                @pl.when(n == half)
                def _():
                    out_ref[2 * quarter + half, 4 * part : 4 * part + wide, :] = acc[
                        2 * rows + quarter * wide : 2 * rows + (quarter + 1) * wide
                    ]
        for half in range(2):
            @pl.when(n == half)
            def _():
                row = acc[3 * rows : 3 * rows + 1]
                for v in range(VIEW):
                    out_ref[v, 6 * part + half : 6 * part + half + 1, :] = row


def gram_products(order, slab, projector, measured):
    _, pixels, det = projector.shape
    rows = measured.shape[2]
    part = rows // VIEW
    total = 5 * rows + 16
    out_rows = 7 * part
    return pl.pallas_call(
        gram_kernel,
        out_shape=jax.ShapeDtypeStruct((VIEW, out_rows, pixels), F32),
        grid_spec=pltpu.PrefetchScalarGridSpec(
            num_scalar_prefetch=2,
            grid=(2, det // CHUNK),
            in_specs=[
                pl.BlockSpec((None, pixels, CHUNK), lambda n, d, o, s: (o[n], 0, d)),
                pl.BlockSpec((None, None, rows, CHUNK), lambda n, d, o, s: (0, o[n], 0, d)),
                pl.BlockSpec((None, None, rows, CHUNK), lambda n, d, o, s: (1, o[n], 0, d)),
            ],
            out_specs=pl.BlockSpec((VIEW, out_rows, pixels), lambda n, d, o, s: (0, 0, 0)),
            scratch_shapes=[pltpu.VMEM((total, pixels), F32)],
        ),
        compiler_params=params(),
        name="gram_products",
    )(order, slab, projector, measured, measured)


def reduce_kernel(core_ref, got_ref, b_ref, g_ref, cov_ref):
    part = 8
    total = got_ref[0]
    for v in range(1, VIEW):
        total = total + got_ref[v]
    cov = total[6 * part : 6 * part + 2]
    scale = RELAXATION / cov
    b_ref[0] = total[0:part] * scale[0:1]
    b_ref[1] = total[part : 2 * part] * scale[1:2]
    b_ref[2] = total[2 * part : 3 * part] * scale[0:1]
    b_ref[3] = total[3 * part : 4 * part] * scale[1:2]
    gram = total[4 * part : 6 * part]
    mine = jnp.where(core_ref[0] == 0, cov[0:1], cov[1:2])
    own = jnp.sum(gram, axis=1, keepdims=True)
    weight = jnp.sum(mine, axis=1, keepdims=True)
    g_ref[...] = (gram - own * (mine / weight)).astype(BF16)
    cov_ref[...] = total[6 * part : 7 * part]


def reduce_views(core, got):
    pixels = got.shape[-1]
    return pl.pallas_call(
        reduce_kernel,
        out_shape=(
            jax.ShapeDtypeStruct((4, 8, pixels), F32),
            jax.ShapeDtypeStruct((16, pixels), BF16),
            jax.ShapeDtypeStruct((8, pixels), F32),
        ),
        in_specs=[SMEM, VMEM],
        out_specs=(VMEM, VMEM, VMEM),
        compiler_params=params(),
        name="reduce_views",
    )(core, got)


def tv_into(x_ref, g_ref, ss_ref, first, depth):
    height, pixels = x_ref.shape
    blocks = pixels // RY
    lane = lax.broadcasted_iota(jnp.int32, (height, RY), 1)
    zindex = first + lax.broadcasted_iota(jnp.int32, (height, RY), 0)
    inside = ((zindex >= 0) & (zindex < depth - 1)).astype(F32)
    column = (lane < RY - 1).astype(F32)
    before = None
    total = None
    here = x_ref[:, 0:RY]
    for i in range(blocks):
        dz = (pltpu.roll(here, height - 1, 0) - here) * inside
        dc = (pltpu.roll(here, RY - 1, 1) - here) * column
        square = dz * dz + dc * dc + SMOOTHING
        if i < blocks - 1:
            following = x_ref[:, (i + 1) * RY : (i + 2) * RY]
            di = following - here
            square = square + di * di
        r = lax.rsqrt(square)
        r = r * (1.5 - 0.5 * square * r * r)
        fz = dz * r
        fc = dc * r
        g = (pltpu.roll(fz, 1, 0) - fz) + (pltpu.roll(fc, 1, 1) - fc)
        if i < blocks - 1:
            fi = di * r
            g = g - fi
        if before is not None:
            g = g + before
        g_ref[:, i * RY : (i + 1) * RY] = g
        inner = g[HALO : height - HALO]
        piece = inner * inner
        total = piece if total is None else total + piece
        if i < blocks - 1:
            before = fi
            here = following
    folded = total[0:8]
    for k in range(1, total.shape[0] // 8):
        folded = folded + total[8 * k : 8 * k + 8]
    for k in range(ss_ref.shape[0]):
        ss_ref[k] = folded


def descend(x, g, sums, step, cells):
    total = jnp.sum(jnp.sum(sums, axis=0), axis=(0, 1), keepdims=True)
    spread = jnp.sqrt(total / cells + NORM_GUARD)
    return x - (STEP_SCALE * STEP_DECAY**step) * (g / spread)


def first_kernel(meta_ref, x_ref, g_ref, ss_ref, *, depth):
    tv_into(x_ref, g_ref, ss_ref, meta_ref[0], depth)


def second_kernel(meta_ref, x_ref, g_ref, sums_ref, x_out, g_out, ss_out, *, depth, step, cells):
    x_out[...] = descend(x_ref[...], g_ref[...], sums_ref[...], step, cells)
    tv_into(x_out, g_out, ss_out, meta_ref[0], depth)


def subset_kernel(
    meta_ref, x_ref, g_ref, sums_ref, gram_ref, b_ref, cov_ref, *outs, depth, step, cells, frame, last, final
):
    x = descend(x_ref[...], g_ref[...], sums_ref[...], step, cells)
    for n in range(2):
        rounded = x.astype(BF16)
        product = jnp.dot(rounded, gram_ref[n], preferred_element_type=F32)
        cov = cov_ref[n : n + 1, :]
        weight = jnp.sum(cov, axis=1, keepdims=True)
        along = jnp.sum(rounded.astype(F32) * cov, axis=1, keepdims=True)
        change = b_ref[2 * frame + n] - product * (RELAXATION / cov) - along * (RELAXATION / weight)
        x = jnp.maximum(x + change, 0.0)
    outs = list(outs)
    if last:
        volume_out = outs.pop(0)
        volume_out[...] = x[HALO : x.shape[0] - HALO]
    if not final:
        x_out, g_out, ss_out = outs
        x_out[...] = x
        tv_into(x_out, g_out, ss_out, meta_ref[0], depth)


def body(sinogram, projector, warm_volume, view_order):
    slices, pixels = warm_volume.shape
    slab_axes = ("tm", "gz")
    slabs = lax.axis_size("tm") * lax.axis_size("gz")
    slab = (lax.axis_index("tm") * lax.axis_size("gz") + lax.axis_index("gz")).astype(jnp.int32)
    view = lax.axis_index("view").astype(jnp.int32)
    depth = slices * slabs
    cells = depth * pixels
    height = slices + 2 * HALO
    meta = (slab * slices - HALO).reshape(1)

    up = [(i, i + 1) for i in range(slabs - 1)]
    down = [(b, a) for a, b in up]

    def widen(array, dim):
        length = array.shape[dim]
        low = lax.ppermute(lax.slice_in_dim(array, length - HALO, length, axis=dim), slab_axes, up)
        high = lax.ppermute(lax.slice_in_dim(array, 0, HALO, axis=dim), slab_axes, down)
        return jnp.concatenate([low, array, high], axis=dim)

    partial = gram_products(view_order, slab.reshape(1), projector, sinogram)
    got = lax.all_to_all(partial, "view", 0, 0, tiled=True)
    b_part, g_part, cov = reduce_views((view % 2).reshape(1), got)

    b_all = lax.all_to_all(
        jnp.broadcast_to(b_part[None], (VIEW, *b_part.shape)), "view", 0, 0, tiled=False
    )
    b_all = b_all.transpose(1, 0, 2, 3).reshape(4, slices, pixels)
    b_wide = widen(b_all, 1)

    lines = [g_part]
    for hop in (2, 4, 6):
        lines.append(lax.ppermute(g_part, "view", [(i, (i + hop) % VIEW) for i in range(VIEW)]))
    z = view // 2
    stack = jnp.stack(lines)
    stack = jnp.take(stack, (z - jnp.arange(4)) % 4, axis=0)
    strip = stack.reshape(slices, pixels)
    whole = lax.all_to_all(
        jnp.broadcast_to(strip[None], (slabs, *strip.shape)), slab_axes, 0, 0, tiled=True
    )
    mine = whole.reshape(depth, pixels)
    other = lax.ppermute(mine, "view", [(i, i ^ 1) for i in range(VIEW)])
    core = view % 2
    gram = jnp.stack([jnp.where(core == 0, mine, other), jnp.where(core == 0, other, mine)])

    shape = jax.ShapeDtypeStruct((height, pixels), F32)
    sums_shape = jax.ShapeDtypeStruct((slabs, 8, RY), F32)

    def everyone(sums):
        return lax.all_to_all(sums, slab_axes, 0, 0, tiled=True)

    x = widen(warm_volume, 0)
    g, sums = pl.pallas_call(
        functools.partial(first_kernel, depth=depth),
        out_shape=(shape, sums_shape),
        in_specs=[SMEM, VMEM],
        out_specs=(VMEM, VMEM),
        compiler_params=params(),
        name="first",
    )(meta, x)
    finished = []
    for frame in range(FRAMES):
        for sweep in range(SWEEPS):
            step = sweep * TV_STEPS
            x, g, sums = pl.pallas_call(
                functools.partial(second_kernel, depth=depth, step=step, cells=cells),
                out_shape=(shape, shape, sums_shape),
                in_specs=[SMEM, VMEM, VMEM, VMEM],
                out_specs=(VMEM, VMEM, VMEM),
                compiler_params=params(),
                name="second",
            )(meta, x, g, everyone(sums))
            last = sweep == SWEEPS - 1
            final = last and frame == FRAMES - 1
            out_shape = ()
            if last:
                out_shape += (jax.ShapeDtypeStruct((slices, pixels), F32),)
            if not final:
                out_shape += (shape, shape, sums_shape)
            outs = pl.pallas_call(
                functools.partial(
                    subset_kernel,
                    depth=depth,
                    step=step + 1,
                    cells=cells,
                    frame=frame,
                    last=last,
                    final=final,
                ),
                out_shape=out_shape,
                in_specs=[SMEM] + [VMEM] * 6,
                out_specs=tuple(VMEM for _ in out_shape),
                compiler_params=params(),
                name="subset",
            )(meta, x, g, everyone(sums), gram, b_wide, cov)
            outs = list(outs)
            if last:
                finished.append(outs.pop(0))
            if not final:
                x, g, sums = outs
    return jnp.stack(finished, axis=0)


def solution(mesh):
    return jax.shard_map(
        body,
        mesh=mesh,
        in_specs=(
            P(None, "view", ("tm", "gz"), None),
            P("view", None, None),
            P(("tm", "gz"), None),
            P(),
        ),
        out_specs=P(None, ("tm", "gz"), None),
        check_vma=False,
    )
```

time: 699 us -> 326 us (0.47); the launches traced: 688 us -> 324 us
  waiting for transfers between devices: 323 us -> 46.3 us
  matrix products: 88.9 us -> 0 us
  Pallas kernels: 0 us -> 69.9 us
  other arithmetic: 54 us -> 9.19 us
  between operations: 27.5 us -> 0.17 us
  blocking collectives: 134 us -> 155 us
  starting transfers between devices: 49.3 us -> 34 us
    all_gather x12 -> x0, waiting for transfers between devices: 280 us -> none  [total_of_pieces(): return lax.all_gather(array, axis).sum(0)]
    dot_general x12 -> x0, matrix products: 88.9 us -> none  [project(): lax.dot_general(mismatch, ray_tile, (((1,), (1,)), ((), ())), preferred_e...]
    pallas_call x0 -> x15, Pallas kernels: none -> 69.9 us  [the longest x6 30.2 us: body(): pl.pallas_call(functools.partial(subset_kernel, depth=depth, step=step +...]
    reduce_sum x38 -> x0, other arithmetic: 44 us -> none  [the longest x12 20.9 us: total_of_pieces(): return lax.all_gather(array, axis).sum(0)]
    all_to_all x2 -> x4, waiting for transfers between devices: 14.2 us -> 42.3 us  [the longest x1 24.3 us: body(): got = lax.all_to_all(partial, 'view', 0, 0, tiled=True)]
    ppermute x12 -> x8, waiting for transfers between devices: 28.7 us -> 3.97 us  [the longest x3 3.33 us: body(): lax.ppermute(g_part, 'view', [(i, (i + hop) % VIEW) for i in range(VIEW)])]
    ppermute x12 -> x8, starting transfers between devices: 37.2 us -> 15.3 us  [the longest x2 9.5 us: widen(): lax.ppermute(lax.slice_in_dim(array, length - HALO, length, axis=dim), sl...]
    all_to_all x11, blocking collectives: 134 us -> 155 us  [the longest x10 121 us: everyone(): return lax.all_to_all(sums, slab_axes, 0, 0, tiled=True)]
  transfers between devices with their start and end apart: 26 -> 12, of which waited for: 19 -> 8; matrix products, arithmetic and copies ran while one was open for 1% -> 4% of each run, Pallas kernels for 0% -> 1%
where the time goes in v1:
time: 326 us; the launch traced here: 324 us
  blocking collectives  155 us (48%)
  Pallas kernels  69.9 us (21%)
  waiting for transfers between devices  46.3 us (14%)
  starting transfers between devices  34 us (10%)
  local copies, waits for them, and re-layouts  9.95 us (3%)
  other arithmetic  9.19 us (3%)
    all_to_all x10, blocking collectives, everyone(): return lax.all_to_all(sums, slab_axes, 0, 0, tiled=True)  121 us
    all_to_all x1, blocking collectives, body(): lax.all_to_all(jnp.broadcast_to(strip[None], (slabs, *strip.shape)), slab...  33.6 us
    pallas_call x6, Pallas kernels, body(): pl.pallas_call(functools.partial(subset_kernel, depth=depth, step=step +...  30.2 us
    all_to_all x1, waiting for transfers between devices, body(): got = lax.all_to_all(partial, 'view', 0, 0, tiled=True)  24.3 us
    pallas_call x1, Pallas kernels, gram_products(): pl.pallas_call(gram_kernel, out_shape=jax.ShapeDtypeStruct((VIEW, out_row...  19.9 us
    pallas_call x6, Pallas kernels, body(): pl.pallas_call(functools.partial(second_kernel, depth=depth, step=step, c...  15.3 us
    ppermute x2, starting transfers between devices, widen(): lax.ppermute(lax.slice_in_dim(array, length - HALO, length, axis=dim), sl...  9.5 us
    all_to_all x2, waiting for transfers between devices, everyone(): return lax.all_to_all(sums, slab_axes, 0, 0, tiled=True)  9.04 us
  transfers between devices with their start and end apart: 12, of which 8 were waited for; matrix products, arithmetic and copies ran while one was open for 4% of the time, Pallas kernels for 1%

profile of v1, /device:TPU:0, one launch (start us, length us, event | category | flops | bytes accessed | tf_op | source)
XLA Modules:
  0.0 324.4 jit_solution(7744957807943161260)
XLA Ops:
  0.0 19.9 %gram_products.1 = f32[8,56,1024]{2,1,0:T(8,128)} custom-call(s32[2]{0:T(128)} %order_ref.1, s32[1]{0:T(128)} %bitcast.2.slab_ref, bf16[2,1024,2560]{2,1,0:T(8,128)(2,1)} %a_ref.1, bf16[2,2,64,2560]{3,2,1,0:T(8,128)(2,1)} %s1_ref.1, bf16[2,2,64,2560]{3,2,1,0:T(8,128)(2,1)} %s1_ref.1), custom_call_target="tpu_custom_call" | custom-call | tf_op jit(solution)/shard_map/gram_products/pallas_call | solution.py:97
  19.9 5.4 %all-to-all-start.2 = ((f32[8,56,1024]{2,1,0:T(8,128)}), f32[8,56,1024]{2,1,0:T(8,128)S(1)}, u32[]{:S(2)}, u32[]{:S(2)}) async-start(f32[8,56,1024]{2,1,0:T(8,128)} %gram_products.1), calls=%async_computation.2 | async-start | bytes 3670016 | tf_op jit(solution)/shard_map/all_to_all | solution.py:251
  25.4 24.3 %all-to-all-done.2.got_ref = f32[8,56,1024]{2,1,0:T(8,128)S(1)} async-done(((f32[8,56,1024]{2,1,0:T(8,128)}), f32[8,56,1024]{2,1,0:T(8,128)S(1)}, u32[]{:S(2)}, u32[]{:S(2)}) %all-to-all-start.2) | async-done | bytes 1835040 | tf_op jit(solution)/shard_map/all_to_all | solution.py:251
  61.7 33.6 %all_to_all.75 = bf16[16,64,1024]{2,1,0:T(8,128)(2,1)S(1)} all-to-all(bf16[16,64,1024]{2,1,0:T(8,128)(2,1)S(1)} %broadcast_in_dim.29), channel_id=1, replica_groups=mesh['tm'=2,'gz'=8,'view'=8] {'tm','gz'}, dimensions={0} | all-to-all | bytes 4194304 | tf_op jit(solution)/shard_map/all_to_all | solution.py:267
  96.4 4.3 %all-to-all-start.4 = ((f32[8,4,8,1024]{3,2,1,0:T(8,128)}), f32[8,4,8,1024]{3,2,1,0:T(8,128)}, u32[]{:S(2)}, u32[]{:S(2)}) async-start(f32[8,4,8,1024]{3,2,1,0:T(8,128)} %broadcast_in_dim.30), calls=%async_computation.4 | async-start | bytes 2097152 | tf_op jit(solution)/shard_map/all_to_all | solution.py:254
  101.3 4.4 %collective-permute-start = (f32[16,1024]{1,0:T(8,128)S(1)}, f32[16,1024]{1,0:T(8,128)S(1)}, u32[]{:S(2)}, u32[]{:S(2)}) collective-permute-start(f32[16,1024]{1,0:T(8,128)S(1)} %get-tuple-element.88), channel_id=1, source_target_pairs={{0,8},{8,16},{16,24},{24,32},{32,40},{40,48},{48,56},{56,64},{64,7... | collective-permute-start | bytes 196616 | tf_op jit(solution)/shard_map/ppermute | solution.py:246
  107.7 8.9 %all-to-all-done.4 = f32[8,4,8,1024]{3,2,1,0:T(8,128)} async-done(((f32[8,4,8,1024]{3,2,1,0:T(8,128)}), f32[8,4,8,1024]{3,2,1,0:T(8,128)}, u32[]{:S(2)}, u32[]{:S(2)}) %all-to-all-start.4) | async-done | bytes 1048608 | tf_op jit(solution)/shard_map/all_to_all | solution.py:254
  118.7 5.1 %collective-permute-start.6 = (f32[4,16,1024]{2,1,0:T(8,128)}, f32[4,16,1024]{2,1,0:T(8,128)}, u32[]{:S(2)}, u32[]{:S(2)}) collective-permute-start(f32[4,16,1024]{2,1,0:T(8,128)} %get-tuple-element.85), channel_id=1, source_target_pairs={{0,8},{8,16},{16,24},{24,32},{32,40},{40,48},{48,56},{56,64},{64,7... | collective-permute-start | bytes 786440 | tf_op jit(solution)/shard_map/ppermute | solution.py:246
  129.9 5.5 %all-to-all-start = ((f32[16,8,128]{2,1,0:T(8,128)}), f32[16,8,128]{2,1,0:T(8,128)S(1)}, u32[]{:S(2)}, u32[]{:S(2)}) async-start(f32[16,8,128]{2,1,0:T(8,128)} %get-tuple-element.45), calls=%async_computation | async-start | bytes 131072 | tf_op jit(solution)/shard_map/all_to_all | solution.py:279
  135.5 7.8 %all-to-all-done.sums_ref = f32[16,8,128]{2,1,0:T(8,128)S(1)} async-done(((f32[16,8,128]{2,1,0:T(8,128)}), f32[16,8,128]{2,1,0:T(8,128)S(1)}, u32[]{:S(2)}, u32[]{:S(2)}) %all-to-all-start) | async-done | bytes 65568 | tf_op jit(solution)/shard_map/all_to_all | solution.py:279
  143.9 2.6 second.6
  146.5 3.5 %all-to-all-start.1 = ((f32[16,8,128]{2,1,0:T(8,128)}), f32[16,8,128]{2,1,0:T(8,128)S(1)}, u32[]{:S(2)}, u32[]{:S(2)}) async-start(f32[16,8,128]{2,1,0:T(8,128)} %get-tuple-element.48), calls=%async_computation.1 | async-start | bytes 131072 | tf_op jit(solution)/shard_map/all_to_all | solution.py:279
  158.4 5.1 %subset.6 = (f32[96,1024]{1,0:T(8,128)}, f32[96,1024]{1,0:T(8,128)}, f32[16,8,128]{2,1,0:T(8,128)}) custom-call(s32[1]{0:T(128)} %bitcast.meta_ref, f32[96,1024]{1,0:T(8,128)} %get-tuple-element.46.x_ref, f32[96,1024]{1,0:T(8,128)} %get-tuple-element.47.g_ref, f32[16,8,128]{2,1,0:T(8,128)} %copy-done.3, bf16[2,1024,1024]{2,1,0:T(8,128)(2,1)} %pad_maximum_fusion.gram_ref, ...), custom_call_target="tpu_custom_call" | custom-call | tf_op jit(solution)/shard_map/subset/pallas_call | solution.py:309
  163.5 13.9 %all_to_all.76.sums_ref = f32[16,8,128]{2,1,0:T(8,128)} all-to-all(f32[16,8,128]{2,1,0:T(8,128)} %get-tuple-element.54), channel_id=1, replica_groups=mesh['tm'=2,'gz'=8,'view'=8] {'tm','gz'}, dimensions={0} | all-to-all | bytes 131072 | tf_op jit(solution)/shard_map/all_to_all | solution.py:279
  179.9 11.9 %all_to_all.77.sums_ref = f32[16,8,128]{2,1,0:T(8,128)} all-to-all(f32[16,8,128]{2,1,0:T(8,128)} %get-tuple-element.57), channel_id=1, replica_groups=mesh['tm'=2,'gz'=8,'view'=8] {'tm','gz'}, dimensions={0} | all-to-all | bytes 131072 | tf_op jit(solution)/shard_map/all_to_all | solution.py:279
  191.8 5.1 %subset.7 = (f32[96,1024]{1,0:T(8,128)}, f32[96,1024]{1,0:T(8,128)}, f32[16,8,128]{2,1,0:T(8,128)}) custom-call(s32[1]{0:T(128)} %bitcast.meta_ref, f32[96,1024]{1,0:T(8,128)} %get-tuple-element.55.x_ref, f32[96,1024]{1,0:T(8,128)} %get-tuple-element.56.g_ref, f32[16,8,128]{2,1,0:T(8,128)} %all_to_all.77.sums_ref, ...), custom_call_target="tpu_custom_call" | custom-call | tf_op jit(solution)/shard_map/subset/pallas_call | solution.py:309
  196.9 11.9 %all_to_all.78.sums_ref = f32[16,8,128]{2,1,0:T(8,128)} all-to-all(f32[16,8,128]{2,1,0:T(8,128)} %get-tuple-element.60), channel_id=1, replica_groups=mesh['tm'=2,'gz'=8,'view'=8] {'tm','gz'}, dimensions={0} | all-to-all | bytes 131072 | tf_op jit(solution)/shard_map/all_to_all | solution.py:279
  208.8 2.6 second.8
  211.4 11.9 %all_to_all.79.sums_ref = f32[16,8,128]{2,1,0:T(8,128)} all-to-all(f32[16,8,128]{2,1,0:T(8,128)} %get-tuple-element.63), channel_id=1, replica_groups=mesh['tm'=2,'gz'=8,'view'=8] {'tm','gz'}, dimensions={0} | all-to-all | bytes 131072 | tf_op jit(solution)/shard_map/all_to_all | solution.py:279
  223.3 5.1 %subset.8 = (f32[64,1024]{1,0:T(8,128)}, f32[96,1024]{1,0:T(8,128)}, f32[96,1024]{1,0:T(8,128)}, f32[16,8,128]{2,1,0:T(8,128)}) custom-call(s32[1]{0:T(128)} %bitcast.meta_ref, f32[96,1024]{1,0:T(8,128)} %get-tuple-element.61.x_ref, f32[96,1024]{1,0:T(8,128)} %get-tuple-element.62.g_ref, f32[16,8,128]{2,1,0:T(8,128)} %all_to_all.79.sums_ref, ...), custom_call_target="tpu_custom_call" | custom-call | tf_op jit(solution)/shard_map/subset/pallas_call | solution.py:309
  228.4 11.9 %all_to_all.80.sums_ref = f32[16,8,128]{2,1,0:T(8,128)} all-to-all(f32[16,8,128]{2,1,0:T(8,128)} %get-tuple-element.67), channel_id=1, replica_groups=mesh['tm'=2,'gz'=8,'view'=8] {'tm','gz'}, dimensions={0} | all-to-all | bytes 131072 | tf_op jit(solution)/shard_map/all_to_all | solution.py:279
  240.3 2.6 second.9
  242.8 11.9 %all_to_all.81.sums_ref = f32[16,8,128]{2,1,0:T(8,128)} all-to-all(f32[16,8,128]{2,1,0:T(8,128)} %get-tuple-element.70), channel_id=1, replica_groups=mesh['tm'=2,'gz'=8,'view'=8] {'tm','gz'}, dimensions={0} | all-to-all | bytes 131072 | tf_op jit(solution)/shard_map/all_to_all | solution.py:279
  254.8 5.1 %subset.9 = (f32[96,1024]{1,0:T(8,128)}, f32[96,1024]{1,0:T(8,128)}, f32[16,8,128]{2,1,0:T(8,128)}) custom-call(s32[1]{0:T(128)} %bitcast.meta_ref, f32[96,1024]{1,0:T(8,128)} %get-tuple-element.68.x_ref, f32[96,1024]{1,0:T(8,128)} %get-tuple-element.69.g_ref, f32[16,8,128]{2,1,0:T(8,128)} %all_to_all.81.sums_ref, ...), custom_call_target="tpu_custom_call" | custom-call | tf_op jit(solution)/shard_map/subset/pallas_call | solution.py:309
  259.8 11.9 %all_to_all.82.sums_ref = f32[16,8,128]{2,1,0:T(8,128)} all-to-all(f32[16,8,128]{2,1,0:T(8,128)} %get-tuple-element.73), channel_id=1, replica_groups=mesh['tm'=2,'gz'=8,'view'=8] {'tm','gz'}, dimensions={0} | all-to-all | bytes 131072 | tf_op jit(solution)/shard_map/all_to_all | solution.py:279
  271.8 2.6 second.10
  274.3 11.9 %all_to_all.83.sums_ref = f32[16,8,128]{2,1,0:T(8,128)} all-to-all(f32[16,8,128]{2,1,0:T(8,128)} %get-tuple-element.76), channel_id=1, replica_groups=mesh['tm'=2,'gz'=8,'view'=8] {'tm','gz'}, dimensions={0} | all-to-all | bytes 131072 | tf_op jit(solution)/shard_map/all_to_all | solution.py:279
  286.2 5.1 %subset.10 = (f32[96,1024]{1,0:T(8,128)}, f32[96,1024]{1,0:T(8,128)}, f32[16,8,128]{2,1,0:T(8,128)}) custom-call(s32[1]{0:T(128)} %bitcast.meta_ref, f32[96,1024]{1,0:T(8,128)} %get-tuple-element.74.x_ref, f32[96,1024]{1,0:T(8,128)} %get-tuple-element.75.g_ref, f32[16,8,128]{2,1,0:T(8,128)} %all_to_all.83.sums_ref, ...), custom_call_target="tpu_custom_call" | custom-call | tf_op jit(solution)/shard_map/subset/pallas_call | solution.py:309
  291.3 12.0 %all_to_all.84.sums_ref = f32[16,8,128]{2,1,0:T(8,128)} all-to-all(f32[16,8,128]{2,1,0:T(8,128)} %get-tuple-element.79), channel_id=1, replica_groups=mesh['tm'=2,'gz'=8,'view'=8] {'tm','gz'}, dimensions={0} | all-to-all | bytes 131072 | tf_op jit(solution)/shard_map/all_to_all | solution.py:279
  303.3 2.6 second.11
  305.9 11.9 %all_to_all.85.sums_ref = f32[16,8,128]{2,1,0:T(8,128)} all-to-all(f32[16,8,128]{2,1,0:T(8,128)} %get-tuple-element.82), channel_id=1, replica_groups=mesh['tm'=2,'gz'=8,'view'=8] {'tm','gz'}, dimensions={0} | all-to-all | bytes 131072 | tf_op jit(solution)/shard_map/all_to_all | solution.py:279
  317.8 4.7 %subset.11 = f32[64,1024]{1,0:T(8,128)} custom-call(s32[1]{0:T(128)} %bitcast.meta_ref, f32[96,1024]{1,0:T(8,128)} %get-tuple-element.80.x_ref, f32[96,1024]{1,0:T(8,128)} %get-tuple-element.81.g_ref, f32[16,8,128]{2,1,0:T(8,128)} %all_to_all.85.sums_ref, bf16[2,1024,1024]{2,1,0:T(8,128)(2,1)} %pad_maximum_fusion.gram_ref, ...), custom_call_target="tpu_custom_call" | custom-call | tf_op jit(solution)/shard_map/subset/pallas_call | solution.py:309
  (52 shorter events, 37.2 us)
Async XLA Ops:
  19.9 29.8 %all-to-all-start.2 = ((f32[8,56,1024]{2,1,0:T(8,128)}), f32[8,56,1024]{2,1,0:T(8,128)S(1)}, u32[]{:S(2)}, u32[]{:S(2)}) async-start(f32[8,56,1024]{2,1,0:T(8,128)} %gram_products.1), calls=%async_computation.2 | async-start | bytes 3670016 | tf_op jit(solution)/shard_map/all_to_all | solution.py:251
  49.7 1.2 copy-start
  53.2 5.3 %collective-permute-start.2 = (bf16[16,1024]{1,0:T(8,128)(2,1)}, bf16[16,1024]{1,0:T(8,128)(2,1)S(1)}, u32[]{:S(2)}, u32[]{:S(2)}) collective-permute-start(bf16[16,1024]{1,0:T(8,128)(2,1)} %get-tuple-element.49), channel_id=1, source_target_pairs={{0,2},{1,3},{2,4},{3,5},{4,6},{5,7},{6,0},{7,1},{8,10},{9,11},{10,... | collective-permute-start | bytes 98312 | tf_op jit(solution)/shard_map/ppermute | solution.py:262
  53.8 5.6 %collective-permute-start.3 = (bf16[16,1024]{1,0:T(8,128)(2,1)}, bf16[16,1024]{1,0:T(8,128)(2,1)S(1)}, u32[]{:S(2)}, u32[]{:S(2)}) collective-permute-start(bf16[16,1024]{1,0:T(8,128)(2,1)} %get-tuple-element.49), channel_id=1, source_target_pairs={{0,4},{1,5},{2,6},{3,7},{4,0},{5,1},{6,2},{7,3},{8,12},{9,13},{10,... | collective-permute-start | bytes 98312 | tf_op jit(solution)/shard_map/ppermute | solution.py:262
  55.8 4.1 %collective-permute-start.4 = (bf16[16,1024]{1,0:T(8,128)(2,1)}, bf16[16,1024]{1,0:T(8,128)(2,1)S(1)}, u32[]{:S(2)}, u32[]{:S(2)}) collective-permute-start(bf16[16,1024]{1,0:T(8,128)(2,1)} %get-tuple-element.49), channel_id=1, source_target_pairs={{0,6},{1,7},{2,0},{3,1},{4,2},{5,3},{6,4},{7,5},{8,14},{9,15},{10,... | collective-permute-start | bytes 98312 | tf_op jit(solution)/shard_map/ppermute | solution.py:262
  61.7 33.6 %copy-start.6 = (f32[4,8,1024]{2,1,0:T(8,128)S(1)}, f32[4,8,1024]{2,1,0:T(8,128)}, u32[]{:S(2)}) copy-start(f32[4,8,1024]{2,1,0:T(8,128)} %get-tuple-element.50) | copy-start | bytes 393220
  95.3 5.4 %copy-start.2 = (f32[64,1024]{1,0:T(8,128)S(1)}, f32[64,1024]{1,0:T(8,128)}, u32[]{:S(2)}) copy-start(f32[64,1024]{1,0:T(8,128)} %param.6) | copy-start | bytes 786436
  95.3 57.0 %collective-permute-start.5 = (bf16[1024,1024]{1,0:T(8,128)(2,1)S(1)}, bf16[1024,1024]{1,0:T(8,128)(2,1)}, u32[]{:S(2)}, u32[]{:S(2)}) collective-permute-start(bf16[1024,1024]{1,0:T(8,128)(2,1)S(1)} %bitcast.25), channel_id=1, source_target_pairs={{0,1},{1,0},{2,3},{3,2},{4,5},{5,4},{6,7},{7,6},{8,9},{9,8},{10,11... | collective-permute-start | bytes 6291464 | tf_op jit(solution)/shard_map/ppermute | solution.py:271
  96.4 20.2 %all-to-all-start.4 = ((f32[8,4,8,1024]{3,2,1,0:T(8,128)}), f32[8,4,8,1024]{3,2,1,0:T(8,128)}, u32[]{:S(2)}, u32[]{:S(2)}) async-start(f32[8,4,8,1024]{3,2,1,0:T(8,128)} %broadcast_in_dim.30), calls=%async_computation.4 | async-start | bytes 2097152 | tf_op jit(solution)/shard_map/all_to_all | solution.py:254
  101.3 6.3 %collective-permute-start = (f32[16,1024]{1,0:T(8,128)S(1)}, f32[16,1024]{1,0:T(8,128)S(1)}, u32[]{:S(2)}, u32[]{:S(2)}) collective-permute-start(f32[16,1024]{1,0:T(8,128)S(1)} %get-tuple-element.88), channel_id=1, source_target_pairs={{0,8},{8,16},{16,24},{24,32},{32,40},{40,48},{48,56},{56,64},{64,7... | collective-permute-start | bytes 196616 | tf_op jit(solution)/shard_map/ppermute | solution.py:246
  105.7 20.4 %collective-permute-start.1 = (f32[16,1024]{1,0:T(8,128)}, f32[16,1024]{1,0:T(8,128)}, u32[]{:S(2)}, u32[]{:S(2)}) collective-permute-start(f32[16,1024]{1,0:T(8,128)} %get-tuple-element.87), channel_id=1, source_target_pairs={{8,0},{16,8},{24,16},{32,24},{40,32},{48,40},{56,48},{64,56},{72,6... | collective-permute-start | bytes 196616 | tf_op jit(solution)/shard_map/ppermute | solution.py:247
  118.7 31.3 %collective-permute-start.6 = (f32[4,16,1024]{2,1,0:T(8,128)}, f32[4,16,1024]{2,1,0:T(8,128)}, u32[]{:S(2)}, u32[]{:S(2)}) collective-permute-start(f32[4,16,1024]{2,1,0:T(8,128)} %get-tuple-element.85), channel_id=1, source_target_pairs={{0,8},{8,16},{16,24},{24,32},{32,40},{40,48},{48,56},{56,64},{64,7... | collective-permute-start | bytes 786440 | tf_op jit(solution)/shard_map/ppermute | solution.py:246
  123.8 26.2 %collective-permute-start.7 = (f32[4,16,1024]{2,1,0:T(8,128)}, f32[4,16,1024]{2,1,0:T(8,128)}, u32[]{:S(2)}, u32[]{:S(2)}) collective-permute-start(f32[4,16,1024]{2,1,0:T(8,128)} %get-tuple-element.86), channel_id=1, source_target_pairs={{8,0},{16,8},{24,16},{32,24},{40,32},{48,40},{56,48},{64,56},{72,6... | collective-permute-start | bytes 786440 | tf_op jit(solution)/shard_map/ppermute | solution.py:247
  127.0 0.7 copy-start.1
  129.9 13.4 %all-to-all-start = ((f32[16,8,128]{2,1,0:T(8,128)}), f32[16,8,128]{2,1,0:T(8,128)S(1)}, u32[]{:S(2)}, u32[]{:S(2)}) async-start(f32[16,8,128]{2,1,0:T(8,128)} %get-tuple-element.45), calls=%async_computation | async-start | bytes 131072 | tf_op jit(solution)/shard_map/all_to_all | solution.py:279
  143.3 0.6 copy-start.4
  146.5 11.2 %all-to-all-start.1 = ((f32[16,8,128]{2,1,0:T(8,128)}), f32[16,8,128]{2,1,0:T(8,128)S(1)}, u32[]{:S(2)}, u32[]{:S(2)}) async-start(f32[16,8,128]{2,1,0:T(8,128)} %get-tuple-element.48), calls=%async_computation.1 | async-start | bytes 131072 | tf_op jit(solution)/shard_map/all_to_all | solution.py:279
  157.7 0.6 copy-start.3
  317.8 4.8 %copy-start.5 = (f32[64,1024]{1,0:T(8,128)S(1)}, f32[64,1024]{1,0:T(8,128)}, u32[]{:S(2)}) copy-start(f32[64,1024]{1,0:T(8,128)} %get-tuple-element.64) | copy-start | bytes 786436

commit v2 on v0

v2 whole, which is shorter than its diff:
```python
import functools

import jax
import jax.numpy as jnp
from jax import lax
from jax.experimental import pallas as pl
from jax.experimental.pallas import tpu as pltpu
from jax.sharding import PartitionSpec as P

RY = 128
FRAMES = 2
SWEEPS = 3
TV_STEPS = 2
HALO = 16
CHUNK = 512
QUARTERS = 4
AXES = ("tm", "gz", "view")

RELAXATION = 0.9
STEP_SCALE = 0.3
STEP_DECAY = 0.7
SMOOTHING = 0.01
NORM_GUARD = 1e-06

F32 = jnp.float32
BF16 = jnp.bfloat16
WHOLE = pl.BlockSpec(memory_space=pltpu.VMEM)
SCALARS = pl.BlockSpec(memory_space=pltpu.SMEM)


def params():
    return pltpu.CompilerParams(vmem_limit_bytes=40 * 1024 * 1024)


def near(array):
    return pltpu.with_memory_space_constraint(array, pltpu.VMEM)


def call(kernel, name, outs, ids, *arrays, scratch=()):
    return pl.pallas_call(
        kernel,
        out_shape=tuple(pltpu.VMEM(shape, dtype) for shape, dtype in outs),
        in_specs=[SCALARS] + [WHOLE] * len(arrays),
        out_specs=tuple(WHOLE for _ in outs),
        scratch_shapes=scratch,
        compiler_params=params(),
        name=name,
    )(ids, *[near(a) for a in arrays])


def keeps(d):
    return d[4] == d[1] // 2


def move(array, rule, source=None):
    pairs = []
    for tm in range(2):
        for y in range(4):
            for h in range(2):
                for z in range(4):
                    for c in range(2):
                        here = (tm, y, h, z, c)
                        if source is not None and not source(here):
                            continue
                        there = rule(*here)
                        if there is None:
                            continue
                        index = [((t * 4 + a) * 2 + b) * 8 + 2 * u + v for t, a, b, u, v in (here, there)]
                        pairs.append(tuple(index))
    return lax.ppermute(array, AXES, pairs)


def flip(dtm=0, dy=0, dh=0, dz=0, dc=0):
    return lambda tm, y, h, z, c: (tm ^ dtm, y ^ dy, h ^ dh, z ^ dz, c ^ dc)


def strip_step(step):
    def rule(tm, y, h, z, c):
        strip = 2 * tm + c + step
        return (strip // 2, y, h, z, strip % 2) if 0 <= strip < 4 else None

    return rule


def gram_kernel(order_ref, ids_ref, a_ref, s0_ref, s1_ref, b_ref, g_ref, acc):
    n = pl.program_id(0)
    d = pl.program_id(1)
    rows = s0_ref.shape[0]
    tile = a_ref[...]
    ray = jnp.sum(tile.astype(F32), axis=0, keepdims=True)
    inverse = 1.0 / ray
    lhs = []
    low = []
    for ref in (s0_ref, s1_ref):
        scaled = ref[...].astype(F32) * inverse
        high = scaled.astype(BF16)
        lhs.append(high)
        low.append((scaled - high.astype(F32)).astype(BF16))
    mine = a_ref[pl.ds(pl.multiple_of(ids_ref[1] * rows, rows), rows), :]
    lhs.append((mine.astype(F32) * inverse).astype(BF16))
    lhs.append(jnp.ones((16, CHUNK), BF16))
    stack = jnp.concatenate(lhs + low, axis=0)
    product = lax.dot_general(stack, tile, (((1,), (1,)), ((), ())), preferred_element_type=F32)
    top = 3 * rows + 16

    @pl.when(d == 0)
    def _():
        acc[...] = product

    @pl.when(d > 0)
    def _():
        acc[...] += product

    @pl.when(d == pl.num_programs(1) - 1)
    def _():
        part = rows // QUARTERS
        for quarter in range(QUARTERS):
            slot = jnp.bitwise_xor(ids_ref[2], quarter)
            for t in range(FRAMES):
                lo = t * rows + quarter * part
                value = acc[lo : lo + part] + acc[top + lo : top + lo + part]
                b_ref[slot, pl.ds(pl.multiple_of((2 * t + n) * part, part), part), :] = value
            lo = 2 * rows + quarter * part
            g_ref[slot, pl.ds(pl.multiple_of(n * part, part), part), :] = acc[lo : lo + part]
        for half in range(2):

            @pl.when(n == half)
            def _():
                cover = acc[3 * rows : 3 * rows + 8]
                for k in range(QUARTERS):
                    b_ref[k, 4 * part + half : 4 * part + 8, :] = cover[half:8]
                    g_ref[k, 2 * part + half : 2 * part + 8, :] = cover[half:8]


def gram_products(order, ids, projector, measured):
    _, pixels, det = projector.shape
    rows = measured.shape[2]
    part = rows // QUARTERS
    b_shape = (QUARTERS, 4 * part + 8, pixels)
    g_shape = (QUARTERS, 2 * part + 8, pixels)
    return pl.pallas_call(
        gram_kernel,
        out_shape=(jax.ShapeDtypeStruct(b_shape, F32), jax.ShapeDtypeStruct(g_shape, F32)),
        grid_spec=pltpu.PrefetchScalarGridSpec(
            num_scalar_prefetch=2,
            grid=(2, det // CHUNK),
            in_specs=[
                pl.BlockSpec((None, pixels, CHUNK), lambda n, d, o, s: (o[n], 0, d)),
                pl.BlockSpec((None, None, rows, CHUNK), lambda n, d, o, s: (0, o[n], 0, d)),
                pl.BlockSpec((None, None, rows, CHUNK), lambda n, d, o, s: (1, o[n], 0, d)),
            ],
            out_specs=(
                pl.BlockSpec(b_shape, lambda n, d, o, s: (0, 0, 0)),
                pl.BlockSpec(g_shape, lambda n, d, o, s: (0, 0, 0)),
            ),
            scratch_shapes=[pltpu.VMEM((5 * rows + 16, pixels), F32)],
        ),
        compiler_params=params(),
        name="gram_products",
    )(order, ids, projector, measured, measured)


def reduce_kernel(ids_ref, b0, b1, b2, b3, g0, g1, g2, g3, first_ref, second_ref, gram_ref, aux_ref):
    part = gram_ref.shape[1]
    b = (b0[...] + b1[...]) + (b2[...] + b3[...])
    g = (g0[...] + g1[...]) + (g2[...] + g3[...])
    keeper = ids_ref[4] == 1
    cov = jnp.where(keeper, b[4 * part : 4 * part + 8], g[2 * part : 2 * part + 8])
    scale = RELAXATION / cov
    for t, ref in enumerate((first_ref, second_ref)):
        for n in range(2):
            lo = (2 * t + n) * part
            ref[n] = b[lo : lo + part] * scale[n : n + 1]
    for n in range(2):
        rows = g[n * part : (n + 1) * part]
        share = cov[n : n + 1] / jnp.sum(cov[n : n + 1], axis=1, keepdims=True)
        own = jnp.sum(rows, axis=1, keepdims=True)
        gram_ref[n] = (rows - own * share).astype(BF16)
        aux_ref[n : n + 1] = RELAXATION * share
        aux_ref[2 + n : 3 + n] = scale[n : n + 1]


def place_gram_kernel(ids_ref, y0, y1, y2, y3, out_ref):
    z, y, h, tm = ids_ref[2], ids_ref[5], ids_ref[6], ids_ref[7]
    part = y0.shape[1]
    for dy, ref in enumerate((y0, y1, y2, y3)):
        for dx in range(4):
            slab = (
                jnp.bitwise_xor(tm, dx // 2) * 8
                + jnp.bitwise_xor(y, dy) * 2
                + jnp.bitwise_xor(h, dx % 2)
            )
            for k in range(QUARTERS):
                row = slab * (QUARTERS * part) + jnp.bitwise_xor(z, k) * part
                out_ref[pl.ds(pl.multiple_of(row, part), part), :] = ref[dx * QUARTERS + k]


def place_rows_kernel(ids_ref, z0, z1, z2, z3, out_ref):
    z = ids_ref[2]
    part = z0.shape[2]
    for k, ref in enumerate((z0, z1, z2, z3)):
        start = jnp.bitwise_xor(z, k) * part
        for slab in range(4):
            for n in range(2):
                row = slab * (QUARTERS * part) + start
                out_ref[n, pl.ds(pl.multiple_of(row, part), part), :] = ref[slab, n]


def tv_into(x_ref, g_ref, ss_ref, flux_ref, first, depth):
    height, pixels = x_ref.shape
    blocks = pixels // RY
    lane = lax.broadcasted_iota(jnp.int32, (height, RY), 1)
    zindex = first + lax.broadcasted_iota(jnp.int32, (height, RY), 0)
    inside = ((zindex >= 0) & (zindex < depth - 1)).astype(F32)
    column = (lane < RY - 1).astype(F32)
    flux_ref[...] = jnp.zeros_like(flux_ref)

    def block(i, folded):
        here_at = pl.ds(pl.multiple_of(i * RY, RY), RY)
        next_at = pl.ds(pl.multiple_of(jnp.minimum(i + 1, blocks - 1) * RY, RY), RY)
        here = x_ref[:, here_at]
        dz = (pltpu.roll(here, height - 1, 0) - here) * inside
        dc = (pltpu.roll(here, RY - 1, 1) - here) * column
        di = x_ref[:, next_at] - here
        square = dz * dz + dc * dc + di * di + SMOOTHING
        r = lax.rsqrt(square)
        r = r * (1.5 - 0.5 * square * r * r)
        fz = dz * r
        fc = dc * r
        fi = di * r
        g = (pltpu.roll(fz, 1, 0) - fz) + (flux_ref[...] - fi) + (pltpu.roll(fc, 1, 1) - fc)
        flux_ref[...] = fi
        g_ref[:, here_at] = g
        inner = g[HALO : height - HALO]
        piece = inner * inner
        for k in range(piece.shape[0] // 8):
            folded = folded + piece[8 * k : 8 * k + 8]
        return folded

    ss_ref[...] = lax.fori_loop(0, blocks, block, jnp.zeros((8, RY), F32))


def descend(x_ref, g_ref, sums, step, cells):
    folded = (sums[0][...] + sums[1][...]) + (sums[2][...] + sums[3][...])
    total = jnp.sum(folded, axis=(0, 1), keepdims=True)
    factor = (STEP_SCALE * STEP_DECAY**step) / jnp.sqrt(total / cells + NORM_GUARD)
    return x_ref[...] - factor * g_ref[...]


def first_kernel(ids_ref, x_ref, g_ref, ss_ref, flux, *, depth):
    tv_into(x_ref, g_ref, ss_ref, flux, ids_ref[0], depth)


def second_kernel(ids_ref, x_ref, g_ref, s0, s1, s2, s3, x_out, g_out, ss_out, flux, *, depth, step, cells):
    x_out[...] = descend(x_ref, g_ref, (s0, s1, s2, s3), step, cells)
    tv_into(x_out, g_out, ss_out, flux, ids_ref[0], depth)


def subset_kernel(
    ids_ref, x_ref, g_ref, s0, s1, s2, s3, mine_ref, other_ref, b_ref, aux_ref, *rest, depth, step, cells, final
):
    flux, product = rest[-2:]
    x_out = rest[0]
    height = x_ref.shape[0]
    x_out[...] = descend(x_ref, g_ref, (s0, s1, s2, s3), step, cells)
    core = ids_ref[3]

    def subset(n, carry):
        rounded = x_out[...].astype(BF16)

        @pl.when(n == core)
        def _():
            product[...] = jnp.dot(rounded, mine_ref[...], preferred_element_type=F32)

        @pl.when(n != core)
        def _():
            product[...] = jnp.dot(rounded, other_ref[...], preferred_element_type=F32)

        along = jnp.sum(rounded.astype(F32) * aux_ref[pl.ds(n, 1), :], axis=1, keepdims=True)
        change = b_ref[n] - product[...] * aux_ref[pl.ds(2 + n, 1), :] - along
        x_out[...] = jnp.maximum(x_out[...] + change, 0.0)
        return carry

    lax.fori_loop(0, 2, subset, 0)
    if not final:
        g_out, ss_out = rest[1:3]
        tv_into(x_out, g_out, ss_out, flux, ids_ref[0], depth)


def body(sinogram, projector, warm_volume, view_order):
    slices, pixels = warm_volume.shape
    part = slices // QUARTERS
    tm = lax.axis_index("tm").astype(jnp.int32)
    gz = lax.axis_index("gz").astype(jnp.int32)
    view = lax.axis_index("view").astype(jnp.int32)
    y, h = gz // 2, gz % 2
    z, c = view // 2, view % 2
    slab = tm * 8 + gz
    keeper = c == y // 2
    depth = slices * 16
    cells = depth * pixels
    inner = 4 * slices
    height = inner + 2 * HALO
    first = (2 * tm + c) * inner - HALO
    ids = jnp.stack([first, slab, z, c, keeper.astype(jnp.int32), y, h, tm])

    def slabs_of_strip(unit):
        across = move(unit, flip(dh=1), keeps)
        pair = jnp.where(h == 0, jnp.stack([unit, across]), jnp.stack([across, unit]))
        one = move(pair, flip(dy=1), keeps)
        two = move(pair, flip(dy=2), keeps)
        three = move(pair, flip(dy=3), keeps)
        same = jnp.where(keeper, pair, two)
        flipped = jnp.where(keeper, one, three)
        return jnp.where(
            y % 2 == 0, jnp.concatenate([same, flipped]), jnp.concatenate([flipped, same])
        )

    def widen(array, dim):
        length = array.shape[dim]
        low = move(lax.slice_in_dim(array, length - HALO, length, axis=dim), strip_step(1))
        high = move(lax.slice_in_dim(array, 0, HALO, axis=dim), strip_step(-1))
        return jnp.concatenate([low, array, high], axis=dim)

    partial_b, partial_g = gram_products(view_order, ids, projector, sinogram)
    got_b = move(partial_b, flip(dc=1), lambda d: not keeps(d))
    got_g = move(partial_g, flip(dc=1), keeps)
    b_terms = [partial_b[0] + got_b[0]]
    g_terms = [partial_g[0] + got_g[0]]
    for k in range(1, QUARTERS):
        b_terms.append(move(partial_b[k] + got_b[k], flip(dz=k), keeps))
        g_terms.append(move(partial_g[k] + got_g[k], flip(dz=k), lambda d: not keeps(d)))
    unit = ((2, part, pixels), F32)
    b_first, b_second, g_unit, aux = call(
        reduce_kernel,
        "reduce_views",
        [unit, unit, ((2, part, pixels), BF16), ((8, pixels), F32)],
        ids,
        *b_terms,
        *g_terms,
    )

    swapped = move(jnp.where(c == 0, g_unit[1], g_unit[0]), flip(dc=1), lambda d: not keeps(d))
    piece = jnp.where(keeper, swapped, jnp.where(c == 0, g_unit[0], g_unit[1]))
    line = jnp.stack([piece] + [move(piece, flip(dz=k)) for k in range(1, 4)])
    plane = jnp.concatenate(
        [line, move(line, flip(dh=1)), move(line, flip(dtm=1)), move(line, flip(dtm=1, dh=1))]
    )
    spread = [plane] + [move(plane, flip(dy=k)) for k in range(1, 4)]
    (mine,) = call(
        place_gram_kernel, "place_gram", [((slices * 16, pixels), BF16)], ids, *spread
    )
    other = move(mine, flip(dc=1))

    def b_rows(unit_b):
        strip = slabs_of_strip(unit_b)
        quarters = [strip] + [move(strip, flip(dz=k)) for k in range(1, 4)]
        (rows,) = call(place_rows_kernel, "place_rows", [((2, inner, pixels), F32)], ids, *quarters)
        return widen(rows, 1)

    b_wide = [b_rows(b_first), b_rows(b_second)]

    big = ((height, pixels), F32)
    small = ((8, RY), F32)
    flux = pltpu.VMEM((height, RY), F32)

    def everyone(sums):
        return [
            sums,
            move(sums, flip(dc=1)),
            move(sums, flip(dtm=1)),
            move(sums, flip(dtm=1, dc=1)),
        ]

    x = widen(slabs_of_strip(warm_volume).reshape(inner, pixels), 0)
    g, sums = call(
        functools.partial(first_kernel, depth=depth), "first", [big, small], ids, x, scratch=[flux]
    )
    finished = []
    for frame in range(FRAMES):
        for sweep in range(SWEEPS):
            step = sweep * TV_STEPS
            x, g, sums = call(
                functools.partial(second_kernel, depth=depth, step=step, cells=cells),
                "second",
                [big, big, small],
                ids,
                x,
                g,
                *everyone(sums),
                scratch=[flux],
            )
            final = sweep == SWEEPS - 1 and frame == FRAMES - 1
            outs = call(
                functools.partial(subset_kernel, depth=depth, step=step + 1, cells=cells, final=final),
                "subset",
                [big] if final else [big, big, small],
                ids,
                x,
                g,
                *everyone(sums),
                mine,
                other,
                b_wide[frame],
                aux,
                scratch=[flux, pltpu.VMEM((height, pixels), F32)],
            )
            if final:
                x = outs[0]
            else:
                x, g, sums = outs
        start = HALO + (gz % 4) * slices
        local = lax.dynamic_slice_in_dim(x, start, slices, axis=0)
        theirs = lax.dynamic_slice_in_dim(x, HALO + (gz % 4) * slices, slices, axis=0)
        passed = move(theirs, flip(dc=1), keeps)
        finished.append(jnp.where(keeper, local, passed))
    return jnp.stack(finished, axis=0)


def solution(mesh):
    return jax.shard_map(
        body,
        mesh=mesh,
        in_specs=(
            P(None, "view", ("tm", "gz"), None),
            P("view", None, None),
            P(("tm", "gz"), None),
            P(),
        ),
        out_specs=P(None, ("tm", "gz"), None),
        check_vma=False,
    )
```

time: 699 us -> 277 us (0.40); the launches traced: 688 us -> 275 us
  waiting for transfers between devices: 323 us -> 72.6 us
  blocking collectives: 134 us -> 0 us
  matrix products: 88.9 us -> 0 us
  starting transfers between devices: 49.3 us -> 124 us
  Pallas kernels: 0 us -> 59.3 us
  other arithmetic: 54 us -> 5.45 us
  between operations: 27.5 us -> 0.85 us
    all_gather x12 -> x0, waiting for transfers between devices: 280 us -> none  [total_of_pieces(): return lax.all_gather(array, axis).sum(0)]
    all_to_all x11 -> x0, blocking collectives: 134 us -> none  [copy_for_each(): lax.all_to_all(jnp.broadcast_to(array[None], (devices, *array.shape)), ax...]
    dot_general x12 -> x0, matrix products: 88.9 us -> none  [project(): lax.dot_general(mismatch, ray_tile, (((1,), (1,)), ((), ())), preferred_e...]
    ppermute x12 -> x81, starting transfers between devices: 37.2 us -> 124 us  [move(): return lax.ppermute(array, AXES, pairs)]
    pallas_call x0 -> x18, Pallas kernels: none -> 59.3 us  [the longest x17 49.4 us: call(): pl.pallas_call(kernel, out_shape=tuple((pltpu.VMEM(shape, dtype) for shap...]
    reduce_sum x38 -> x0, other arithmetic: 44 us -> none  [the longest x12 20.9 us: total_of_pieces(): return lax.all_gather(array, axis).sum(0)]
    ppermute x12 -> x81, waiting for transfers between devices: 28.7 us -> 72.6 us  [move(): return lax.ppermute(array, AXES, pairs)]
    all_to_all x2 -> x0, waiting for transfers between devices: 14.2 us -> none  [copy_for_each(): lax.all_to_all(jnp.broadcast_to(array[None], (devices, *array.shape)), ax...]
  transfers between devices with their start and end apart: 26 -> 81, of which waited for: 19 -> 35; matrix products, arithmetic and copies ran while one was open for 1% -> 2% of each run, Pallas kernels for 0% -> 17%
where the time goes in v2:
time: 277 us; the launch traced here: 275 us
  starting transfers between devices  124 us (45%)
  waiting for transfers between devices  72.6 us (26%)
  Pallas kernels  59.3 us (21%)
  local copies, waits for them, and re-layouts  12.5 us (5%)
  other arithmetic  5.45 us (2%)
    ppermute x81, starting transfers between devices, move(): return lax.ppermute(array, AXES, pairs)  124 us
    ppermute x81, waiting for transfers between devices, move(): return lax.ppermute(array, AXES, pairs)  72.6 us
    pallas_call x17, Pallas kernels, call(): pl.pallas_call(kernel, out_shape=tuple((pltpu.VMEM(shape, dtype) for shap...  49.4 us
    unnamed x31, local copies, waits for them, and re-layouts  11.6 us
    pallas_call x1, Pallas kernels, gram_products(): pl.pallas_call(gram_kernel, out_shape=(jax.ShapeDtypeStruct(b_shape, F32)...  9.88 us
  transfers between devices with their start and end apart: 81, of which 35 were waited for; matrix products, arithmetic and copies ran while one was open for 2% of the time, Pallas kernels for 17%

profile of v2, /device:TPU:0, one launch (start us, length us, event | category | flops | bytes accessed | tf_op | source)
XLA Modules:
  0.0 274.9 jit_solution(35512176320197713)
XLA Ops:
  0.1 4.0 %copy-done.5 = bf16[2,1024,2560]{2,1,0:T(8,128)(2,1)S(1)} copy-done((bf16[2,1024,2560]{2,1,0:T(8,128)(2,1)S(1)}, bf16[2,1024,2560]{2,1,0:T(8,128)(2,1)}, u32[]{:S(2)}) %copy-start.5) | copy-done | bytes 10485784
  6.0 9.9 %gram_products.1 = (f32[4,72,1024]{2,1,0:T(8,128)S(1)}, f32[4,40,1024]{2,1,0:T(8,128)S(1)}) custom-call(s32[2]{0:T(128)S(1)} %copy-done.11, s32[8]{0:T(128)S(1)} %stack.105.ids_ref, bf16[2,1024,2560]{2,1,0:T(8,128)(2,1)S(1)} %copy-done.5, bf16[2,2,64,2560]{3,2,1,0:T(8,128)(2,1)S(1)} %copy-done.8, bf16[2,2,64,2560]{3,2,1,0:T(8,128)(2,1)S(1)} %copy-done.8), custom_call_target="tpu_custom_call" | custom-call | tf_op jit(solution)/shard_map/gram_products/pallas_call | solution.py:141
  17.2 3.1 %collective-permute-start.16 = (f32[4,40,1024]{2,1,0:T(8,128)S(1)}, f32[4,40,1024]{2,1,0:T(8,128)S(1)}, u32[]{:S(2)}, u32[]{:S(2)}) collective-permute-start(f32[4,40,1024]{2,1,0:T(8,128)S(1)} %get-tuple-element.52), channel_id=1, source_target_pairs={{0,1},{2,3},{4,5},{6,7},{8,9},{10,11},{12,13},{14,15},{16,17},{18,... | collective-permute-start | bytes 1966088 | tf_op jit(solution)/shard_map/ppermute | solution.py:70
  20.4 5.1 %collective-permute-start = (f32[64,1024]{1,0:T(8,128)S(1)}, f32[64,1024]{1,0:T(8,128)S(1)}, u32[]{:S(2)}, u32[]{:S(2)}) collective-permute-start(f32[64,1024]{1,0:T(8,128)S(1)} %copy-done.12), channel_id=1, source_target_pairs={{0,8},{2,10},{4,12},{6,14},{8,0},{10,2},{12,4},{14,6},{16,24},{18,... | collective-permute-start | bytes 786440 | tf_op jit(solution)/shard_map/ppermute | solution.py:70
  27.8 3.8 %collective-permute-start.13 = (f32[72,1024]{1,0:T(8,128)}, f32[72,1024]{1,0:T(8,128)S(1)}, u32[]{:S(2)}, u32[]{:S(2)}) collective-permute-start(f32[72,1024]{1,0:T(8,128)} %get-tuple-element.91), channel_id=1, source_target_pairs={{0,2},{2,0},{4,6},{6,4},{8,10},{10,8},{12,14},{14,12},{16,18},{18,... | collective-permute-start | bytes 884744 | tf_op jit(solution)/shard_map/ppermute | solution.py:70
  31.6 5.5 %collective-permute-start.14 = (f32[72,1024]{1,0:T(8,128)S(1)}, f32[72,1024]{1,0:T(8,128)S(1)}, u32[]{:S(2)}, u32[]{:S(2)}) collective-permute-start(f32[72,1024]{1,0:T(8,128)S(1)} %get-tuple-element.90), channel_id=1, source_target_pairs={{0,4},{2,6},{4,0},{6,2},{8,12},{10,14},{12,8},{14,10},{16,20},{18,... | collective-permute-start | bytes 884744 | tf_op jit(solution)/shard_map/ppermute | solution.py:70
  41.2 3.5 %collective-permute-start.2 = (f32[2,64,1024]{2,1,0:T(8,128)}, f32[2,64,1024]{2,1,0:T(8,128)S(1)}, u32[]{:S(2)}, u32[]{:S(2)}) collective-permute-start(f32[2,64,1024]{2,1,0:T(8,128)} %maximum_select_fusion.1), channel_id=1, source_target_pairs={{0,16},{2,18},{4,20},{6,22},{8,24},{10,26},{12,28},{14,30},{16,0},... | collective-permute-start | bytes 1572872 | tf_op jit(solution)/shard_map/ppermute | solution.py:70
  44.7 8.1 %collective-permute-start.3 = (f32[2,64,1024]{2,1,0:T(8,128)}, f32[2,64,1024]{2,1,0:T(8,128)}, u32[]{:S(2)}, u32[]{:S(2)}) collective-permute-start(f32[2,64,1024]{2,1,0:T(8,128)} %maximum_select_fusion.1), channel_id=1, source_target_pairs={{0,48},{2,50},{4,52},{6,54},{8,56},{10,58},{12,60},{14,62},{16,32}... | collective-permute-start | bytes 1572872 | tf_op jit(solution)/shard_map/ppermute | solution.py:70
  54.8 3.3 %collective-permute-start.1 = (f32[2,64,1024]{2,1,0:T(8,128)}, f32[2,64,1024]{2,1,0:T(8,128)S(1)}, u32[]{:S(2)}, u32[]{:S(2)}) collective-permute-start(f32[2,64,1024]{2,1,0:T(8,128)} %maximum_select_fusion.1), channel_id=1, source_target_pairs={{0,32},{2,34},{4,36},{6,38},{8,40},{10,42},{12,44},{14,46},{16,48}... | collective-permute-start | bytes 1572872 | tf_op jit(solution)/shard_map/ppermute | solution.py:70
  60.0 3.0 %collective-permute-start.23 = (bf16[16,1024]{1,0:T(8,128)(2,1)S(1)}, bf16[16,1024]{1,0:T(8,128)(2,1)S(1)}, u32[]{:S(2)}, u32[]{:S(2)}) collective-permute-start(bf16[16,1024]{1,0:T(8,128)(2,1)S(1)} %get-tuple-element.88), channel_id=1, source_target_pairs={{0,6},{1,7},{2,4},{3,5},{4,2},{5,3},{6,0},{7,1},{8,14},{9,15},{10,... | collective-permute-start | bytes 98312 | tf_op jit(solution)/shard_map/ppermute | solution.py:70
  79.1 3.4 %collective-permute-start.31 = (f32[2,16,1024]{2,1,0:T(8,128)S(1)}, f32[2,16,1024]{2,1,0:T(8,128)S(1)}, u32[]{:S(2)}, u32[]{:S(2)}) collective-permute-start(f32[2,16,1024]{2,1,0:T(8,128)S(1)} %get-tuple-element.54), channel_id=1, source_target_pairs={{0,8},{2,10},{4,12},{6,14},{8,0},{10,2},{12,4},{14,6},{16,24},{18,... | collective-permute-start | bytes 393224 | tf_op jit(solution)/shard_map/ppermute | solution.py:70
  83.9 3.6 %collective-permute-done.31 = f32[2,16,1024]{2,1,0:T(8,128)S(1)} collective-permute-done((f32[2,16,1024]{2,1,0:T(8,128)S(1)}, f32[2,16,1024]{2,1,0:T(8,128)S(1)}, u32[]{:S(2)}, u32[]{:S(2)}) %collective-permute-start.31) | collective-permute-done | bytes 131104 | tf_op jit(solution)/shard_map/ppermute | solution.py:70
  89.1 3.4 %collective-permute-start.59 = (f32[2,16,1024]{2,1,0:T(8,128)S(1)}, f32[2,16,1024]{2,1,0:T(8,128)S(1)}, u32[]{:S(2)}, u32[]{:S(2)}) collective-permute-start(f32[2,16,1024]{2,1,0:T(8,128)S(1)} %get-tuple-element.74), channel_id=1, source_target_pairs={{0,8},{2,10},{4,12},{6,14},{8,0},{10,2},{12,4},{14,6},{16,24},{18,... | collective-permute-start | bytes 393224 | tf_op jit(solution)/shard_map/ppermute | solution.py:70
  92.5 7.4 %collective-permute-done.28.y2 = bf16[16,16,1024]{2,1,0:T(8,128)(2,1)S(1)} collective-permute-done((bf16[16,16,1024]{2,1,0:T(8,128)(2,1)S(1)}, bf16[16,16,1024]{2,1,0:T(8,128)(2,1)S(1)}, u32[]{:S(2)}, u32[]{:S(2)}) %collective-permute-start.28) | collective-permute-done | bytes 524320 | tf_op jit(solution)/shard_map/ppermute | solution.py:70
  113.3 3.0 %collective-permute-done.8.s3 = f32[8,128]{1,0:T(8,128)S(1)} collective-permute-done((f32[8,128]{1,0:T(8,128)S(1)}, f32[8,128]{1,0:T(8,128)S(1)}, u32[]{:S(2)}, u32[]{:S(2)}) %collective-permute-start.8) | collective-permute-done | bytes 4128 | tf_op jit(solution)/shard_map/ppermute | solution.py:70
  116.3 2.7 second.6
  121.6 4.4 %collective-permute-start.61 = (f32[2,2,16,1024]{3,2,1,0:T(8,128)S(1)}, f32[2,2,16,1024]{3,2,1,0:T(8,128)S(1)}, u32[]{:S(2)}, u32[]{:S(2)}) collective-permute-start(f32[2,2,16,1024]{3,2,1,0:T(8,128)S(1)} %maximum_select_fusion.5), channel_id=1, source_target_pairs={{0,16},{2,18},{4,20},{6,22},{8,24},{10,26},{12,28},{14,30},{16,0},... | collective-permute-start | bytes 786440 | tf_op jit(solution)/shard_map/ppermute | solution.py:70
  127.6 3.8 %collective-permute-start.36 = (f32[4,2,16,1024]{3,2,1,0:T(8,128)S(1)}, f32[4,2,16,1024]{3,2,1,0:T(8,128)S(1)}, u32[]{:S(2)}, u32[]{:S(2)}) collective-permute-start(f32[4,2,16,1024]{3,2,1,0:T(8,128)S(1)} %maximum_select_fusion.2.z0), channel_id=1, source_target_pairs={{0,4},{1,5},{2,6},{3,7},{4,0},{5,1},{6,2},{7,3},{8,12},{9,13},{10,... | collective-permute-start | bytes 1572872 | tf_op jit(solution)/shard_map/ppermute | solution.py:70
  137.3 5.1 %collective-permute-done.35.z1 = f32[4,2,16,1024]{3,2,1,0:T(8,128)S(1)} collective-permute-done((f32[4,2,16,1024]{3,2,1,0:T(8,128)S(1)}, f32[4,2,16,1024]{3,2,1,0:T(8,128)S(1)}, u32[]{:S(2)}, u32[]{:S(2)}) %collective-permute-start.35) | collective-permute-done | bytes 524320 | tf_op jit(solution)/shard_map/ppermute | solution.py:70
  142.4 12.6 %collective-permute-done.36.z2 = f32[4,2,16,1024]{3,2,1,0:T(8,128)S(1)} collective-permute-done((f32[4,2,16,1024]{3,2,1,0:T(8,128)S(1)}, f32[4,2,16,1024]{3,2,1,0:T(8,128)S(1)}, u32[]{:S(2)}, u32[]{:S(2)}) %collective-permute-start.36) | collective-permute-done | bytes 524320 | tf_op jit(solution)/shard_map/ppermute | solution.py:70
  164.6 4.1 %collective-permute-done.39 = f32[2,16,1024]{2,1,0:T(8,128)S(1)} collective-permute-done((f32[2,16,1024]{2,1,0:T(8,128)S(1)}, f32[2,16,1024]{2,1,0:T(8,128)S(1)}, u32[]{:S(2)}, u32[]{:S(2)}) %collective-permute-start.39) | collective-permute-done | bytes 131104 | tf_op jit(solution)/shard_map/ppermute | solution.py:70
  168.7 4.5 %collective-permute-start.9 = (f32[8,128]{1,0:T(8,128)S(1)}, f32[8,128]{1,0:T(8,128)S(1)}, u32[]{:S(2)}, u32[]{:S(2)}) collective-permute-start(f32[8,128]{1,0:T(8,128)S(1)} %get-tuple-element.50.s0), channel_id=1, source_target_pairs={{0,1},{1,0},{2,3},{3,2},{4,5},{5,4},{6,7},{7,6},{8,9},{9,8},{10,11... | collective-permute-start | bytes 12296 | tf_op jit(solution)/shard_map/ppermute | solution.py:70
  174.1 5.0 %subset.6 = (f32[288,1024]{1,0:T(8,128)S(1)}, f32[288,1024]{1,0:T(8,128)S(1)}, f32[8,128]{1,0:T(8,128)S(1)}) custom-call(s32[8]{0:T(128)S(1)} %stack.105.ids_ref, f32[288,1024]{1,0:T(8,128)S(1)} %get-tuple-element.48.x_ref, f32[288,1024]{1,0:T(8,128)S(1)} %get-tuple-element.49.g_ref, f32[8,128]{1,0:T(8,128)S(1)} %get-tuple-element.50.s0, ...), custom_call_target="tpu_custom_call" | custom-call | tf_op jit(solution)/shard_map/subset/pallas_call | solution.py:40
  181.1 3.3 %collective-permute-done.65.z3 = f32[4,2,16,1024]{3,2,1,0:T(8,128)S(1)} collective-permute-done((f32[4,2,16,1024]{3,2,1,0:T(8,128)S(1)}, f32[4,2,16,1024]{3,2,1,0:T(8,128)S(1)}, u32[]{:S(2)}, u32[]{:S(2)}) %collective-permute-start.65) | collective-permute-done | bytes 524320 | tf_op jit(solution)/shard_map/ppermute | solution.py:70
  194.2 5.0 %subset.7 = (f32[288,1024]{1,0:T(8,128)S(1)}, f32[288,1024]{1,0:T(8,128)S(1)}, f32[8,128]{1,0:T(8,128)S(1)}) custom-call(s32[8]{0:T(128)S(1)} %stack.105.ids_ref, f32[288,1024]{1,0:T(8,128)S(1)} %get-tuple-element.59.x_ref, f32[288,1024]{1,0:T(8,128)S(1)} %get-tuple-element.60.g_ref, f32[8,128]{1,0:T(8,128)S(1)} %get-tuple-element.61.s0, ...), custom_call_target="tpu_custom_call" | custom-call | tf_op jit(solution)/shard_map/subset/pallas_call | solution.py:40
  206.4 2.7 second.8
  218.4 5.0 %subset.8 = (f32[288,1024]{1,0:T(8,128)S(1)}, f32[288,1024]{1,0:T(8,128)S(1)}, f32[8,128]{1,0:T(8,128)S(1)}) custom-call(s32[8]{0:T(128)S(1)} %stack.105.ids_ref, f32[288,1024]{1,0:T(8,128)S(1)} %get-tuple-element.65.x_ref, f32[288,1024]{1,0:T(8,128)S(1)} %copy-done.10, f32[8,128]{1,0:T(8,128)S(1)} %get-tuple-element.67.s0, ...), custom_call_target="tpu_custom_call" | custom-call | tf_op jit(solution)/shard_map/subset/pallas_call | solution.py:40
  228.1 2.7 second.9
  235.3 5.0 %subset.9 = (f32[288,1024]{1,0:T(8,128)S(1)}, f32[288,1024]{1,0:T(8,128)S(1)}, f32[8,128]{1,0:T(8,128)S(1)}) custom-call(s32[8]{0:T(128)S(1)} %stack.105.ids_ref, f32[288,1024]{1,0:T(8,128)S(1)} %get-tuple-element.71.x_ref, f32[288,1024]{1,0:T(8,128)S(1)} %get-tuple-element.72.g_ref, f32[8,128]{1,0:T(8,128)S(1)} %get-tuple-element.73.s0, ...), custom_call_target="tpu_custom_call" | custom-call | tf_op jit(solution)/shard_map/subset/pallas_call | solution.py:40
  251.5 5.0 %subset.10 = (f32[288,1024]{1,0:T(8,128)S(1)}, f32[288,1024]{1,0:T(8,128)S(1)}, f32[8,128]{1,0:T(8,128)S(1)}) custom-call(s32[8]{0:T(128)S(1)} %stack.105.ids_ref, f32[288,1024]{1,0:T(8,128)S(1)} %get-tuple-element.78.x_ref, f32[288,1024]{1,0:T(8,128)S(1)} %get-tuple-element.79.g_ref, f32[8,128]{1,0:T(8,128)S(1)} %get-tuple-element.80.s0, ...), custom_call_target="tpu_custom_call" | custom-call | tf_op jit(solution)/shard_map/subset/pallas_call | solution.py:40
  260.6 2.7 second.11
  267.6 3.2 %subset.11 = f32[288,1024]{1,0:T(8,128)S(1)} custom-call(s32[8]{0:T(128)S(1)} %stack.105.ids_ref, f32[288,1024]{1,0:T(8,128)S(1)} %get-tuple-element.84.x_ref, f32[288,1024]{1,0:T(8,128)S(1)} %get-tuple-element.85.g_ref, f32[8,128]{1,0:T(8,128)S(1)} %get-tuple-element.86.s0, f32[8,128]{1,0:T(8,128)S(1)} %collective-permute-done.77.s1, ...), custom_call_target="tpu_custom_call" | custom-call | tf_op jit(solution)/shard_map/subset/pallas_call | solution.py:40
  (209 shorter events, 127.2 us)
Async XLA Ops:
  15.9 10.9 %collective-permute-start.12 = (f32[4,72,1024]{2,1,0:T(8,128)S(1)}, f32[4,72,1024]{2,1,0:T(8,128)S(1)}, u32[]{:S(2)}, u32[]{:S(2)}) collective-permute-start(f32[4,72,1024]{2,1,0:T(8,128)S(1)} %get-tuple-element.51), channel_id=1, source_target_pairs={{1,0},{3,2},{5,4},{7,6},{9,8},{11,10},{13,12},{15,14},{17,16},{19,... | collective-permute-start | bytes 3538952 | tf_op jit(solution)/shard_map/ppermute | solution.py:70
  20.4 18.6 %collective-permute-start = (f32[64,1024]{1,0:T(8,128)S(1)}, f32[64,1024]{1,0:T(8,128)S(1)}, u32[]{:S(2)}, u32[]{:S(2)}) collective-permute-start(f32[64,1024]{1,0:T(8,128)S(1)} %copy-done.12), channel_id=1, source_target_pairs={{0,8},{2,10},{4,12},{6,14},{8,0},{10,2},{12,4},{14,6},{16,24},{18,... | collective-permute-start | bytes 786440 | tf_op jit(solution)/shard_map/ppermute | solution.py:70
  26.2 13.5 %collective-permute-start.17 = (f32[40,1024]{1,0:T(8,128)S(1)}, f32[40,1024]{1,0:T(8,128)S(1)}, u32[]{:S(2)}, u32[]{:S(2)}) collective-permute-start(f32[40,1024]{1,0:T(8,128)S(1)} %get-tuple-element.99), channel_id=1, source_target_pairs={{1,3},{3,1},{5,7},{7,5},{9,11},{11,9},{13,15},{15,13},{17,19},{19,... | collective-permute-start | bytes 491528 | tf_op jit(solution)/shard_map/ppermute | solution.py:70
  27.8 25.0 %collective-permute-start.13 = (f32[72,1024]{1,0:T(8,128)}, f32[72,1024]{1,0:T(8,128)S(1)}, u32[]{:S(2)}, u32[]{:S(2)}) collective-permute-start(f32[72,1024]{1,0:T(8,128)} %get-tuple-element.91), channel_id=1, source_target_pairs={{0,2},{2,0},{4,6},{6,4},{8,10},{10,8},{12,14},{14,12},{16,18},{18,... | collective-permute-start | bytes 884744 | tf_op jit(solution)/shard_map/ppermute | solution.py:70
  31.6 21.2 %collective-permute-start.14 = (f32[72,1024]{1,0:T(8,128)S(1)}, f32[72,1024]{1,0:T(8,128)S(1)}, u32[]{:S(2)}, u32[]{:S(2)}) collective-permute-start(f32[72,1024]{1,0:T(8,128)S(1)} %get-tuple-element.90), channel_id=1, source_target_pairs={{0,4},{2,6},{4,0},{6,2},{8,12},{10,14},{12,8},{14,10},{16,20},{18,... | collective-permute-start | bytes 884744 | tf_op jit(solution)/shard_map/ppermute | solution.py:70
  37.1 15.7 %collective-permute-start.15 = (f32[72,1024]{1,0:T(8,128)S(1)}, f32[72,1024]{1,0:T(8,128)S(1)}, u32[]{:S(2)}, u32[]{:S(2)}) collective-permute-start(f32[72,1024]{1,0:T(8,128)S(1)} %get-tuple-element.89), channel_id=1, source_target_pairs={{0,6},{2,4},{4,2},{6,0},{8,14},{10,12},{12,10},{14,8},{16,22},{18,... | collective-permute-start | bytes 884744 | tf_op jit(solution)/shard_map/ppermute | solution.py:70
  41.2 18.8 %collective-permute-start.2 = (f32[2,64,1024]{2,1,0:T(8,128)}, f32[2,64,1024]{2,1,0:T(8,128)S(1)}, u32[]{:S(2)}, u32[]{:S(2)}) collective-permute-start(f32[2,64,1024]{2,1,0:T(8,128)} %maximum_select_fusion.1), channel_id=1, source_target_pairs={{0,16},{2,18},{4,20},{6,22},{8,24},{10,26},{12,28},{14,30},{16,0},... | collective-permute-start | bytes 1572872 | tf_op jit(solution)/shard_map/ppermute | solution.py:70
  44.7 18.3 %collective-permute-start.3 = (f32[2,64,1024]{2,1,0:T(8,128)}, f32[2,64,1024]{2,1,0:T(8,128)}, u32[]{:S(2)}, u32[]{:S(2)}) collective-permute-start(f32[2,64,1024]{2,1,0:T(8,128)} %maximum_select_fusion.1), channel_id=1, source_target_pairs={{0,48},{2,50},{4,52},{6,54},{8,56},{10,58},{12,60},{14,62},{16,32}... | collective-permute-start | bytes 1572872 | tf_op jit(solution)/shard_map/ppermute | solution.py:70
  54.8 24.1 %collective-permute-start.1 = (f32[2,64,1024]{2,1,0:T(8,128)}, f32[2,64,1024]{2,1,0:T(8,128)S(1)}, u32[]{:S(2)}, u32[]{:S(2)}) collective-permute-start(f32[2,64,1024]{2,1,0:T(8,128)} %maximum_select_fusion.1), channel_id=1, source_target_pairs={{0,32},{2,34},{4,36},{6,38},{8,40},{10,42},{12,44},{14,46},{16,48}... | collective-permute-start | bytes 1572872 | tf_op jit(solution)/shard_map/ppermute | solution.py:70
  74.2 14.9 %collective-permute-start.27 = (bf16[16,16,1024]{2,1,0:T(8,128)(2,1)S(1)}, bf16[16,16,1024]{2,1,0:T(8,128)(2,1)S(1)}, u32[]{:S(2)}, u32[]{:S(2)}) collective-permute-start(bf16[16,16,1024]{2,1,0:T(8,128)(2,1)S(1)} %constant_dynamic-update-slice_fusion.y0), channel_id=1, source_target_pairs={{0,16},{1,17},{2,18},{3,19},{4,20},{5,21},{6,22},{7,23},{8,24},{9,... | collective-permute-start | bytes 1572872 | tf_op jit(solution)/shard_map/ppermute | solution.py:70
  74.7 25.1 %collective-permute-start.28 = (bf16[16,16,1024]{2,1,0:T(8,128)(2,1)S(1)}, bf16[16,16,1024]{2,1,0:T(8,128)(2,1)S(1)}, u32[]{:S(2)}, u32[]{:S(2)}) collective-permute-start(bf16[16,16,1024]{2,1,0:T(8,128)(2,1)S(1)} %constant_dynamic-update-slice_fusion.y0), channel_id=1, source_target_pairs={{0,32},{1,33},{2,34},{3,35},{4,36},{5,37},{6,38},{7,39},{8,40},{9,... | collective-permute-start | bytes 1572872 | tf_op jit(solution)/shard_map/ppermute | solution.py:70
  76.6 25.8 %collective-permute-start.29 = (bf16[16,16,1024]{2,1,0:T(8,128)(2,1)S(1)}, bf16[16,16,1024]{2,1,0:T(8,128)(2,1)S(1)}, u32[]{:S(2)}, u32[]{:S(2)}) collective-permute-start(bf16[16,16,1024]{2,1,0:T(8,128)(2,1)S(1)} %constant_dynamic-update-slice_fusion.y0), channel_id=1, source_target_pairs={{0,48},{1,49},{2,50},{3,51},{4,52},{5,53},{6,54},{7,55},{8,56},{9,... | collective-permute-start | bytes 1572872 | tf_op jit(solution)/shard_map/ppermute | solution.py:70
  82.6 22.8 %collective-permute-start.4 = (f32[16,1024]{1,0:T(8,128)S(1)}, f32[16,1024]{1,0:T(8,128)S(1)}, u32[]{:S(2)}, u32[]{:S(2)}) collective-permute-start(f32[16,1024]{1,0:T(8,128)S(1)} %get-tuple-element.101), channel_id=1, source_target_pairs={{0,1},{1,64},{2,3},{3,66},{4,5},{5,68},{6,7},{7,70},{8,9},{9,72},{... | collective-permute-start | bytes 196616 | tf_op jit(solution)/shard_map/ppermute | solution.py:70
  87.5 18.0 %collective-permute-start.5 = (f32[16,1024]{1,0:T(8,128)S(1)}, f32[16,1024]{1,0:T(8,128)S(1)}, u32[]{:S(2)}, u32[]{:S(2)}) collective-permute-start(f32[16,1024]{1,0:T(8,128)S(1)} %get-tuple-element.102), channel_id=1, source_target_pairs={{1,0},{3,2},{5,4},{7,6},{9,8},{11,10},{13,12},{15,14},{17,16},{19,... | collective-permute-start | bytes 196616 | tf_op jit(solution)/shard_map/ppermute | solution.py:70
  89.1 31.2 %collective-permute-start.59 = (f32[2,16,1024]{2,1,0:T(8,128)S(1)}, f32[2,16,1024]{2,1,0:T(8,128)S(1)}, u32[]{:S(2)}, u32[]{:S(2)}) collective-permute-start(f32[2,16,1024]{2,1,0:T(8,128)S(1)} %get-tuple-element.74), channel_id=1, source_target_pairs={{0,8},{2,10},{4,12},{6,14},{8,0},{10,2},{12,4},{14,6},{16,24},{18,... | collective-permute-start | bytes 393224 | tf_op jit(solution)/shard_map/ppermute | solution.py:70
  99.9 21.8 %collective-permute-start.33 = (f32[2,2,16,1024]{3,2,1,0:T(8,128)S(1)}, f32[2,2,16,1024]{3,2,1,0:T(8,128)S(1)}, u32[]{:S(2)}, u32[]{:S(2)}) collective-permute-start(f32[2,2,16,1024]{3,2,1,0:T(8,128)S(1)} %maximum_select_fusion.4), channel_id=1, source_target_pairs={{0,16},{2,18},{4,20},{6,22},{8,24},{10,26},{12,28},{14,30},{16,0},... | collective-permute-start | bytes 786440 | tf_op jit(solution)/shard_map/ppermute | solution.py:70
  102.4 23.6 %collective-permute-start.34 = (f32[2,2,16,1024]{3,2,1,0:T(8,128)S(1)}, f32[2,2,16,1024]{3,2,1,0:T(8,128)S(1)}, u32[]{:S(2)}, u32[]{:S(2)}) collective-permute-start(f32[2,2,16,1024]{3,2,1,0:T(8,128)S(1)} %maximum_select_fusion.4), channel_id=1, source_target_pairs={{0,48},{2,50},{4,52},{6,54},{8,56},{10,58},{12,60},{14,62},{16,32}... | collective-permute-start | bytes 786440 | tf_op jit(solution)/shard_map/ppermute | solution.py:70
  105.4 68.7 %collective-permute-start.30 = (bf16[1024,1024]{1,0:T(8,128)(2,1)S(1)}, bf16[1024,1024]{1,0:T(8,128)(2,1)S(1)}, u32[]{:S(2)}, u32[]{:S(2)}) collective-permute-start(bf16[1024,1024]{1,0:T(8,128)(2,1)S(1)} %place_gram.1.mine_ref), channel_id=1, source_target_pairs={{0,1},{1,0},{2,3},{3,2},{4,5},{5,4},{6,7},{7,6},{8,9},{9,8},{10,11... | collective-permute-start | bytes 6291464 | tf_op jit(solution)/shard_map/ppermute | solution.py:70
  119.0 8.4 %collective-permute-start.32 = (f32[2,2,16,1024]{3,2,1,0:T(8,128)S(1)}, f32[2,2,16,1024]{3,2,1,0:T(8,128)S(1)}, u32[]{:S(2)}, u32[]{:S(2)}) collective-permute-start(f32[2,2,16,1024]{3,2,1,0:T(8,128)S(1)} %maximum_select_fusion.4), channel_id=1, source_target_pairs={{0,32},{2,34},{4,36},{6,38},{8,40},{10,42},{12,44},{14,46},{16,48}... | collective-permute-start | bytes 786440 | tf_op jit(solution)/shard_map/ppermute | solution.py:70
  121.6 11.0 %collective-permute-start.61 = (f32[2,2,16,1024]{3,2,1,0:T(8,128)S(1)}, f32[2,2,16,1024]{3,2,1,0:T(8,128)S(1)}, u32[]{:S(2)}, u32[]{:S(2)}) collective-permute-start(f32[2,2,16,1024]{3,2,1,0:T(8,128)S(1)} %maximum_select_fusion.5), channel_id=1, source_target_pairs={{0,16},{2,18},{4,20},{6,22},{8,24},{10,26},{12,28},{14,30},{16,0},... | collective-permute-start | bytes 786440 | tf_op jit(solution)/shard_map/ppermute | solution.py:70
  126.0 9.1 %collective-permute-start.62 = (f32[2,2,16,1024]{3,2,1,0:T(8,128)S(1)}, f32[2,2,16,1024]{3,2,1,0:T(8,128)S(1)}, u32[]{:S(2)}, u32[]{:S(2)}) collective-permute-start(f32[2,2,16,1024]{3,2,1,0:T(8,128)S(1)} %maximum_select_fusion.5), channel_id=1, source_target_pairs={{0,48},{2,50},{4,52},{6,54},{8,56},{10,58},{12,60},{14,62},{16,32}... | collective-permute-start | bytes 786440 | tf_op jit(solution)/shard_map/ppermute | solution.py:70
  127.5 14.9 %collective-permute-start.35 = (f32[4,2,16,1024]{3,2,1,0:T(8,128)S(1)}, f32[4,2,16,1024]{3,2,1,0:T(8,128)S(1)}, u32[]{:S(2)}, u32[]{:S(2)}) collective-permute-start(f32[4,2,16,1024]{3,2,1,0:T(8,128)S(1)} %maximum_select_fusion.2.z0), channel_id=1, source_target_pairs={{0,2},{1,3},{2,0},{3,1},{4,6},{5,7},{6,4},{7,5},{8,10},{9,11},{10,... | collective-permute-start | bytes 1572872 | tf_op jit(solution)/shard_map/ppermute | solution.py:70
  127.6 27.4 %collective-permute-start.36 = (f32[4,2,16,1024]{3,2,1,0:T(8,128)S(1)}, f32[4,2,16,1024]{3,2,1,0:T(8,128)S(1)}, u32[]{:S(2)}, u32[]{:S(2)}) collective-permute-start(f32[4,2,16,1024]{3,2,1,0:T(8,128)S(1)} %maximum_select_fusion.2.z0), channel_id=1, source_target_pairs={{0,4},{1,5},{2,6},{3,7},{4,0},{5,1},{6,2},{7,3},{8,12},{9,13},{10,... | collective-permute-start | bytes 1572872 | tf_op jit(solution)/shard_map/ppermute | solution.py:70
  132.7 24.9 %collective-permute-start.37 = (f32[4,2,16,1024]{3,2,1,0:T(8,128)S(1)}, f32[4,2,16,1024]{3,2,1,0:T(8,128)S(1)}, u32[]{:S(2)}, u32[]{:S(2)}) collective-permute-start(f32[4,2,16,1024]{3,2,1,0:T(8,128)S(1)} %maximum_select_fusion.2.z0), channel_id=1, source_target_pairs={{0,6},{1,7},{2,4},{3,5},{4,2},{5,3},{6,0},{7,1},{8,14},{9,15},{10,... | collective-permute-start | bytes 1572872 | tf_op jit(solution)/shard_map/ppermute | solution.py:70
  135.1 23.2 %collective-permute-start.10 = (f32[8,128]{1,0:T(8,128)S(1)}, f32[8,128]{1,0:T(8,128)S(1)}, u32[]{:S(2)}, u32[]{:S(2)}) collective-permute-start(f32[8,128]{1,0:T(8,128)S(1)} %get-tuple-element.50.s0), channel_id=1, source_target_pairs={{0,64},{1,65},{2,66},{3,67},{4,68},{5,69},{6,70},{7,71},{8,72},{9,... | collective-permute-start | bytes 12296 | tf_op jit(solution)/shard_map/ppermute | solution.py:70
  142.4 18.2 %collective-permute-start.11 = (f32[8,128]{1,0:T(8,128)S(1)}, f32[8,128]{1,0:T(8,128)S(1)}, u32[]{:S(2)}, u32[]{:S(2)}) collective-permute-start(f32[8,128]{1,0:T(8,128)S(1)} %get-tuple-element.50.s0), channel_id=1, source_target_pairs={{0,65},{1,64},{2,67},{3,66},{4,69},{5,68},{6,71},{7,70},{8,73},{9,... | collective-permute-start | bytes 12296 | tf_op jit(solution)/shard_map/ppermute | solution.py:70
  155.0 24.6 %collective-permute-start.63 = (f32[4,2,16,1024]{3,2,1,0:T(8,128)S(1)}, f32[4,2,16,1024]{3,2,1,0:T(8,128)S(1)}, u32[]{:S(2)}, u32[]{:S(2)}) collective-permute-start(f32[4,2,16,1024]{3,2,1,0:T(8,128)S(1)} %maximum_select_fusion.3.z0), channel_id=1, source_target_pairs={{0,2},{1,3},{2,0},{3,1},{4,6},{5,7},{6,4},{7,5},{8,10},{9,11},{10,... | collective-permute-start | bytes 1572872 | tf_op jit(solution)/shard_map/ppermute | solution.py:70
  157.6 23.5 %collective-permute-start.64 = (f32[4,2,16,1024]{3,2,1,0:T(8,128)S(1)}, f32[4,2,16,1024]{3,2,1,0:T(8,128)S(1)}, u32[]{:S(2)}, u32[]{:S(2)}) collective-permute-start(f32[4,2,16,1024]{3,2,1,0:T(8,128)S(1)} %maximum_select_fusion.3.z0), channel_id=1, source_target_pairs={{0,4},{1,5},{2,6},{3,7},{4,0},{5,1},{6,2},{7,3},{8,12},{9,13},{10,... | collective-permute-start | bytes 1572872 | tf_op jit(solution)/shard_map/ppermute | solution.py:70
  158.3 26.0 %collective-permute-start.65 = (f32[4,2,16,1024]{3,2,1,0:T(8,128)S(1)}, f32[4,2,16,1024]{3,2,1,0:T(8,128)S(1)}, u32[]{:S(2)}, u32[]{:S(2)}) collective-permute-start(f32[4,2,16,1024]{3,2,1,0:T(8,128)S(1)} %maximum_select_fusion.3.z0), channel_id=1, source_target_pairs={{0,6},{1,7},{2,4},{3,5},{4,2},{5,3},{6,0},{7,1},{8,14},{9,15},{10,... | collective-permute-start | bytes 1572872 | tf_op jit(solution)/shard_map/ppermute | solution.py:70
  190.7 41.6 %collective-permute-start.66 = (f32[2,16,1024]{2,1,0:T(8,128)}, f32[2,16,1024]{2,1,0:T(8,128)S(1)}, u32[]{:S(2)}, u32[]{:S(2)}) collective-permute-start(f32[2,16,1024]{2,1,0:T(8,128)} %get-tuple-element.93), channel_id=1, source_target_pairs={{0,1},{1,64},{2,3},{3,66},{4,5},{5,68},{6,7},{7,70},{8,9},{9,72},{... | collective-permute-start | bytes 393224 | tf_op jit(solution)/shard_map/ppermute | solution.py:70
  192.8 39.9 %collective-permute-start.67 = (f32[2,16,1024]{2,1,0:T(8,128)}, f32[2,16,1024]{2,1,0:T(8,128)}, u32[]{:S(2)}, u32[]{:S(2)}) collective-permute-start(f32[2,16,1024]{2,1,0:T(8,128)} %get-tuple-element.94), channel_id=1, source_target_pairs={{1,0},{3,2},{5,4},{7,6},{9,8},{11,10},{13,12},{15,14},{17,16},{19,... | collective-permute-start | bytes 393224 | tf_op jit(solution)/shard_map/ppermute | solution.py:70
  225.4 47.5 %collective-permute-start.52 = (f32[64,1024]{1,0:T(8,128)S(1)}, f32[64,1024]{1,0:T(8,128)S(1)}, u32[]{:S(2)}, u32[]{:S(2)}) collective-permute-start(f32[64,1024]{1,0:T(8,128)S(1)} %constant_dynamic-slice_fusion.1), channel_id=1, source_target_pairs={{0,1},{2,3},{4,5},{6,7},{8,9},{10,11},{12,13},{14,15},{16,17},{18,... | collective-permute-start | bytes 786440 | tf_op jit(solution)/shard_map/ppermute | solution.py:70
  (62 other events, 279.6 us)

commit v3 on v2

--- a/solution.py
+++ b/solution.py
@@ -28,8 +28,8 @@
 SCALARS = pl.BlockSpec(memory_space=pltpu.SMEM)
 
 
-def params():
-    return pltpu.CompilerParams(vmem_limit_bytes=40 * 1024 * 1024)
+def params(mib):
+    return pltpu.CompilerParams(vmem_limit_bytes=mib * 1024 * 1024)
 
 
 def near(array):
@@ -43,7 +43,7 @@
         in_specs=[SCALARS] + [WHOLE] * len(arrays),
         out_specs=tuple(WHOLE for _ in outs),
         scratch_shapes=scratch,
-        compiler_params=params(),
+        compiler_params=params(12),
         name=name,
     )(ids, *[near(a) for a in arrays])
 
@@ -70,6 +70,10 @@
     return lax.ppermute(array, AXES, pairs)
 
 
+def after(array, *others):
+    return lax.optimization_barrier((array, *others))[0]
+
+
 def flip(dtm=0, dy=0, dh=0, dz=0, dc=0):
     return lambda tm, y, h, z, c: (tm ^ dtm, y ^ dy, h ^ dh, z ^ dz, c ^ dc)
 
@@ -82,7 +86,7 @@
     return rule
 
 
-def gram_kernel(order_ref, ids_ref, a_ref, s0_ref, s1_ref, b_ref, g_ref, acc):
+def gram_kernel(order_ref, ids_ref, a_ref, s0_ref, s1_ref, own_ref, send_ref, acc):
     n = pl.program_id(0)
     d = pl.program_id(1)
     rows = s0_ref.shape[0]
@@ -114,33 +118,46 @@
     @pl.when(d == pl.num_programs(1) - 1)
     def _():
         part = rows // QUARTERS
-        for quarter in range(QUARTERS):
-            slot = jnp.bitwise_xor(ids_ref[2], quarter)
-            for t in range(FRAMES):
-                lo = t * rows + quarter * part
-                value = acc[lo : lo + part] + acc[top + lo : top + lo + part]
-                b_ref[slot, pl.ds(pl.multiple_of((2 * t + n) * part, part), part), :] = value
-            lo = 2 * rows + quarter * part
-            g_ref[slot, pl.ds(pl.multiple_of(n * part, part), part), :] = acc[lo : lo + part]
-        for half in range(2):
-
-            @pl.when(n == half)
+        at = pl.ds(pl.multiple_of(n * part, part), part)
+        for t in range(FRAMES):
+            for ref, who in ((own_ref, 1 - t), (send_ref, t)):
+
+                @pl.when(ids_ref[4] == who)
+                def _():
+                    for quarter in range(QUARTERS):
+                        lo = t * rows + quarter * part
+                        ref[jnp.bitwise_xor(ids_ref[2], quarter), at, :] = (
+                            acc[lo : lo + part] + acc[top + lo : top + lo + part]
+                        )
+
+        for ref, mine_too in ((own_ref, True), (send_ref, False)):
+
+            @pl.when((ids_ref[3] == n) == mine_too)
             def _():
-                cover = acc[3 * rows : 3 * rows + 8]
-                for k in range(QUARTERS):
-                    b_ref[k, 4 * part + half : 4 * part + 8, :] = cover[half:8]
-                    g_ref[k, 2 * part + half : 2 * part + 8, :] = cover[half:8]
+                for quarter in range(QUARTERS):
+                    lo = 2 * rows + quarter * part
+                    ref[jnp.bitwise_xor(ids_ref[2], quarter), 2 * part : 3 * part, :] = acc[lo : lo + part]
+
+            for half in range(2):
+
+                @pl.when(n == half)
+                def _():
+                    cover = acc[3 * rows : 3 * rows + 8]
+                    for k in range(QUARTERS):
+                        ref[k, 3 * part + half : 3 * part + 8, :] = cover[half:8]
 
 
 def gram_products(order, ids, projector, measured):
     _, pixels, det = projector.shape
     rows = measured.shape[2]
     part = rows // QUARTERS
-    b_shape = (QUARTERS, 4 * part + 8, pixels)
-    g_shape = (QUARTERS, 2 * part + 8, pixels)
+    shape = (QUARTERS, 3 * part + 8, pixels)
+    out = pl.BlockSpec(shape, lambda n, d, o, s: (0, 0, 0))
+    projector = pltpu.with_memory_space_constraint(projector, pltpu.HBM)
+    measured = pltpu.with_memory_space_constraint(measured, pltpu.HBM)
     return pl.pallas_call(
         gram_kernel,
-        out_shape=(jax.ShapeDtypeStruct(b_shape, F32), jax.ShapeDtypeStruct(g_shape, F32)),
+        out_shape=(jax.ShapeDtypeStruct(shape, F32),) * 2,
         grid_spec=pltpu.PrefetchScalarGridSpec(
             num_scalar_prefetch=2,
             grid=(2, det // CHUNK),
@@ -149,35 +166,28 @@
                 pl.BlockSpec((None, None, rows, CHUNK), lambda n, d, o, s: (0, o[n], 0, d)),
                 pl.BlockSpec((None, None, rows, CHUNK), lambda n, d, o, s: (1, o[n], 0, d)),
             ],
-            out_specs=(
-                pl.BlockSpec(b_shape, lambda n, d, o, s: (0, 0, 0)),
-                pl.BlockSpec(g_shape, lambda n, d, o, s: (0, 0, 0)),
-            ),
+            out_specs=(out, out),
             scratch_shapes=[pltpu.VMEM((5 * rows + 16, pixels), F32)],
         ),
-        compiler_params=params(),
+        compiler_params=params(24),
         name="gram_products",
     )(order, ids, projector, measured, measured)
 
 
-def reduce_kernel(ids_ref, b0, b1, b2, b3, g0, g1, g2, g3, first_ref, second_ref, gram_ref, aux_ref):
-    part = gram_ref.shape[1]
-    b = (b0[...] + b1[...]) + (b2[...] + b3[...])
-    g = (g0[...] + g1[...]) + (g2[...] + g3[...])
-    keeper = ids_ref[4] == 1
-    cov = jnp.where(keeper, b[4 * part : 4 * part + 8], g[2 * part : 2 * part + 8])
+def reduce_kernel(ids_ref, a0, a1, a2, a3, b_ref, gram_ref, aux_ref):
+    part = gram_ref.shape[0]
+    total = (a0[...] + a1[...]) + (a2[...] + a3[...])
+    cov = total[3 * part : 3 * part + 8]
     scale = RELAXATION / cov
-    for t, ref in enumerate((first_ref, second_ref)):
-        for n in range(2):
-            lo = (2 * t + n) * part
-            ref[n] = b[lo : lo + part] * scale[n : n + 1]
+    share = cov / jnp.sum(cov, axis=1, keepdims=True)
     for n in range(2):
-        rows = g[n * part : (n + 1) * part]
-        share = cov[n : n + 1] / jnp.sum(cov[n : n + 1], axis=1, keepdims=True)
-        own = jnp.sum(rows, axis=1, keepdims=True)
-        gram_ref[n] = (rows - own * share).astype(BF16)
-        aux_ref[n : n + 1] = RELAXATION * share
+        b_ref[n] = total[n * part : (n + 1) * part] * scale[n : n + 1]
+        aux_ref[n : n + 1] = RELAXATION * share[n : n + 1]
         aux_ref[2 + n : 3 + n] = scale[n : n + 1]
+    rows = total[2 * part : 3 * part]
+    own = jnp.sum(rows, axis=1, keepdims=True)
+    mine = jnp.where(ids_ref[3] == 0, share[0:1], share[1:2])
+    gram_ref[...] = (rows - own * mine).astype(BF16)
 
 
 def place_gram_kernel(ids_ref, y0, y1, y2, y3, out_ref):
@@ -322,43 +332,32 @@
         high = move(lax.slice_in_dim(array, 0, HALO, axis=dim), strip_step(-1))
         return jnp.concatenate([low, array, high], axis=dim)
 
-    partial_b, partial_g = gram_products(view_order, ids, projector, sinogram)
-    got_b = move(partial_b, flip(dc=1), lambda d: not keeps(d))
-    got_g = move(partial_g, flip(dc=1), keeps)
-    b_terms = [partial_b[0] + got_b[0]]
-    g_terms = [partial_g[0] + got_g[0]]
-    for k in range(1, QUARTERS):
-        b_terms.append(move(partial_b[k] + got_b[k], flip(dz=k), keeps))
-        g_terms.append(move(partial_g[k] + got_g[k], flip(dz=k), lambda d: not keeps(d)))
-    unit = ((2, part, pixels), F32)
-    b_first, b_second, g_unit, aux = call(
+    own, send = gram_products(view_order, ids, projector, sinogram)
+    both = own + move(send, flip(dc=1))
+    terms = [both[0]] + [move(both[k], flip(dz=k)) for k in range(1, QUARTERS)]
+    b_unit, piece, aux = call(
         reduce_kernel,
         "reduce_views",
-        [unit, unit, ((2, part, pixels), BF16), ((8, pixels), F32)],
+        [((2, part, pixels), F32), ((part, pixels), BF16), ((8, pixels), F32)],
         ids,
-        *b_terms,
-        *g_terms,
+        *terms,
     )
 
-    swapped = move(jnp.where(c == 0, g_unit[1], g_unit[0]), flip(dc=1), lambda d: not keeps(d))
-    piece = jnp.where(keeper, swapped, jnp.where(c == 0, g_unit[0], g_unit[1]))
     line = jnp.stack([piece] + [move(piece, flip(dz=k)) for k in range(1, 4)])
     plane = jnp.concatenate(
         [line, move(line, flip(dh=1)), move(line, flip(dtm=1)), move(line, flip(dtm=1, dh=1))]
     )
-    spread = [plane] + [move(plane, flip(dy=k)) for k in range(1, 4)]
-    (mine,) = call(
-        place_gram_kernel, "place_gram", [((slices * 16, pixels), BF16)], ids, *spread
-    )
-    other = move(mine, flip(dc=1))
-
-    def b_rows(unit_b):
+    spread = [move(plane, flip(dy=k)) for k in range(1, 4)]
+
+    def b_strip(unit_b):
         strip = slabs_of_strip(unit_b)
-        quarters = [strip] + [move(strip, flip(dz=k)) for k in range(1, 4)]
+        return [strip] + [move(strip, flip(dz=k)) for k in range(1, 4)]
+
+    def b_rows(quarters):
         (rows,) = call(place_rows_kernel, "place_rows", [((2, inner, pixels), F32)], ids, *quarters)
         return widen(rows, 1)
 
-    b_wide = [b_rows(b_first), b_rows(b_second)]
+    quarters = b_strip(b_unit)
 
     big = ((height, pixels), F32)
     small = ((8, RY), F32)
@@ -372,10 +371,11 @@
             move(sums, flip(dtm=1, dc=1)),
         ]
 
-    x = widen(slabs_of_strip(warm_volume).reshape(inner, pixels), 0)
+    x = widen(slabs_of_strip(after(warm_volume, both)).reshape(inner, pixels), 0)
     g, sums = call(
         functools.partial(first_kernel, depth=depth), "first", [big, small], ids, x, scratch=[flux]
     )
+    b_wide = [None, None]
     finished = []
     for frame in range(FRAMES):
         for sweep in range(SWEEPS):
@@ -390,6 +390,20 @@
                 *everyone(sums),
                 scratch=[flux],
             )
+            if frame == 0 and sweep == 0:
+                (mine,) = call(
+                    place_gram_kernel,
+                    "place_gram",
+                    [((slices * 16, pixels), BF16)],
+                    ids,
+                    after(plane, sums),
+                    *spread,
+                )
+                other = move(mine, flip(dc=1))
+                b_wide[0] = b_rows(quarters)
+            if frame == 0 and sweep == 1:
+                later = move(after(b_unit, x), flip(dc=1), lambda d: not keeps(d))
+                b_wide[1] = b_rows(b_strip(later))
             final = sweep == SWEEPS - 1 and frame == FRAMES - 1
             outs = call(
                 functools.partial(subset_kernel, depth=depth, step=step + 1, cells=cells, final=final),
@@ -411,8 +425,7 @@
                 x, g, sums = outs
         start = HALO + (gz % 4) * slices
         local = lax.dynamic_slice_in_dim(x, start, slices, axis=0)
-        theirs = lax.dynamic_slice_in_dim(x, HALO + (gz % 4) * slices, slices, axis=0)
-        passed = move(theirs, flip(dc=1), keeps)
+        passed = move(local, flip(dc=1), keeps)
         finished.append(jnp.where(keeper, local, passed))
     return jnp.stack(finished, axis=0)
 

time: 277 us -> 279 us (level)
  waiting for transfers between devices: 72.6 us -> 102 us
  starting transfers between devices: 124 us -> 102 us
  local copies, waits for them, and re-layouts: 12.5 us -> 7.38 us
    ppermute x81 -> x77, waiting for transfers between devices: 72.6 us -> 102 us  [move(): return lax.ppermute(array, AXES, pairs)]
    ppermute x81 -> x77, starting transfers between devices: 124 us -> 102 us  [move(): return lax.ppermute(array, AXES, pairs)]
    unnamed x31 -> x28, local copies, waits for them, and re-layouts: 11.6 us -> 6.34 us
  transfers between devices with their start and end apart: 81 -> 77, of which waited for: 35 -> 35; matrix products, arithmetic and copies ran while one was open for 2% -> 1% of each run, Pallas kernels for 17% -> 15%
where the time goes in v3:
time: 279 us; the launch traced here: 277 us
  starting transfers between devices  102 us (37%)
  waiting for transfers between devices  102 us (37%)
  Pallas kernels  61.7 us (22%)
  local copies, waits for them, and re-layouts  7.38 us (3%)
  other arithmetic  3.27 us (1%)
    ppermute x77, starting transfers between devices, move(): return lax.ppermute(array, AXES, pairs)  102 us
    ppermute x77, waiting for transfers between devices, move(): return lax.ppermute(array, AXES, pairs)  102 us
    pallas_call x17, Pallas kernels, call(): pl.pallas_call(kernel, out_shape=tuple((pltpu.VMEM(shape, dtype) for shap...  49.5 us
    pallas_call x1, Pallas kernels, gram_products(): pl.pallas_call(gram_kernel, out_shape=(jax.ShapeDtypeStruct(shape, F32),)...  12.2 us
    unnamed x28, local copies, waits for them, and re-layouts  6.34 us
  transfers between devices with their start and end apart: 77, of which 35 were waited for; matrix products, arithmetic and copies ran while one was open for 1% of the time, Pallas kernels for 15%

profile of v3, /device:TPU:0, one launch (start us, length us, event | category | flops | bytes accessed | tf_op | source)
XLA Modules:
  0.0 276.8 jit_solution(11438429238973976526)
XLA Ops:
  0.7 12.2 %gram_products.1 = (f32[4,56,1024]{2,1,0:T(8,128)S(1)}, f32[4,56,1024]{2,1,0:T(8,128)S(1)}) custom-call(s32[2]{0:T(128)S(1)} %copy-done.9, s32[8]{0:T(128)S(1)} %stack.105.ids_ref, bf16[2,1024,2560]{2,1,0:T(8,128)(2,1)} %a_ref.1, bf16[2,2,64,2560]{3,2,1,0:T(8,128)(2,1)} %s1_ref.1, bf16[2,2,64,2560]{3,2,1,0:T(8,128)(2,1)} %s1_ref.1), custom_call_target="tpu_custom_call" | custom-call | tf_op jit(solution)/shard_map/gram_products/pallas_call | solution.py:158
  15.7 4.2 %collective-permute-start.15 = (f32[56,1024]{1,0:T(8,128)S(1)}, f32[56,1024]{1,0:T(8,128)S(1)}, u32[]{:S(2)}, u32[]{:S(2)}) collective-permute-start(f32[56,1024]{1,0:T(8,128)S(1)} %get-tuple-element.97), channel_id=1, source_target_pairs={{0,6},{1,7},{2,4},{3,5},{4,2},{5,3},{6,0},{7,1},{8,14},{9,15},{10,... | collective-permute-start | bytes 688136 | tf_op jit(solution)/shard_map/ppermute | solution.py:70
  20.9 4.9 %collective-permute-start.1 = (f32[64,1024]{1,0:T(8,128)S(1)}, f32[64,1024]{1,0:T(8,128)S(1)}, u32[]{:S(2)}, u32[]{:S(2)}) collective-permute-start(f32[64,1024]{1,0:T(8,128)S(1)} %copy-done.10), channel_id=1, source_target_pairs={{0,8},{2,10},{4,12},{6,14},{8,0},{10,2},{12,4},{14,6},{16,24},{18,... | collective-permute-start | bytes 786440 | tf_op jit(solution)/shard_map/ppermute | solution.py:70
  25.9 4.9 %collective-permute-done.15.a3 = f32[56,1024]{1,0:T(8,128)S(1)} collective-permute-done((f32[56,1024]{1,0:T(8,128)S(1)}, f32[56,1024]{1,0:T(8,128)S(1)}, u32[]{:S(2)}, u32[]{:S(2)}) %collective-permute-start.15) | collective-permute-done | bytes 229408 | tf_op jit(solution)/shard_map/ppermute | solution.py:70
  32.1 2.9 %collective-permute-start.18 = (bf16[16,1024]{1,0:T(8,128)(2,1)S(1)}, bf16[16,1024]{1,0:T(8,128)(2,1)S(1)}, u32[]{:S(2)}, u32[]{:S(2)}) collective-permute-start(bf16[16,1024]{1,0:T(8,128)(2,1)S(1)} %get-tuple-element.56), channel_id=1, source_target_pairs={{0,6},{1,7},{2,4},{3,5},{4,2},{5,3},{6,0},{7,1},{8,14},{9,15},{10,... | collective-permute-start | bytes 98312 | tf_op jit(solution)/shard_map/ppermute | solution.py:70
  36.4 3.5 %collective-permute-start.3 = (f32[2,64,1024]{2,1,0:T(8,128)S(1)}, f32[2,64,1024]{2,1,0:T(8,128)S(1)}, u32[]{:S(2)}, u32[]{:S(2)}) collective-permute-start(f32[2,64,1024]{2,1,0:T(8,128)S(1)} %maximum_select_fusion.1), channel_id=1, source_target_pairs={{0,16},{2,18},{4,20},{6,22},{8,24},{10,26},{12,28},{14,30},{16,0},... | collective-permute-start | bytes 1572872 | tf_op jit(solution)/shard_map/ppermute | solution.py:70
  45.1 2.8 collective-permute-start.19
  47.9 4.4 %collective-permute-done.19 = bf16[4,16,1024]{2,1,0:T(8,128)(2,1)S(1)} collective-permute-done((bf16[4,16,1024]{2,1,0:T(8,128)(2,1)S(1)}, bf16[4,16,1024]{2,1,0:T(8,128)(2,1)S(1)}, u32[]{:S(2)}, u32[]{:S(2)}) %collective-permute-start.19) | collective-permute-done | bytes 131104 | tf_op jit(solution)/shard_map/ppermute | solution.py:70
  53.7 4.7 %collective-permute-done.21 = bf16[4,16,1024]{2,1,0:T(8,128)(2,1)S(1)} collective-permute-done((bf16[4,16,1024]{2,1,0:T(8,128)(2,1)S(1)}, bf16[4,16,1024]{2,1,0:T(8,128)(2,1)S(1)}, u32[]{:S(2)}, u32[]{:S(2)}) %collective-permute-start.21) | collective-permute-done | bytes 131104 | tf_op jit(solution)/shard_map/ppermute | solution.py:70
  65.6 2.7 collective-permute-start.26
  70.8 3.0 %collective-permute-done.9.s3 = f32[8,128]{1,0:T(8,128)S(1)} collective-permute-done((f32[8,128]{1,0:T(8,128)S(1)}, f32[8,128]{1,0:T(8,128)S(1)}, u32[]{:S(2)}, u32[]{:S(2)}) %collective-permute-start.9) | collective-permute-done | bytes 4128 | tf_op jit(solution)/shard_map/ppermute | solution.py:70
  73.9 4.4 %collective-permute-start.8 = (f32[8,128]{1,0:T(8,128)S(1)}, f32[8,128]{1,0:T(8,128)S(1)}, u32[]{:S(2)}, u32[]{:S(2)}) collective-permute-start(f32[8,128]{1,0:T(8,128)S(1)} %get-tuple-element.52.s0), channel_id=1, source_target_pairs={{0,64},{1,65},{2,66},{3,67},{4,68},{5,69},{6,70},{7,71},{8,72},{9,... | collective-permute-start | bytes 12296 | tf_op jit(solution)/shard_map/ppermute | solution.py:70
  84.7 3.3 %collective-permute-start.27 = (f32[2,2,16,1024]{3,2,1,0:T(8,128)S(1)}, f32[2,2,16,1024]{3,2,1,0:T(8,128)S(1)}, u32[]{:S(2)}, u32[]{:S(2)}) collective-permute-start(f32[2,2,16,1024]{3,2,1,0:T(8,128)S(1)} %maximum_select_fusion.4), channel_id=1, source_target_pairs={{0,32},{2,34},{4,36},{6,38},{8,40},{10,42},{12,44},{14,46},{16,48}... | collective-permute-start | bytes 786440 | tf_op jit(solution)/shard_map/ppermute | solution.py:70
  91.9 4.4 %collective-permute-done.28 = f32[2,2,16,1024]{3,2,1,0:T(8,128)S(1)} collective-permute-done((f32[2,2,16,1024]{3,2,1,0:T(8,128)S(1)}, f32[2,2,16,1024]{3,2,1,0:T(8,128)S(1)}, u32[]{:S(2)}, u32[]{:S(2)}) %collective-permute-start.28) | collective-permute-done | bytes 262176 | tf_op jit(solution)/shard_map/ppermute | solution.py:70
  96.4 3.6 %collective-permute-start.32 = (f32[4,2,16,1024]{3,2,1,0:T(8,128)S(1)}, f32[4,2,16,1024]{3,2,1,0:T(8,128)S(1)}, u32[]{:S(2)}, u32[]{:S(2)}) collective-permute-start(f32[4,2,16,1024]{3,2,1,0:T(8,128)S(1)} %maximum_select_fusion.2.z0), channel_id=1, source_target_pairs={{0,6},{1,7},{2,4},{3,5},{4,2},{5,3},{6,0},{7,1},{8,14},{9,15},{10,... | collective-permute-start | bytes 1572872 | tf_op jit(solution)/shard_map/ppermute | solution.py:70
  101.0 22.6 %collective-permute-done.32.z3 = f32[4,2,16,1024]{3,2,1,0:T(8,128)S(1)} collective-permute-done((f32[4,2,16,1024]{3,2,1,0:T(8,128)S(1)}, f32[4,2,16,1024]{3,2,1,0:T(8,128)S(1)}, u32[]{:S(2)}, u32[]{:S(2)}) %collective-permute-start.32) | collective-permute-done | bytes 524320 | tf_op jit(solution)/shard_map/ppermute | solution.py:70
  133.0 5.1 %subset.6 = (f32[288,1024]{1,0:T(8,128)S(1)}, f32[288,1024]{1,0:T(8,128)S(1)}, f32[8,128]{1,0:T(8,128)S(1)}) custom-call(s32[8]{0:T(128)S(1)} %stack.105.ids_ref, f32[288,1024]{1,0:T(8,128)S(1)} %get-tuple-element.53.x_ref, f32[288,1024]{1,0:T(8,128)S(1)} %get-tuple-element.54.g_ref, f32[8,128]{1,0:T(8,128)S(1)} %get-tuple-element.55.s0, ...), custom_call_target="tpu_custom_call" | custom-call | tf_op jit(solution)/shard_map/subset/pallas_call | solution.py:40
  147.8 5.2 %collective-permute-start.55 = (f32[2,16,1024]{2,1,0:T(8,128)S(1)}, f32[2,16,1024]{2,1,0:T(8,128)S(1)}, u32[]{:S(2)}, u32[]{:S(2)}) collective-permute-start(f32[2,16,1024]{2,1,0:T(8,128)S(1)} %collective-permute-done.54), channel_id=1, source_target_pairs={{0,8},{2,10},{4,12},{6,14},{8,0},{10,2},{12,4},{14,6},{16,24},{18,... | collective-permute-start | bytes 393224 | tf_op jit(solution)/shard_map/ppermute | solution.py:70
  153.0 3.1 %collective-permute-done.55 = f32[2,16,1024]{2,1,0:T(8,128)S(1)} collective-permute-done((f32[2,16,1024]{2,1,0:T(8,128)S(1)}, f32[2,16,1024]{2,1,0:T(8,128)S(1)}, u32[]{:S(2)}, u32[]{:S(2)}) %collective-permute-start.55) | collective-permute-done | bytes 131104 | tf_op jit(solution)/shard_map/ppermute | solution.py:70
  157.4 2.8 %collective-permute-start.57 = (f32[2,2,16,1024]{3,2,1,0:T(8,128)S(1)}, f32[2,2,16,1024]{3,2,1,0:T(8,128)S(1)}, u32[]{:S(2)}, u32[]{:S(2)}) collective-permute-start(f32[2,2,16,1024]{3,2,1,0:T(8,128)S(1)} %maximum_select_fusion.5), channel_id=1, source_target_pairs={{0,16},{2,18},{4,20},{6,22},{8,24},{10,26},{12,28},{14,30},{16,0},... | collective-permute-start | bytes 786440 | tf_op jit(solution)/shard_map/ppermute | solution.py:70
  161.6 4.1 %collective-permute-done.57 = f32[2,2,16,1024]{3,2,1,0:T(8,128)S(1)} collective-permute-done((f32[2,2,16,1024]{3,2,1,0:T(8,128)S(1)}, f32[2,2,16,1024]{3,2,1,0:T(8,128)S(1)}, u32[]{:S(2)}, u32[]{:S(2)}) %collective-permute-start.57) | collective-permute-done | bytes 262176 | tf_op jit(solution)/shard_map/ppermute | solution.py:70
  165.8 3.0 %collective-permute-start.61 = (f32[4,2,16,1024]{3,2,1,0:T(8,128)S(1)}, f32[4,2,16,1024]{3,2,1,0:T(8,128)S(1)}, u32[]{:S(2)}, u32[]{:S(2)}) collective-permute-start(f32[4,2,16,1024]{3,2,1,0:T(8,128)S(1)} %maximum_select_fusion.3.z0), channel_id=1, source_target_pairs={{0,6},{1,7},{2,4},{3,5},{4,2},{5,3},{6,0},{7,1},{8,14},{9,15},{10,... | collective-permute-start | bytes 1572872 | tf_op jit(solution)/shard_map/ppermute | solution.py:70
  171.5 21.2 %collective-permute-done.61.z3 = f32[4,2,16,1024]{3,2,1,0:T(8,128)S(1)} collective-permute-done((f32[4,2,16,1024]{3,2,1,0:T(8,128)S(1)}, f32[4,2,16,1024]{3,2,1,0:T(8,128)S(1)}, u32[]{:S(2)}, u32[]{:S(2)}) %collective-permute-start.61) | collective-permute-done | bytes 524320 | tf_op jit(solution)/shard_map/ppermute | solution.py:70
  198.0 5.1 %subset.7 = (f32[288,1024]{1,0:T(8,128)S(1)}, f32[288,1024]{1,0:T(8,128)S(1)}, f32[8,128]{1,0:T(8,128)S(1)}) custom-call(s32[8]{0:T(128)S(1)} %stack.105.ids_ref, f32[288,1024]{1,0:T(8,128)S(1)} %get-tuple-element.63.x_ref, f32[288,1024]{1,0:T(8,128)S(1)} %get-tuple-element.64.g_ref, f32[8,128]{1,0:T(8,128)S(1)} %get-tuple-element.65.s0, ...), custom_call_target="tpu_custom_call" | custom-call | tf_op jit(solution)/shard_map/subset/pallas_call | solution.py:40
  203.0 2.9 %collective-permute-start.43 = (f32[8,128]{1,0:T(8,128)S(1)}, f32[8,128]{1,0:T(8,128)S(1)}, u32[]{:S(2)}, u32[]{:S(2)}) collective-permute-start(f32[8,128]{1,0:T(8,128)S(1)} %get-tuple-element.68.s0), channel_id=1, source_target_pairs={{0,65},{1,64},{2,67},{3,66},{4,69},{5,68},{6,71},{7,70},{8,73},{9,... | collective-permute-start | bytes 12296 | tf_op jit(solution)/shard_map/ppermute | solution.py:70
  209.6 2.7 second.8
  221.6 5.0 %subset.8 = (f32[288,1024]{1,0:T(8,128)S(1)}, f32[288,1024]{1,0:T(8,128)S(1)}, f32[8,128]{1,0:T(8,128)S(1)}) custom-call(s32[8]{0:T(128)S(1)} %stack.105.ids_ref, f32[288,1024]{1,0:T(8,128)S(1)} %get-tuple-element.69.x_ref, f32[288,1024]{1,0:T(8,128)S(1)} %copy-done.8, f32[8,128]{1,0:T(8,128)S(1)} %get-tuple-element.71.s0, ...), custom_call_target="tpu_custom_call" | custom-call | tf_op jit(solution)/shard_map/subset/pallas_call | solution.py:40
  231.8 2.7 second.9
  238.3 5.1 %subset.9 = (f32[288,1024]{1,0:T(8,128)S(1)}, f32[288,1024]{1,0:T(8,128)S(1)}, f32[8,128]{1,0:T(8,128)S(1)}) custom-call(s32[8]{0:T(128)S(1)} %stack.105.ids_ref, f32[288,1024]{1,0:T(8,128)S(1)} %get-tuple-element.75.x_ref, f32[288,1024]{1,0:T(8,128)S(1)} %get-tuple-element.76.g_ref, f32[8,128]{1,0:T(8,128)S(1)} %get-tuple-element.77.s0, ...), custom_call_target="tpu_custom_call" | custom-call | tf_op jit(solution)/shard_map/subset/pallas_call | solution.py:40
  247.7 2.7 second.10
  254.1 5.1 %subset.10 = (f32[288,1024]{1,0:T(8,128)S(1)}, f32[288,1024]{1,0:T(8,128)S(1)}, f32[8,128]{1,0:T(8,128)S(1)}) custom-call(s32[8]{0:T(128)S(1)} %stack.105.ids_ref, f32[288,1024]{1,0:T(8,128)S(1)} %get-tuple-element.82.x_ref, f32[288,1024]{1,0:T(8,128)S(1)} %get-tuple-element.83.g_ref, f32[8,128]{1,0:T(8,128)S(1)} %get-tuple-element.84.s0, ...), custom_call_target="tpu_custom_call" | custom-call | tf_op jit(solution)/shard_map/subset/pallas_call | solution.py:40
  269.9 3.3 %subset.11 = f32[288,1024]{1,0:T(8,128)S(1)} custom-call(s32[8]{0:T(128)S(1)} %stack.105.ids_ref, f32[288,1024]{1,0:T(8,128)S(1)} %get-tuple-element.88.x_ref, f32[288,1024]{1,0:T(8,128)S(1)} %get-tuple-element.89.g_ref, f32[8,128]{1,0:T(8,128)S(1)} %get-tuple-element.90.s0, f32[8,128]{1,0:T(8,128)S(1)} %collective-permute-done.73.s1, ...), custom_call_target="tpu_custom_call" | custom-call | tf_op jit(solution)/shard_map/subset/pallas_call | solution.py:40
  (196 shorter events, 108.4 us)
Async XLA Ops:
  15.7 15.0 %collective-permute-start.15 = (f32[56,1024]{1,0:T(8,128)S(1)}, f32[56,1024]{1,0:T(8,128)S(1)}, u32[]{:S(2)}, u32[]{:S(2)}) collective-permute-start(f32[56,1024]{1,0:T(8,128)S(1)} %get-tuple-element.97), channel_id=1, source_target_pairs={{0,6},{1,7},{2,4},{3,5},{4,2},{5,3},{6,0},{7,1},{8,14},{9,15},{10,... | collective-permute-start | bytes 688136 | tf_op jit(solution)/shard_map/ppermute | solution.py:70
  19.9 10.8 %collective-permute-start.14 = (f32[56,1024]{1,0:T(8,128)S(1)}, f32[56,1024]{1,0:T(8,128)S(1)}, u32[]{:S(2)}, u32[]{:S(2)}) collective-permute-start(f32[56,1024]{1,0:T(8,128)S(1)} %get-tuple-element.98), channel_id=1, source_target_pairs={{0,4},{1,5},{2,6},{3,7},{4,0},{5,1},{6,2},{7,3},{8,12},{9,13},{10,... | collective-permute-start | bytes 688136 | tf_op jit(solution)/shard_map/ppermute | solution.py:70
  20.0 11.5 %collective-permute-start.13 = (f32[56,1024]{1,0:T(8,128)S(1)}, f32[56,1024]{1,0:T(8,128)S(1)}, u32[]{:S(2)}, u32[]{:S(2)}) collective-permute-start(f32[56,1024]{1,0:T(8,128)S(1)} %get-tuple-element.99), channel_id=1, source_target_pairs={{0,2},{1,3},{2,0},{3,1},{4,6},{5,7},{6,4},{7,5},{8,10},{9,11},{10,... | collective-permute-start | bytes 688136 | tf_op jit(solution)/shard_map/ppermute | solution.py:70
  20.9 15.4 %collective-permute-start.1 = (f32[64,1024]{1,0:T(8,128)S(1)}, f32[64,1024]{1,0:T(8,128)S(1)}, u32[]{:S(2)}, u32[]{:S(2)}) collective-permute-start(f32[64,1024]{1,0:T(8,128)S(1)} %copy-done.10), channel_id=1, source_target_pairs={{0,8},{2,10},{4,12},{6,14},{8,0},{10,2},{12,4},{14,6},{16,24},{18,... | collective-permute-start | bytes 786440 | tf_op jit(solution)/shard_map/ppermute | solution.py:70
  32.1 9.9 %collective-permute-start.18 = (bf16[16,1024]{1,0:T(8,128)(2,1)S(1)}, bf16[16,1024]{1,0:T(8,128)(2,1)S(1)}, u32[]{:S(2)}, u32[]{:S(2)}) collective-permute-start(bf16[16,1024]{1,0:T(8,128)(2,1)S(1)} %get-tuple-element.56), channel_id=1, source_target_pairs={{0,6},{1,7},{2,4},{3,5},{4,2},{5,3},{6,0},{7,1},{8,14},{9,15},{10,... | collective-permute-start | bytes 98312 | tf_op jit(solution)/shard_map/ppermute | solution.py:70
  35.1 8.5 %collective-permute-start.17 = (bf16[16,1024]{1,0:T(8,128)(2,1)S(1)}, bf16[16,1024]{1,0:T(8,128)(2,1)S(1)}, u32[]{:S(2)}, u32[]{:S(2)}) collective-permute-start(bf16[16,1024]{1,0:T(8,128)(2,1)S(1)} %get-tuple-element.56), channel_id=1, source_target_pairs={{0,4},{1,5},{2,6},{3,7},{4,0},{5,1},{6,2},{7,3},{8,12},{9,13},{10,... | collective-permute-start | bytes 98312 | tf_op jit(solution)/shard_map/ppermute | solution.py:70
  35.4 8.2 %collective-permute-start.16 = (bf16[16,1024]{1,0:T(8,128)(2,1)S(1)}, bf16[16,1024]{1,0:T(8,128)(2,1)S(1)}, u32[]{:S(2)}, u32[]{:S(2)}) collective-permute-start(bf16[16,1024]{1,0:T(8,128)(2,1)S(1)} %get-tuple-element.56), channel_id=1, source_target_pairs={{0,2},{1,3},{2,0},{3,1},{4,6},{5,7},{6,4},{7,5},{8,10},{9,11},{10,... | collective-permute-start | bytes 98312 | tf_op jit(solution)/shard_map/ppermute | solution.py:70
  36.4 26.4 %collective-permute-start.3 = (f32[2,64,1024]{2,1,0:T(8,128)S(1)}, f32[2,64,1024]{2,1,0:T(8,128)S(1)}, u32[]{:S(2)}, u32[]{:S(2)}) collective-permute-start(f32[2,64,1024]{2,1,0:T(8,128)S(1)} %maximum_select_fusion.1), channel_id=1, source_target_pairs={{0,16},{2,18},{4,20},{6,22},{8,24},{10,26},{12,28},{14,30},{16,0},... | collective-permute-start | bytes 1572872 | tf_op jit(solution)/shard_map/ppermute | solution.py:70
  39.9 22.9 %collective-permute-start.4 = (f32[2,64,1024]{2,1,0:T(8,128)S(1)}, f32[2,64,1024]{2,1,0:T(8,128)S(1)}, u32[]{:S(2)}, u32[]{:S(2)}) collective-permute-start(f32[2,64,1024]{2,1,0:T(8,128)S(1)} %maximum_select_fusion.1), channel_id=1, source_target_pairs={{0,48},{2,50},{4,52},{6,54},{8,56},{10,58},{12,60},{14,62},{16,32}... | collective-permute-start | bytes 1572872 | tf_op jit(solution)/shard_map/ppermute | solution.py:70
  42.0 19.3 %collective-permute-start.2 = (f32[2,64,1024]{2,1,0:T(8,128)S(1)}, f32[2,64,1024]{2,1,0:T(8,128)S(1)}, u32[]{:S(2)}, u32[]{:S(2)}) collective-permute-start(f32[2,64,1024]{2,1,0:T(8,128)S(1)} %maximum_select_fusion.1), channel_id=1, source_target_pairs={{0,32},{2,34},{4,36},{6,38},{8,40},{10,42},{12,44},{14,46},{16,48}... | collective-permute-start | bytes 1572872 | tf_op jit(solution)/shard_map/ppermute | solution.py:70
  43.6 10.1 %collective-permute-start.20 = (bf16[4,16,1024]{2,1,0:T(8,128)(2,1)S(1)}, bf16[4,16,1024]{2,1,0:T(8,128)(2,1)S(1)}, u32[]{:S(2)}, u32[]{:S(2)}) collective-permute-start(bf16[4,16,1024]{2,1,0:T(8,128)(2,1)S(1)} %pad_maximum_fusion.4), channel_id=1, source_target_pairs={{0,64},{1,65},{2,66},{3,67},{4,68},{5,69},{6,70},{7,71},{8,72},{9,... | collective-permute-start | bytes 393224 | tf_op jit(solution)/shard_map/ppermute | solution.py:70
  45.1 7.2 %collective-permute-start.19 = (bf16[4,16,1024]{2,1,0:T(8,128)(2,1)S(1)}, bf16[4,16,1024]{2,1,0:T(8,128)(2,1)S(1)}, u32[]{:S(2)}, u32[]{:S(2)}) collective-permute-start(bf16[4,16,1024]{2,1,0:T(8,128)(2,1)S(1)} %pad_maximum_fusion.4), channel_id=1, source_target_pairs={{0,8},{1,9},{2,10},{3,11},{4,12},{5,13},{6,14},{7,15},{8,0},{9,1},... | collective-permute-start | bytes 393224 | tf_op jit(solution)/shard_map/ppermute | solution.py:70
  58.5 25.2 %collective-permute-start.24 = (bf16[16,16,1024]{2,1,0:T(8,128)(2,1)S(1)}, bf16[16,16,1024]{2,1,0:T(8,128)(2,1)S(1)}, u32[]{:S(2)}, u32[]{:S(2)}) collective-permute-start(bf16[16,16,1024]{2,1,0:T(8,128)(2,1)S(1)} %constant_dynamic-update-slice_fusion.y0), channel_id=1, source_target_pairs={{0,48},{1,49},{2,50},{3,51},{4,52},{5,53},{6,54},{7,55},{8,56},{9,... | collective-permute-start | bytes 1572872 | tf_op jit(solution)/shard_map/ppermute | solution.py:70
  59.7 24.0 %collective-permute-start.23 = (bf16[16,16,1024]{2,1,0:T(8,128)(2,1)S(1)}, bf16[16,16,1024]{2,1,0:T(8,128)(2,1)S(1)}, u32[]{:S(2)}, u32[]{:S(2)}) collective-permute-start(bf16[16,16,1024]{2,1,0:T(8,128)(2,1)S(1)} %constant_dynamic-update-slice_fusion.y0), channel_id=1, source_target_pairs={{0,32},{1,33},{2,34},{3,35},{4,36},{5,37},{6,38},{7,39},{8,40},{9,... | collective-permute-start | bytes 1572872 | tf_op jit(solution)/shard_map/ppermute | solution.py:70
  61.3 22.3 %collective-permute-start.22 = (bf16[16,16,1024]{2,1,0:T(8,128)(2,1)S(1)}, bf16[16,16,1024]{2,1,0:T(8,128)(2,1)S(1)}, u32[]{:S(2)}, u32[]{:S(2)}) collective-permute-start(bf16[16,16,1024]{2,1,0:T(8,128)(2,1)S(1)} %constant_dynamic-update-slice_fusion.y0), channel_id=1, source_target_pairs={{0,16},{1,17},{2,18},{3,19},{4,20},{5,21},{6,22},{7,23},{8,24},{9,... | collective-permute-start | bytes 1572872 | tf_op jit(solution)/shard_map/ppermute | solution.py:70
  65.6 19.1 %collective-permute-start.26 = (f32[2,16,1024]{2,1,0:T(8,128)S(1)}, f32[2,16,1024]{2,1,0:T(8,128)S(1)}, u32[]{:S(2)}, u32[]{:S(2)}) collective-permute-start(f32[2,16,1024]{2,1,0:T(8,128)S(1)} %get-tuple-element.78), channel_id=1, source_target_pairs={{0,8},{2,10},{4,12},{6,14},{8,0},{10,2},{12,4},{14,6},{16,24},{18,... | collective-permute-start | bytes 393224 | tf_op jit(solution)/shard_map/ppermute | solution.py:70
  84.4 48.5 %collective-permute-start.25 = (bf16[1024,1024]{1,0:T(8,128)(2,1)S(1)}, bf16[1024,1024]{1,0:T(8,128)(2,1)S(1)}, u32[]{:S(2)}, u32[]{:S(2)}) collective-permute-start(bf16[1024,1024]{1,0:T(8,128)(2,1)S(1)} %place_gram.1.mine_ref), channel_id=1, source_target_pairs={{0,1},{1,0},{2,3},{3,2},{4,5},{5,4},{6,7},{7,6},{8,9},{9,8},{10,11... | collective-permute-start | bytes 6291464 | tf_op jit(solution)/shard_map/ppermute | solution.py:70
  84.7 7.2 %collective-permute-start.27 = (f32[2,2,16,1024]{3,2,1,0:T(8,128)S(1)}, f32[2,2,16,1024]{3,2,1,0:T(8,128)S(1)}, u32[]{:S(2)}, u32[]{:S(2)}) collective-permute-start(f32[2,2,16,1024]{3,2,1,0:T(8,128)S(1)} %maximum_select_fusion.4), channel_id=1, source_target_pairs={{0,32},{2,34},{4,36},{6,38},{8,40},{10,42},{12,44},{14,46},{16,48}... | collective-permute-start | bytes 786440 | tf_op jit(solution)/shard_map/ppermute | solution.py:70
  88.0 8.3 %collective-permute-start.28 = (f32[2,2,16,1024]{3,2,1,0:T(8,128)S(1)}, f32[2,2,16,1024]{3,2,1,0:T(8,128)S(1)}, u32[]{:S(2)}, u32[]{:S(2)}) collective-permute-start(f32[2,2,16,1024]{3,2,1,0:T(8,128)S(1)} %maximum_select_fusion.4), channel_id=1, source_target_pairs={{0,16},{2,18},{4,20},{6,22},{8,24},{10,26},{12,28},{14,30},{16,0},... | collective-permute-start | bytes 786440 | tf_op jit(solution)/shard_map/ppermute | solution.py:70
  96.4 27.3 %collective-permute-start.32 = (f32[4,2,16,1024]{3,2,1,0:T(8,128)S(1)}, f32[4,2,16,1024]{3,2,1,0:T(8,128)S(1)}, u32[]{:S(2)}, u32[]{:S(2)}) collective-permute-start(f32[4,2,16,1024]{3,2,1,0:T(8,128)S(1)} %maximum_select_fusion.2.z0), channel_id=1, source_target_pairs={{0,6},{1,7},{2,4},{3,5},{4,2},{5,3},{6,0},{7,1},{8,14},{9,15},{10,... | collective-permute-start | bytes 1572872 | tf_op jit(solution)/shard_map/ppermute | solution.py:70
  100.0 23.6 %collective-permute-start.31 = (f32[4,2,16,1024]{3,2,1,0:T(8,128)S(1)}, f32[4,2,16,1024]{3,2,1,0:T(8,128)S(1)}, u32[]{:S(2)}, u32[]{:S(2)}) collective-permute-start(f32[4,2,16,1024]{3,2,1,0:T(8,128)S(1)} %maximum_select_fusion.2.z0), channel_id=1, source_target_pairs={{0,4},{1,5},{2,6},{3,7},{4,0},{5,1},{6,2},{7,3},{8,12},{9,13},{10,... | collective-permute-start | bytes 1572872 | tf_op jit(solution)/shard_map/ppermute | solution.py:70
  101.0 23.3 %collective-permute-start.30 = (f32[4,2,16,1024]{3,2,1,0:T(8,128)S(1)}, f32[4,2,16,1024]{3,2,1,0:T(8,128)S(1)}, u32[]{:S(2)}, u32[]{:S(2)}) collective-permute-start(f32[4,2,16,1024]{3,2,1,0:T(8,128)S(1)} %maximum_select_fusion.2.z0), channel_id=1, source_target_pairs={{0,2},{1,3},{2,0},{3,1},{4,6},{5,7},{6,4},{7,5},{8,10},{9,11},{10,... | collective-permute-start | bytes 1572872 | tf_op jit(solution)/shard_map/ppermute | solution.py:70
  147.8 8.4 %collective-permute-start.55 = (f32[2,16,1024]{2,1,0:T(8,128)S(1)}, f32[2,16,1024]{2,1,0:T(8,128)S(1)}, u32[]{:S(2)}, u32[]{:S(2)}) collective-permute-start(f32[2,16,1024]{2,1,0:T(8,128)S(1)} %collective-permute-done.54), channel_id=1, source_target_pairs={{0,8},{2,10},{4,12},{6,14},{8,0},{10,2},{12,4},{14,6},{16,24},{18,... | collective-permute-start | bytes 393224 | tf_op jit(solution)/shard_map/ppermute | solution.py:70
  157.4 8.3 %collective-permute-start.57 = (f32[2,2,16,1024]{3,2,1,0:T(8,128)S(1)}, f32[2,2,16,1024]{3,2,1,0:T(8,128)S(1)}, u32[]{:S(2)}, u32[]{:S(2)}) collective-permute-start(f32[2,2,16,1024]{3,2,1,0:T(8,128)S(1)} %maximum_select_fusion.5), channel_id=1, source_target_pairs={{0,16},{2,18},{4,20},{6,22},{8,24},{10,26},{12,28},{14,30},{16,0},... | collective-permute-start | bytes 786440 | tf_op jit(solution)/shard_map/ppermute | solution.py:70
  165.8 26.9 %collective-permute-start.61 = (f32[4,2,16,1024]{3,2,1,0:T(8,128)S(1)}, f32[4,2,16,1024]{3,2,1,0:T(8,128)S(1)}, u32[]{:S(2)}, u32[]{:S(2)}) collective-permute-start(f32[4,2,16,1024]{3,2,1,0:T(8,128)S(1)} %maximum_select_fusion.3.z0), channel_id=1, source_target_pairs={{0,6},{1,7},{2,4},{3,5},{4,2},{5,3},{6,0},{7,1},{8,14},{9,15},{10,... | collective-permute-start | bytes 1572872 | tf_op jit(solution)/shard_map/ppermute | solution.py:70
  168.8 23.9 %collective-permute-start.60 = (f32[4,2,16,1024]{3,2,1,0:T(8,128)S(1)}, f32[4,2,16,1024]{3,2,1,0:T(8,128)S(1)}, u32[]{:S(2)}, u32[]{:S(2)}) collective-permute-start(f32[4,2,16,1024]{3,2,1,0:T(8,128)S(1)} %maximum_select_fusion.3.z0), channel_id=1, source_target_pairs={{0,4},{1,5},{2,6},{3,7},{4,0},{5,1},{6,2},{7,3},{8,12},{9,13},{10,... | collective-permute-start | bytes 1572872 | tf_op jit(solution)/shard_map/ppermute | solution.py:70
  169.4 24.0 %collective-permute-start.59 = (f32[4,2,16,1024]{3,2,1,0:T(8,128)S(1)}, f32[4,2,16,1024]{3,2,1,0:T(8,128)S(1)}, u32[]{:S(2)}, u32[]{:S(2)}) collective-permute-start(f32[4,2,16,1024]{3,2,1,0:T(8,128)S(1)} %maximum_select_fusion.3.z0), channel_id=1, source_target_pairs={{0,2},{1,3},{2,0},{3,1},{4,6},{5,7},{6,4},{7,5},{8,10},{9,11},{10,... | collective-permute-start | bytes 1572872 | tf_op jit(solution)/shard_map/ppermute | solution.py:70
  170.0 27.9 %collective-permute-start.40 = (f32[8,128]{1,0:T(8,128)S(1)}, f32[8,128]{1,0:T(8,128)S(1)}, u32[]{:S(2)}, u32[]{:S(2)}) collective-permute-start(f32[8,128]{1,0:T(8,128)S(1)} %get-tuple-element.65.s0), channel_id=1, source_target_pairs={{0,65},{1,64},{2,67},{3,66},{4,69},{5,68},{6,71},{7,70},{8,73},{9,... | collective-permute-start | bytes 12296 | tf_op jit(solution)/shard_map/ppermute | solution.py:70
  170.7 27.2 %collective-permute-start.39 = (f32[8,128]{1,0:T(8,128)S(1)}, f32[8,128]{1,0:T(8,128)S(1)}, u32[]{:S(2)}, u32[]{:S(2)}) collective-permute-start(f32[8,128]{1,0:T(8,128)S(1)} %get-tuple-element.65.s0), channel_id=1, source_target_pairs={{0,64},{1,65},{2,66},{3,67},{4,68},{5,69},{6,70},{7,71},{8,72},{9,... | collective-permute-start | bytes 12296 | tf_op jit(solution)/shard_map/ppermute | solution.py:70
  194.8 40.8 %collective-permute-start.62 = (f32[2,16,1024]{2,1,0:T(8,128)}, f32[2,16,1024]{2,1,0:T(8,128)S(1)}, u32[]{:S(2)}, u32[]{:S(2)}) collective-permute-start(f32[2,16,1024]{2,1,0:T(8,128)} %get-tuple-element.91), channel_id=1, source_target_pairs={{0,1},{1,64},{2,3},{3,66},{4,5},{5,68},{6,7},{7,70},{8,9},{9,72},{... | collective-permute-start | bytes 393224 | tf_op jit(solution)/shard_map/ppermute | solution.py:70
  196.6 39.8 %collective-permute-start.63 = (f32[2,16,1024]{2,1,0:T(8,128)}, f32[2,16,1024]{2,1,0:T(8,128)}, u32[]{:S(2)}, u32[]{:S(2)}) collective-permute-start(f32[2,16,1024]{2,1,0:T(8,128)} %get-tuple-element.92), channel_id=1, source_target_pairs={{1,0},{3,2},{5,4},{7,6},{9,8},{11,10},{13,12},{15,14},{17,16},{19,... | collective-permute-start | bytes 393224 | tf_op jit(solution)/shard_map/ppermute | solution.py:70
  229.8 45.0 %collective-permute-start.47 = (f32[64,1024]{1,0:T(8,128)S(1)}, f32[64,1024]{1,0:T(8,128)S(1)}, u32[]{:S(2)}, u32[]{:S(2)}) collective-permute-start(f32[64,1024]{1,0:T(8,128)S(1)} %constant_dynamic-slice_fusion.1), channel_id=1, source_target_pairs={{0,1},{2,3},{4,5},{6,7},{8,9},{10,11},{12,13},{14,15},{16,17},{18,... | collective-permute-start | bytes 786440 | tf_op jit(solution)/shard_map/ppermute | solution.py:70
  (56 other events, 319.0 us)

commit v4 on v3

--- a/solution.py
+++ b/solution.py
@@ -36,7 +36,7 @@
     return pltpu.with_memory_space_constraint(array, pltpu.VMEM)
 
 
-def call(kernel, name, outs, ids, *arrays, scratch=()):
+def call(kernel, outs, ids, *arrays, scratch=()):
     return pl.pallas_call(
         kernel,
         out_shape=tuple(pltpu.VMEM(shape, dtype) for shape, dtype in outs),
@@ -44,7 +44,6 @@
         out_specs=tuple(WHOLE for _ in outs),
         scratch_shapes=scratch,
         compiler_params=params(12),
-        name=name,
     )(ids, *[near(a) for a in arrays])
 
 
@@ -271,7 +270,6 @@
 ):
     flux, product = rest[-2:]
     x_out = rest[0]
-    height = x_ref.shape[0]
     x_out[...] = descend(x_ref, g_ref, (s0, s1, s2, s3), step, cells)
     core = ids_ref[3]
 
@@ -314,9 +312,11 @@
     first = (2 * tm + c) * inner - HALO
     ids = jnp.stack([first, slab, z, c, keeper.astype(jnp.int32), y, h, tm])
 
-    def slabs_of_strip(unit):
+    def pair_of(unit):
         across = move(unit, flip(dh=1), keeps)
-        pair = jnp.where(h == 0, jnp.stack([unit, across]), jnp.stack([across, unit]))
+        return jnp.where(h == 0, jnp.stack([unit, across]), jnp.stack([across, unit]))
+
+    def strip_of(pair):
         one = move(pair, flip(dy=1), keeps)
         two = move(pair, flip(dy=2), keeps)
         three = move(pair, flip(dy=3), keeps)
@@ -337,7 +337,6 @@
     terms = [both[0]] + [move(both[k], flip(dz=k)) for k in range(1, QUARTERS)]
     b_unit, piece, aux = call(
         reduce_kernel,
-        "reduce_views",
         [((2, part, pixels), F32), ((part, pixels), BF16), ((8, pixels), F32)],
         ids,
         *terms,
@@ -349,15 +348,16 @@
     )
     spread = [move(plane, flip(dy=k)) for k in range(1, 4)]
 
-    def b_strip(unit_b):
-        strip = slabs_of_strip(unit_b)
+    def along_z(strip):
         return [strip] + [move(strip, flip(dz=k)) for k in range(1, 4)]
 
     def b_rows(quarters):
-        (rows,) = call(place_rows_kernel, "place_rows", [((2, inner, pixels), F32)], ids, *quarters)
+        (rows,) = call(place_rows_kernel, [((2, inner, pixels), F32)], ids, *quarters)
         return widen(rows, 1)
 
-    quarters = b_strip(b_unit)
+    strip = strip_of(pair_of(b_unit))
+    quarters = along_z(strip)
+    later = pair_of(move(after(b_unit, strip), flip(dc=1), lambda d: not keeps(d)))
 
     big = ((height, pixels), F32)
     small = ((8, RY), F32)
@@ -371,9 +371,10 @@
             move(sums, flip(dtm=1, dc=1)),
         ]
 
-    x = widen(slabs_of_strip(after(warm_volume, both)).reshape(inner, pixels), 0)
+    x = widen(strip_of(pair_of(after(warm_volume, both))).reshape(inner, pixels), 0)
+    x = after(x, strip)
     g, sums = call(
-        functools.partial(first_kernel, depth=depth), "first", [big, small], ids, x, scratch=[flux]
+        functools.partial(first_kernel, depth=depth), [big, small], ids, x, scratch=[flux]
     )
     b_wide = [None, None]
     finished = []
@@ -382,7 +383,6 @@
             step = sweep * TV_STEPS
             x, g, sums = call(
                 functools.partial(second_kernel, depth=depth, step=step, cells=cells),
-                "second",
                 [big, big, small],
                 ids,
                 x,
@@ -393,7 +393,6 @@
             if frame == 0 and sweep == 0:
                 (mine,) = call(
                     place_gram_kernel,
-                    "place_gram",
                     [((slices * 16, pixels), BF16)],
                     ids,
                     after(plane, sums),
@@ -402,12 +401,12 @@
                 other = move(mine, flip(dc=1))
                 b_wide[0] = b_rows(quarters)
             if frame == 0 and sweep == 1:
-                later = move(after(b_unit, x), flip(dc=1), lambda d: not keeps(d))
-                b_wide[1] = b_rows(b_strip(later))
+                later = along_z(after(later, x))
+            if frame == 1 and sweep == 0:
+                b_wide[1] = b_rows([after(later[0], x)] + later[1:])
             final = sweep == SWEEPS - 1 and frame == FRAMES - 1
             outs = call(
                 functools.partial(subset_kernel, depth=depth, step=step + 1, cells=cells, final=final),
-                "subset",
                 [big] if final else [big, big, small],
                 ids,
                 x,
@@ -423,6 +422,8 @@
                 x = outs[0]
             else:
                 x, g, sums = outs
+            if frame == 0 and sweep == 0:
+                later = strip_of(after(later, x))
         start = HALO + (gz % 4) * slices
         local = lax.dynamic_slice_in_dim(x, start, slices, axis=0)
         passed = move(local, flip(dc=1), keeps)

time: 279 us -> 260 us (0.932)
  waiting for transfers between devices: 102 us -> 73.8 us
  starting transfers between devices: 102 us -> 113 us
    ppermute x77, waiting for transfers between devices: 102 us -> 73.8 us  [move(): return lax.ppermute(array, AXES, pairs)]
    ppermute x77, starting transfers between devices: 102 us -> 113 us  [move(): return lax.ppermute(array, AXES, pairs)]
    unnamed x28 -> x24, local copies, waits for them, and re-layouts: 6.34 us -> 4.33 us
  transfers between devices with their start and end apart: 77 -> 77, of which waited for: 35 -> 35; matrix products, arithmetic and copies ran while one was open for 1% -> 1% of each run, Pallas kernels for 15% -> 16%
where the time goes in v4:
time: 260 us; the launch traced here: 258 us
  starting transfers between devices  113 us (43%)
  waiting for transfers between devices  73.8 us (28%)
  Pallas kernels  61.1 us (24%)
  local copies, waits for them, and re-layouts  5.31 us (2%)
  other arithmetic  3.9 us (2%)
    ppermute x77, starting transfers between devices, move(): return lax.ppermute(array, AXES, pairs)  113 us
    ppermute x77, waiting for transfers between devices, move(): return lax.ppermute(array, AXES, pairs)  73.8 us
    pallas_call x17, Pallas kernels, call(): pl.pallas_call(kernel, out_shape=tuple((pltpu.VMEM(shape, dtype) for shap...  48.9 us
    pallas_call x1, Pallas kernels, gram_products(): pl.pallas_call(gram_kernel, out_shape=(jax.ShapeDtypeStruct(shape, F32),)...  12.2 us
  transfers between devices with their start and end apart: 77, of which 35 were waited for; matrix products, arithmetic and copies ran while one was open for 1% of the time, Pallas kernels for 16%

profile of v4, /device:TPU:0, one launch (start us, length us, event | category | flops | bytes accessed | tf_op | source)
XLA Modules:
  0.0 258.3 jit_solution(10373377108740687466)
XLA Ops:
  0.7 12.2 %gram_products.1 = (f32[4,56,1024]{2,1,0:T(8,128)S(1)}, f32[4,56,1024]{2,1,0:T(8,128)S(1)}) custom-call(s32[2]{0:T(128)S(1)} %copy-done.7, s32[8]{0:T(128)S(1)} %stack.105.ids_ref, bf16[2,1024,2560]{2,1,0:T(8,128)(2,1)} %a_ref.1, bf16[2,2,64,2560]{3,2,1,0:T(8,128)(2,1)} %s1_ref.1, bf16[2,2,64,2560]{3,2,1,0:T(8,128)(2,1)} %s1_ref.1), custom_call_target="tpu_custom_call" | custom-call | tf_op jit(solution)/shard_map/gram_products/pallas_call | solution.py:157
  15.7 4.2 %collective-permute-start.9 = (f32[56,1024]{1,0:T(8,128)S(1)}, f32[56,1024]{1,0:T(8,128)S(1)}, u32[]{:S(2)}, u32[]{:S(2)}) collective-permute-start(f32[56,1024]{1,0:T(8,128)S(1)} %get-tuple-element.105), channel_id=1, source_target_pairs={{0,6},{1,7},{2,4},{3,5},{4,2},{5,3},{6,0},{7,1},{8,14},{9,15},{10,... | collective-permute-start | bytes 688136 | tf_op jit(solution)/shard_map/ppermute | solution.py:69
  20.9 4.9 %collective-permute-start.1 = (f32[64,1024]{1,0:T(8,128)S(1)}, f32[64,1024]{1,0:T(8,128)S(1)}, u32[]{:S(2)}, u32[]{:S(2)}) collective-permute-start(f32[64,1024]{1,0:T(8,128)S(1)} %copy-done.8), channel_id=1, source_target_pairs={{0,8},{2,10},{4,12},{6,14},{8,0},{10,2},{12,4},{14,6},{16,24},{18,... | collective-permute-start | bytes 786440 | tf_op jit(solution)/shard_map/ppermute | solution.py:69
  25.8 4.9 %collective-permute-done.9.a3 = f32[56,1024]{1,0:T(8,128)S(1)} collective-permute-done((f32[56,1024]{1,0:T(8,128)S(1)}, f32[56,1024]{1,0:T(8,128)S(1)}, u32[]{:S(2)}, u32[]{:S(2)}) %collective-permute-start.9) | collective-permute-done | bytes 229408 | tf_op jit(solution)/shard_map/ppermute | solution.py:69
  32.1 2.9 %collective-permute-start.22 = (bf16[16,1024]{1,0:T(8,128)(2,1)S(1)}, bf16[16,1024]{1,0:T(8,128)(2,1)S(1)}, u32[]{:S(2)}, u32[]{:S(2)}) collective-permute-start(bf16[16,1024]{1,0:T(8,128)(2,1)S(1)} %get-tuple-element.62), channel_id=1, source_target_pairs={{0,6},{1,7},{2,4},{3,5},{4,2},{5,3},{6,0},{7,1},{8,14},{9,15},{10,... | collective-permute-start | bytes 98312 | tf_op jit(solution)/shard_map/ppermute | solution.py:69
  36.3 4.9 %collective-permute-start.10 = (f32[2,16,1024]{2,1,0:T(8,128)S(1)}, f32[2,16,1024]{2,1,0:T(8,128)S(1)}, u32[]{:S(2)}, u32[]{:S(2)}) collective-permute-start(f32[2,16,1024]{2,1,0:T(8,128)S(1)} %get-tuple-element.83), channel_id=1, source_target_pairs={{0,8},{2,10},{4,12},{6,14},{8,0},{10,2},{12,4},{14,6},{16,24},{18,... | collective-permute-start | bytes 393224 | tf_op jit(solution)/shard_map/ppermute | solution.py:69
  41.3 3.5 %collective-permute-start.3 = (f32[2,64,1024]{2,1,0:T(8,128)S(1)}, f32[2,64,1024]{2,1,0:T(8,128)S(1)}, u32[]{:S(2)}, u32[]{:S(2)}) collective-permute-start(f32[2,64,1024]{2,1,0:T(8,128)S(1)} %maximum_select_fusion.1), channel_id=1, source_target_pairs={{0,16},{2,18},{4,20},{6,22},{8,24},{10,26},{12,28},{14,30},{16,0},... | collective-permute-start | bytes 1572872 | tf_op jit(solution)/shard_map/ppermute | solution.py:69
  50.5 3.4 %collective-permute-done.23 = bf16[4,16,1024]{2,1,0:T(8,128)(2,1)S(1)} collective-permute-done((bf16[4,16,1024]{2,1,0:T(8,128)(2,1)S(1)}, bf16[4,16,1024]{2,1,0:T(8,128)(2,1)S(1)}, u32[]{:S(2)}, u32[]{:S(2)}) %collective-permute-start.23) | collective-permute-done | bytes 131104 | tf_op jit(solution)/shard_map/ppermute | solution.py:69
  56.1 2.9 %collective-permute-start.12 = (f32[2,2,16,1024]{3,2,1,0:T(8,128)S(1)}, f32[2,2,16,1024]{3,2,1,0:T(8,128)S(1)}, u32[]{:S(2)}, u32[]{:S(2)}) collective-permute-start(f32[2,2,16,1024]{3,2,1,0:T(8,128)S(1)} %maximum_select_fusion.4), channel_id=1, source_target_pairs={{0,16},{2,18},{4,20},{6,22},{8,24},{10,26},{12,28},{14,30},{16,0},... | collective-permute-start | bytes 786440 | tf_op jit(solution)/shard_map/ppermute | solution.py:69
  60.4 5.6 %collective-permute-start.4 = (f32[2,64,1024]{2,1,0:T(8,128)S(1)}, f32[2,64,1024]{2,1,0:T(8,128)S(1)}, u32[]{:S(2)}, u32[]{:S(2)}) collective-permute-start(f32[2,64,1024]{2,1,0:T(8,128)S(1)} %maximum_select_fusion.1), channel_id=1, source_target_pairs={{0,48},{2,50},{4,52},{6,54},{8,56},{10,58},{12,60},{14,62},{16,32}... | collective-permute-start | bytes 1572872 | tf_op jit(solution)/shard_map/ppermute | solution.py:69
  70.4 17.4 %collective-permute-done.4 = f32[2,64,1024]{2,1,0:T(8,128)S(1)} collective-permute-done((f32[2,64,1024]{2,1,0:T(8,128)S(1)}, f32[2,64,1024]{2,1,0:T(8,128)S(1)}, u32[]{:S(2)}, u32[]{:S(2)}) %collective-permute-start.4) | collective-permute-done | bytes 524320 | tf_op jit(solution)/shard_map/ppermute | solution.py:69
  96.0 4.4 %collective-permute-start.15 = (f32[8,128]{1,0:T(8,128)S(1)}, f32[8,128]{1,0:T(8,128)S(1)}, u32[]{:S(2)}, u32[]{:S(2)}) collective-permute-start(f32[8,128]{1,0:T(8,128)S(1)} %get-tuple-element.58.s0), channel_id=1, source_target_pairs={{0,64},{1,65},{2,66},{3,67},{4,68},{5,69},{6,70},{7,71},{8,72},{9,... | collective-permute-start | bytes 12296 | tf_op jit(solution)/shard_map/ppermute | solution.py:69
  102.6 2.6 %shard_map.48 = (f32[288,1024]{1,0:T(8,128)S(1)}, f32[288,1024]{1,0:T(8,128)S(1)}, f32[8,128]{1,0:T(8,128)S(1)}) custom-call(s32[8]{0:T(128)S(1)} %stack.105.ids_ref, f32[288,1024]{1,0:T(8,128)S(1)} %pad_maximum_fusion.2.x_ref, f32[288,1024]{1,0:T(8,128)S(1)} %get-tuple-element.57.g_ref, f32[8,128]{1,0:T(8,128)S(1)} %get-tuple-element.58.s0, ...), custom_call_target="tpu_custom_call" | custom-call | tf_op jit(solution)/shard_map/pallas_call | solution.py:40
  106.5 2.7 %collective-permute-start.32 = (f32[4,2,16,1024]{3,2,1,0:T(8,128)S(1)}, f32[4,2,16,1024]{3,2,1,0:T(8,128)S(1)}, u32[]{:S(2)}, u32[]{:S(2)}) collective-permute-start(f32[4,2,16,1024]{3,2,1,0:T(8,128)S(1)} %maximum_select_fusion.2.z0), channel_id=1, source_target_pairs={{0,6},{1,7},{2,4},{3,5},{4,2},{5,3},{6,0},{7,1},{8,14},{9,15},{10,... | collective-permute-start | bytes 1572872 | tf_op jit(solution)/shard_map/ppermute | solution.py:69
  113.8 3.9 %collective-permute-start.55 = (f32[2,16,1024]{2,1,0:T(8,128)S(1)}, f32[2,16,1024]{2,1,0:T(8,128)S(1)}, u32[]{:S(2)}, u32[]{:S(2)}) collective-permute-start(f32[2,16,1024]{2,1,0:T(8,128)S(1)} %collective-permute-done.54), channel_id=1, source_target_pairs={{0,8},{2,10},{4,12},{6,14},{8,0},{10,2},{12,4},{14,6},{16,24},{18,... | collective-permute-start | bytes 393224 | tf_op jit(solution)/shard_map/ppermute | solution.py:69
  117.7 15.2 %collective-permute-done.32.z3 = f32[4,2,16,1024]{3,2,1,0:T(8,128)S(1)} collective-permute-done((f32[4,2,16,1024]{3,2,1,0:T(8,128)S(1)}, f32[4,2,16,1024]{3,2,1,0:T(8,128)S(1)}, u32[]{:S(2)}, u32[]{:S(2)}) %collective-permute-start.32) | collective-permute-done | bytes 524320 | tf_op jit(solution)/shard_map/ppermute | solution.py:69
  136.8 2.8 %collective-permute-start.19 = (f32[8,128]{1,0:T(8,128)S(1)}, f32[8,128]{1,0:T(8,128)S(1)}, u32[]{:S(2)}, u32[]{:S(2)}) collective-permute-start(f32[8,128]{1,0:T(8,128)S(1)} %get-tuple-element.61.s0), channel_id=1, source_target_pairs={{0,65},{1,64},{2,67},{3,66},{4,69},{5,68},{6,71},{7,70},{8,73},{9,... | collective-permute-start | bytes 12296 | tf_op jit(solution)/shard_map/ppermute | solution.py:69
  144.3 5.0 %shard_map.51 = (f32[288,1024]{1,0:T(8,128)S(1)}, f32[288,1024]{1,0:T(8,128)S(1)}, f32[8,128]{1,0:T(8,128)S(1)}) custom-call(s32[8]{0:T(128)S(1)} %stack.105.ids_ref, f32[288,1024]{1,0:T(8,128)S(1)} %get-tuple-element.59.x_ref, f32[288,1024]{1,0:T(8,128)S(1)} %get-tuple-element.60.g_ref, f32[8,128]{1,0:T(8,128)S(1)} %get-tuple-element.61.s0, ...), custom_call_target="tpu_custom_call" | custom-call | tf_op jit(solution)/shard_map/pallas_call | solution.py:40
  149.2 4.2 %collective-permute-start.56 = (f32[2,2,16,1024]{3,2,1,0:T(8,128)S(1)}, f32[2,2,16,1024]{3,2,1,0:T(8,128)S(1)}, u32[]{:S(2)}, u32[]{:S(2)}) collective-permute-start(f32[2,2,16,1024]{3,2,1,0:T(8,128)S(1)} %maximum_select_fusion.5), channel_id=1, source_target_pairs={{0,32},{2,34},{4,36},{6,38},{8,40},{10,42},{12,44},{14,46},{16,48}... | collective-permute-start | bytes 786440 | tf_op jit(solution)/shard_map/ppermute | solution.py:69
  153.4 2.7 %collective-permute-start.58 = (f32[2,2,16,1024]{3,2,1,0:T(8,128)S(1)}, f32[2,2,16,1024]{3,2,1,0:T(8,128)S(1)}, u32[]{:S(2)}, u32[]{:S(2)}) collective-permute-start(f32[2,2,16,1024]{3,2,1,0:T(8,128)S(1)} %maximum_select_fusion.5), channel_id=1, source_target_pairs={{0,48},{2,50},{4,52},{6,54},{8,56},{10,58},{12,60},{14,62},{16,32}... | collective-permute-start | bytes 786440 | tf_op jit(solution)/shard_map/ppermute | solution.py:69
  156.2 2.8 %collective-permute-start.57 = (f32[2,2,16,1024]{3,2,1,0:T(8,128)S(1)}, f32[2,2,16,1024]{3,2,1,0:T(8,128)S(1)}, u32[]{:S(2)}, u32[]{:S(2)}) collective-permute-start(f32[2,2,16,1024]{3,2,1,0:T(8,128)S(1)} %maximum_select_fusion.5), channel_id=1, source_target_pairs={{0,16},{2,18},{4,20},{6,22},{8,24},{10,26},{12,28},{14,30},{16,0},... | collective-permute-start | bytes 786440 | tf_op jit(solution)/shard_map/ppermute | solution.py:69
  163.2 2.6 %shard_map.52 = (f32[288,1024]{1,0:T(8,128)S(1)}, f32[288,1024]{1,0:T(8,128)S(1)}, f32[8,128]{1,0:T(8,128)S(1)}) custom-call(s32[8]{0:T(128)S(1)} %stack.105.ids_ref, f32[288,1024]{1,0:T(8,128)S(1)} %get-tuple-element.65.x_ref, f32[288,1024]{1,0:T(8,128)S(1)} %get-tuple-element.66.g_ref, f32[8,128]{1,0:T(8,128)S(1)} %get-tuple-element.67.s0, ...), custom_call_target="tpu_custom_call" | custom-call | tf_op jit(solution)/shard_map/pallas_call | solution.py:40
  166.0 2.8 %collective-permute-start.61 = (f32[4,2,16,1024]{3,2,1,0:T(8,128)S(1)}, f32[4,2,16,1024]{3,2,1,0:T(8,128)S(1)}, u32[]{:S(2)}, u32[]{:S(2)}) collective-permute-start(f32[4,2,16,1024]{3,2,1,0:T(8,128)S(1)} %maximum_select_fusion.3.z0), channel_id=1, source_target_pairs={{0,6},{1,7},{2,4},{3,5},{4,2},{5,3},{6,0},{7,1},{8,14},{9,15},{10,... | collective-permute-start | bytes 1572872 | tf_op jit(solution)/shard_map/ppermute | solution.py:69
  174.4 5.0 %shard_map.53 = (f32[288,1024]{1,0:T(8,128)S(1)}, f32[288,1024]{1,0:T(8,128)S(1)}, f32[8,128]{1,0:T(8,128)S(1)}) custom-call(s32[8]{0:T(128)S(1)} %stack.105.ids_ref, f32[288,1024]{1,0:T(8,128)S(1)} %get-tuple-element.68.x_ref, f32[288,1024]{1,0:T(8,128)S(1)} %get-tuple-element.69.g_ref, f32[8,128]{1,0:T(8,128)S(1)} %get-tuple-element.70.s0, ...), custom_call_target="tpu_custom_call" | custom-call | tf_op jit(solution)/shard_map/pallas_call | solution.py:40
  191.0 5.0 %shard_map.55 = (f32[288,1024]{1,0:T(8,128)S(1)}, f32[288,1024]{1,0:T(8,128)S(1)}, f32[8,128]{1,0:T(8,128)S(1)}) custom-call(s32[8]{0:T(128)S(1)} %stack.105.ids_ref, f32[288,1024]{1,0:T(8,128)S(1)} %get-tuple-element.74.x_ref, f32[288,1024]{1,0:T(8,128)S(1)} %get-tuple-element.75.g_ref, f32[8,128]{1,0:T(8,128)S(1)} %get-tuple-element.76.s0, ...), custom_call_target="tpu_custom_call" | custom-call | tf_op jit(solution)/shard_map/pallas_call | solution.py:40
  200.3 2.6 %shard_map.56 = (f32[288,1024]{1,0:T(8,128)S(1)}, f32[288,1024]{1,0:T(8,128)S(1)}, f32[8,128]{1,0:T(8,128)S(1)}) custom-call(s32[8]{0:T(128)S(1)} %stack.105.ids_ref, f32[288,1024]{1,0:T(8,128)S(1)} %get-tuple-element.77.x_ref, f32[288,1024]{1,0:T(8,128)S(1)} %get-tuple-element.78.g_ref, f32[8,128]{1,0:T(8,128)S(1)} %get-tuple-element.79.s0, ...), custom_call_target="tpu_custom_call" | custom-call | tf_op jit(solution)/shard_map/pallas_call | solution.py:40
  211.2 3.7 %collective-permute-start.47 = (f32[64,1024]{1,0:T(8,128)S(1)}, f32[64,1024]{1,0:T(8,128)S(1)}, u32[]{:S(2)}, u32[]{:S(2)}) collective-permute-start(f32[64,1024]{1,0:T(8,128)S(1)} %constant_dynamic-slice_fusion.1), channel_id=1, source_target_pairs={{0,1},{2,3},{4,5},{6,7},{8,9},{10,11},{12,13},{14,15},{16,17},{18,... | collective-permute-start | bytes 786440 | tf_op jit(solution)/shard_map/ppermute | solution.py:69
  219.2 5.0 %shard_map.58 = (f32[288,1024]{1,0:T(8,128)S(1)}, f32[288,1024]{1,0:T(8,128)S(1)}, f32[8,128]{1,0:T(8,128)S(1)}) custom-call(s32[8]{0:T(128)S(1)} %stack.105.ids_ref, f32[288,1024]{1,0:T(8,128)S(1)} %copy-done.4, f32[288,1024]{1,0:T(8,128)S(1)} %copy-done.6, f32[8,128]{1,0:T(8,128)S(1)} %get-tuple-element.82.s0, f32[8,128]{1,0:T(8,128)S(1)} %collective-permute-done.51.s1, ...), custom_call_target="tpu_custom_call" | custom-call | tf_op jit(solution)/shard_map/pallas_call | solution.py:40
  228.5 2.6 %shard_map.59 = (f32[288,1024]{1,0:T(8,128)S(1)}, f32[288,1024]{1,0:T(8,128)S(1)}, f32[8,128]{1,0:T(8,128)S(1)}) custom-call(s32[8]{0:T(128)S(1)} %stack.105.ids_ref, f32[288,1024]{1,0:T(8,128)S(1)} %get-tuple-element.87.x_ref, f32[288,1024]{1,0:T(8,128)S(1)} %get-tuple-element.88.g_ref, f32[8,128]{1,0:T(8,128)S(1)} %get-tuple-element.89.s0, ...), custom_call_target="tpu_custom_call" | custom-call | tf_op jit(solution)/shard_map/pallas_call | solution.py:40
  234.9 5.0 %shard_map.60 = (f32[288,1024]{1,0:T(8,128)S(1)}, f32[288,1024]{1,0:T(8,128)S(1)}, f32[8,128]{1,0:T(8,128)S(1)}) custom-call(s32[8]{0:T(128)S(1)} %stack.105.ids_ref, f32[288,1024]{1,0:T(8,128)S(1)} %get-tuple-element.90.x_ref, f32[288,1024]{1,0:T(8,128)S(1)} %get-tuple-element.91.g_ref, f32[8,128]{1,0:T(8,128)S(1)} %get-tuple-element.92.s0, ...), custom_call_target="tpu_custom_call" | custom-call | tf_op jit(solution)/shard_map/pallas_call | solution.py:40
  244.4 2.6 %shard_map.61 = (f32[288,1024]{1,0:T(8,128)S(1)}, f32[288,1024]{1,0:T(8,128)S(1)}, f32[8,128]{1,0:T(8,128)S(1)}) custom-call(s32[8]{0:T(128)S(1)} %stack.105.ids_ref, f32[288,1024]{1,0:T(8,128)S(1)} %get-tuple-element.93.x_ref, f32[288,1024]{1,0:T(8,128)S(1)} %get-tuple-element.94.g_ref, f32[8,128]{1,0:T(8,128)S(1)} %get-tuple-element.95.s0, ...), custom_call_target="tpu_custom_call" | custom-call | tf_op jit(solution)/shard_map/pallas_call | solution.py:40
  250.8 3.2 %shard_map.62 = f32[288,1024]{1,0:T(8,128)S(1)} custom-call(s32[8]{0:T(128)S(1)} %stack.105.ids_ref, f32[288,1024]{1,0:T(8,128)S(1)} %get-tuple-element.96.x_ref, f32[288,1024]{1,0:T(8,128)S(1)} %get-tuple-element.97.g_ref, f32[8,128]{1,0:T(8,128)S(1)} %get-tuple-element.98.s0, f32[8,128]{1,0:T(8,128)S(1)} %collective-permute-done.73.s1, ...), custom_call_target="tpu_custom_call" | custom-call | tf_op jit(solution)/shard_map/pallas_call | solution.py:40
  (192 shorter events, 104.1 us)
Async XLA Ops:
  15.7 15.0 %collective-permute-start.9 = (f32[56,1024]{1,0:T(8,128)S(1)}, f32[56,1024]{1,0:T(8,128)S(1)}, u32[]{:S(2)}, u32[]{:S(2)}) collective-permute-start(f32[56,1024]{1,0:T(8,128)S(1)} %get-tuple-element.105), channel_id=1, source_target_pairs={{0,6},{1,7},{2,4},{3,5},{4,2},{5,3},{6,0},{7,1},{8,14},{9,15},{10,... | collective-permute-start | bytes 688136 | tf_op jit(solution)/shard_map/ppermute | solution.py:69
  19.9 10.8 %collective-permute-start.8 = (f32[56,1024]{1,0:T(8,128)S(1)}, f32[56,1024]{1,0:T(8,128)S(1)}, u32[]{:S(2)}, u32[]{:S(2)}) collective-permute-start(f32[56,1024]{1,0:T(8,128)S(1)} %get-tuple-element.106), channel_id=1, source_target_pairs={{0,4},{1,5},{2,6},{3,7},{4,0},{5,1},{6,2},{7,3},{8,12},{9,13},{10,... | collective-permute-start | bytes 688136 | tf_op jit(solution)/shard_map/ppermute | solution.py:69
  19.9 11.5 %collective-permute-start.7 = (f32[56,1024]{1,0:T(8,128)S(1)}, f32[56,1024]{1,0:T(8,128)S(1)}, u32[]{:S(2)}, u32[]{:S(2)}) collective-permute-start(f32[56,1024]{1,0:T(8,128)S(1)} %get-tuple-element.107), channel_id=1, source_target_pairs={{0,2},{1,3},{2,0},{3,1},{4,6},{5,7},{6,4},{7,5},{8,10},{9,11},{10,... | collective-permute-start | bytes 688136 | tf_op jit(solution)/shard_map/ppermute | solution.py:69
  20.9 20.4 %collective-permute-start.1 = (f32[64,1024]{1,0:T(8,128)S(1)}, f32[64,1024]{1,0:T(8,128)S(1)}, u32[]{:S(2)}, u32[]{:S(2)}) collective-permute-start(f32[64,1024]{1,0:T(8,128)S(1)} %copy-done.8), channel_id=1, source_target_pairs={{0,8},{2,10},{4,12},{6,14},{8,0},{10,2},{12,4},{14,6},{16,24},{18,... | collective-permute-start | bytes 786440 | tf_op jit(solution)/shard_map/ppermute | solution.py:69
  32.1 12.7 %collective-permute-start.22 = (bf16[16,1024]{1,0:T(8,128)(2,1)S(1)}, bf16[16,1024]{1,0:T(8,128)(2,1)S(1)}, u32[]{:S(2)}, u32[]{:S(2)}) collective-permute-start(bf16[16,1024]{1,0:T(8,128)(2,1)S(1)} %get-tuple-element.62), channel_id=1, source_target_pairs={{0,6},{1,7},{2,4},{3,5},{4,2},{5,3},{6,0},{7,1},{8,14},{9,15},{10,... | collective-permute-start | bytes 98312 | tf_op jit(solution)/shard_map/ppermute | solution.py:69
  35.1 11.1 %collective-permute-start.21 = (bf16[16,1024]{1,0:T(8,128)(2,1)S(1)}, bf16[16,1024]{1,0:T(8,128)(2,1)S(1)}, u32[]{:S(2)}, u32[]{:S(2)}) collective-permute-start(bf16[16,1024]{1,0:T(8,128)(2,1)S(1)} %get-tuple-element.62), channel_id=1, source_target_pairs={{0,4},{1,5},{2,6},{3,7},{4,0},{5,1},{6,2},{7,3},{8,12},{9,13},{10,... | collective-permute-start | bytes 98312 | tf_op jit(solution)/shard_map/ppermute | solution.py:69
  35.3 10.8 %collective-permute-start.20 = (bf16[16,1024]{1,0:T(8,128)(2,1)S(1)}, bf16[16,1024]{1,0:T(8,128)(2,1)S(1)}, u32[]{:S(2)}, u32[]{:S(2)}) collective-permute-start(bf16[16,1024]{1,0:T(8,128)(2,1)S(1)} %get-tuple-element.62), channel_id=1, source_target_pairs={{0,2},{1,3},{2,0},{3,1},{4,6},{5,7},{6,4},{7,5},{8,10},{9,11},{10,... | collective-permute-start | bytes 98312 | tf_op jit(solution)/shard_map/ppermute | solution.py:69
  36.3 12.6 %collective-permute-start.10 = (f32[2,16,1024]{2,1,0:T(8,128)S(1)}, f32[2,16,1024]{2,1,0:T(8,128)S(1)}, u32[]{:S(2)}, u32[]{:S(2)}) collective-permute-start(f32[2,16,1024]{2,1,0:T(8,128)S(1)} %get-tuple-element.83), channel_id=1, source_target_pairs={{0,8},{2,10},{4,12},{6,14},{8,0},{10,2},{12,4},{14,6},{16,24},{18,... | collective-permute-start | bytes 393224 | tf_op jit(solution)/shard_map/ppermute | solution.py:69
  41.3 29.1 %collective-permute-start.3 = (f32[2,64,1024]{2,1,0:T(8,128)S(1)}, f32[2,64,1024]{2,1,0:T(8,128)S(1)}, u32[]{:S(2)}, u32[]{:S(2)}) collective-permute-start(f32[2,64,1024]{2,1,0:T(8,128)S(1)} %maximum_select_fusion.1), channel_id=1, source_target_pairs={{0,16},{2,18},{4,20},{6,22},{8,24},{10,26},{12,28},{14,30},{16,0},... | collective-permute-start | bytes 1572872 | tf_op jit(solution)/shard_map/ppermute | solution.py:69
  44.8 23.9 %collective-permute-start.2 = (f32[2,64,1024]{2,1,0:T(8,128)S(1)}, f32[2,64,1024]{2,1,0:T(8,128)S(1)}, u32[]{:S(2)}, u32[]{:S(2)}) collective-permute-start(f32[2,64,1024]{2,1,0:T(8,128)S(1)} %maximum_select_fusion.1), channel_id=1, source_target_pairs={{0,32},{2,34},{4,36},{6,38},{8,40},{10,42},{12,44},{14,46},{16,48}... | collective-permute-start | bytes 1572872 | tf_op jit(solution)/shard_map/ppermute | solution.py:69
  46.2 12.8 %collective-permute-start.25 = (bf16[4,16,1024]{2,1,0:T(8,128)(2,1)S(1)}, bf16[4,16,1024]{2,1,0:T(8,128)(2,1)S(1)}, u32[]{:S(2)}, u32[]{:S(2)}) collective-permute-start(bf16[4,16,1024]{2,1,0:T(8,128)(2,1)S(1)} %pad_maximum_fusion.4), channel_id=1, source_target_pairs={{0,72},{1,73},{2,74},{3,75},{4,76},{5,77},{6,78},{7,79},{8,64},{9,... | collective-permute-start | bytes 393224 | tf_op jit(solution)/shard_map/ppermute | solution.py:69
  48.9 7.1 %collective-permute-start.24 = (bf16[4,16,1024]{2,1,0:T(8,128)(2,1)S(1)}, bf16[4,16,1024]{2,1,0:T(8,128)(2,1)S(1)}, u32[]{:S(2)}, u32[]{:S(2)}) collective-permute-start(bf16[4,16,1024]{2,1,0:T(8,128)(2,1)S(1)} %pad_maximum_fusion.4), channel_id=1, source_target_pairs={{0,64},{1,65},{2,66},{3,67},{4,68},{5,69},{6,70},{7,71},{8,72},{9,... | collective-permute-start | bytes 393224 | tf_op jit(solution)/shard_map/ppermute | solution.py:69
  56.1 9.9 %collective-permute-start.12 = (f32[2,2,16,1024]{3,2,1,0:T(8,128)S(1)}, f32[2,2,16,1024]{3,2,1,0:T(8,128)S(1)}, u32[]{:S(2)}, u32[]{:S(2)}) collective-permute-start(f32[2,2,16,1024]{3,2,1,0:T(8,128)S(1)} %maximum_select_fusion.4), channel_id=1, source_target_pairs={{0,16},{2,18},{4,20},{6,22},{8,24},{10,26},{12,28},{14,30},{16,0},... | collective-permute-start | bytes 786440 | tf_op jit(solution)/shard_map/ppermute | solution.py:69
  59.0 7.1 %collective-permute-start.13 = (f32[2,2,16,1024]{3,2,1,0:T(8,128)S(1)}, f32[2,2,16,1024]{3,2,1,0:T(8,128)S(1)}, u32[]{:S(2)}, u32[]{:S(2)}) collective-permute-start(f32[2,2,16,1024]{3,2,1,0:T(8,128)S(1)} %maximum_select_fusion.4), channel_id=1, source_target_pairs={{0,48},{2,50},{4,52},{6,54},{8,56},{10,58},{12,60},{14,62},{16,32}... | collective-permute-start | bytes 786440 | tf_op jit(solution)/shard_map/ppermute | solution.py:69
  60.4 27.5 %collective-permute-start.4 = (f32[2,64,1024]{2,1,0:T(8,128)S(1)}, f32[2,64,1024]{2,1,0:T(8,128)S(1)}, u32[]{:S(2)}, u32[]{:S(2)}) collective-permute-start(f32[2,64,1024]{2,1,0:T(8,128)S(1)} %maximum_select_fusion.1), channel_id=1, source_target_pairs={{0,48},{2,50},{4,52},{6,54},{8,56},{10,58},{12,60},{14,62},{16,32}... | collective-permute-start | bytes 1572872 | tf_op jit(solution)/shard_map/ppermute | solution.py:69
  66.0 39.2 %collective-permute-start.28 = (bf16[16,16,1024]{2,1,0:T(8,128)(2,1)S(1)}, bf16[16,16,1024]{2,1,0:T(8,128)(2,1)S(1)}, u32[]{:S(2)}, u32[]{:S(2)}) collective-permute-start(bf16[16,16,1024]{2,1,0:T(8,128)(2,1)S(1)} %constant_dynamic-update-slice_fusion.y0), channel_id=1, source_target_pairs={{0,48},{1,49},{2,50},{3,51},{4,52},{5,53},{6,54},{7,55},{8,56},{9,... | collective-permute-start | bytes 1572872 | tf_op jit(solution)/shard_map/ppermute | solution.py:69
  66.1 39.1 %collective-permute-start.27 = (bf16[16,16,1024]{2,1,0:T(8,128)(2,1)S(1)}, bf16[16,16,1024]{2,1,0:T(8,128)(2,1)S(1)}, u32[]{:S(2)}, u32[]{:S(2)}) collective-permute-start(bf16[16,16,1024]{2,1,0:T(8,128)(2,1)S(1)} %constant_dynamic-update-slice_fusion.y0), channel_id=1, source_target_pairs={{0,32},{1,33},{2,34},{3,35},{4,36},{5,37},{6,38},{7,39},{8,40},{9,... | collective-permute-start | bytes 1572872 | tf_op jit(solution)/shard_map/ppermute | solution.py:69
  68.7 36.6 %collective-permute-start.26 = (bf16[16,16,1024]{2,1,0:T(8,128)(2,1)S(1)}, bf16[16,16,1024]{2,1,0:T(8,128)(2,1)S(1)}, u32[]{:S(2)}, u32[]{:S(2)}) collective-permute-start(bf16[16,16,1024]{2,1,0:T(8,128)(2,1)S(1)} %constant_dynamic-update-slice_fusion.y0), channel_id=1, source_target_pairs={{0,16},{1,17},{2,18},{3,19},{4,20},{5,21},{6,22},{7,23},{8,24},{9,... | collective-permute-start | bytes 1572872 | tf_op jit(solution)/shard_map/ppermute | solution.py:69
  106.0 38.2 %collective-permute-start.29 = (bf16[1024,1024]{1,0:T(8,128)(2,1)S(1)}, bf16[1024,1024]{1,0:T(8,128)(2,1)S(1)}, u32[]{:S(2)}, u32[]{:S(2)}) collective-permute-start(bf16[1024,1024]{1,0:T(8,128)(2,1)S(1)} %shard_map.49.mine_ref), channel_id=1, source_target_pairs={{0,1},{1,0},{2,3},{3,2},{4,5},{5,4},{6,7},{7,6},{8,9},{9,8},{10,11... | collective-permute-start | bytes 6291464 | tf_op jit(solution)/shard_map/ppermute | solution.py:69
  106.5 26.4 %collective-permute-start.32 = (f32[4,2,16,1024]{3,2,1,0:T(8,128)S(1)}, f32[4,2,16,1024]{3,2,1,0:T(8,128)S(1)}, u32[]{:S(2)}, u32[]{:S(2)}) collective-permute-start(f32[4,2,16,1024]{3,2,1,0:T(8,128)S(1)} %maximum_select_fusion.2.z0), channel_id=1, source_target_pairs={{0,6},{1,7},{2,4},{3,5},{4,2},{5,3},{6,0},{7,1},{8,14},{9,15},{10,... | collective-permute-start | bytes 1572872 | tf_op jit(solution)/shard_map/ppermute | solution.py:69
  109.2 23.7 %collective-permute-start.31 = (f32[4,2,16,1024]{3,2,1,0:T(8,128)S(1)}, f32[4,2,16,1024]{3,2,1,0:T(8,128)S(1)}, u32[]{:S(2)}, u32[]{:S(2)}) collective-permute-start(f32[4,2,16,1024]{3,2,1,0:T(8,128)S(1)} %maximum_select_fusion.2.z0), channel_id=1, source_target_pairs={{0,4},{1,5},{2,6},{3,7},{4,0},{5,1},{6,2},{7,3},{8,12},{9,13},{10,... | collective-permute-start | bytes 1572872 | tf_op jit(solution)/shard_map/ppermute | solution.py:69
  109.7 23.8 %collective-permute-start.30 = (f32[4,2,16,1024]{3,2,1,0:T(8,128)S(1)}, f32[4,2,16,1024]{3,2,1,0:T(8,128)S(1)}, u32[]{:S(2)}, u32[]{:S(2)}) collective-permute-start(f32[4,2,16,1024]{3,2,1,0:T(8,128)S(1)} %maximum_select_fusion.2.z0), channel_id=1, source_target_pairs={{0,2},{1,3},{2,0},{3,1},{4,6},{5,7},{6,4},{7,5},{8,10},{9,11},{10,... | collective-permute-start | bytes 1572872 | tf_op jit(solution)/shard_map/ppermute | solution.py:69
  113.8 25.9 %collective-permute-start.55 = (f32[2,16,1024]{2,1,0:T(8,128)S(1)}, f32[2,16,1024]{2,1,0:T(8,128)S(1)}, u32[]{:S(2)}, u32[]{:S(2)}) collective-permute-start(f32[2,16,1024]{2,1,0:T(8,128)S(1)} %collective-permute-done.54), channel_id=1, source_target_pairs={{0,8},{2,10},{4,12},{6,14},{8,0},{10,2},{12,4},{14,6},{16,24},{18,... | collective-permute-start | bytes 393224 | tf_op jit(solution)/shard_map/ppermute | solution.py:69
  134.2 7.2 %collective-permute-start.33 = (f32[2,16,1024]{2,1,0:T(8,128)S(1)}, f32[2,16,1024]{2,1,0:T(8,128)S(1)}, u32[]{:S(2)}, u32[]{:S(2)}) collective-permute-start(f32[2,16,1024]{2,1,0:T(8,128)S(1)} %get-tuple-element.101), channel_id=1, source_target_pairs={{0,1},{1,64},{2,3},{3,66},{4,5},{5,68},{6,7},{7,70},{8,9},{9,72},{... | collective-permute-start | bytes 393224 | tf_op jit(solution)/shard_map/ppermute | solution.py:69
  149.2 16.6 %collective-permute-start.56 = (f32[2,2,16,1024]{3,2,1,0:T(8,128)S(1)}, f32[2,2,16,1024]{3,2,1,0:T(8,128)S(1)}, u32[]{:S(2)}, u32[]{:S(2)}) collective-permute-start(f32[2,2,16,1024]{3,2,1,0:T(8,128)S(1)} %maximum_select_fusion.5), channel_id=1, source_target_pairs={{0,32},{2,34},{4,36},{6,38},{8,40},{10,42},{12,44},{14,46},{16,48}... | collective-permute-start | bytes 786440 | tf_op jit(solution)/shard_map/ppermute | solution.py:69
  153.4 12.5 %collective-permute-start.58 = (f32[2,2,16,1024]{3,2,1,0:T(8,128)S(1)}, f32[2,2,16,1024]{3,2,1,0:T(8,128)S(1)}, u32[]{:S(2)}, u32[]{:S(2)}) collective-permute-start(f32[2,2,16,1024]{3,2,1,0:T(8,128)S(1)} %maximum_select_fusion.5), channel_id=1, source_target_pairs={{0,48},{2,50},{4,52},{6,54},{8,56},{10,58},{12,60},{14,62},{16,32}... | collective-permute-start | bytes 786440 | tf_op jit(solution)/shard_map/ppermute | solution.py:69
  156.2 9.8 %collective-permute-start.57 = (f32[2,2,16,1024]{3,2,1,0:T(8,128)S(1)}, f32[2,2,16,1024]{3,2,1,0:T(8,128)S(1)}, u32[]{:S(2)}, u32[]{:S(2)}) collective-permute-start(f32[2,2,16,1024]{3,2,1,0:T(8,128)S(1)} %maximum_select_fusion.5), channel_id=1, source_target_pairs={{0,16},{2,18},{4,20},{6,22},{8,24},{10,26},{12,28},{14,30},{16,0},... | collective-permute-start | bytes 786440 | tf_op jit(solution)/shard_map/ppermute | solution.py:69
  166.0 39.0 %collective-permute-start.61 = (f32[4,2,16,1024]{3,2,1,0:T(8,128)S(1)}, f32[4,2,16,1024]{3,2,1,0:T(8,128)S(1)}, u32[]{:S(2)}, u32[]{:S(2)}) collective-permute-start(f32[4,2,16,1024]{3,2,1,0:T(8,128)S(1)} %maximum_select_fusion.3.z0), channel_id=1, source_target_pairs={{0,6},{1,7},{2,4},{3,5},{4,2},{5,3},{6,0},{7,1},{8,14},{9,15},{10,... | collective-permute-start | bytes 1572872 | tf_op jit(solution)/shard_map/ppermute | solution.py:69
  168.8 36.2 %collective-permute-start.60 = (f32[4,2,16,1024]{3,2,1,0:T(8,128)S(1)}, f32[4,2,16,1024]{3,2,1,0:T(8,128)S(1)}, u32[]{:S(2)}, u32[]{:S(2)}) collective-permute-start(f32[4,2,16,1024]{3,2,1,0:T(8,128)S(1)} %maximum_select_fusion.3.z0), channel_id=1, source_target_pairs={{0,4},{1,5},{2,6},{3,7},{4,0},{5,1},{6,2},{7,3},{8,12},{9,13},{10,... | collective-permute-start | bytes 1572872 | tf_op jit(solution)/shard_map/ppermute | solution.py:69
  169.3 35.7 %collective-permute-start.59 = (f32[4,2,16,1024]{3,2,1,0:T(8,128)S(1)}, f32[4,2,16,1024]{3,2,1,0:T(8,128)S(1)}, u32[]{:S(2)}, u32[]{:S(2)}) collective-permute-start(f32[4,2,16,1024]{3,2,1,0:T(8,128)S(1)} %maximum_select_fusion.3.z0), channel_id=1, source_target_pairs={{0,2},{1,3},{2,0},{3,1},{4,6},{5,7},{6,4},{7,5},{8,10},{9,11},{10,... | collective-permute-start | bytes 1572872 | tf_op jit(solution)/shard_map/ppermute | solution.py:69
  207.7 8.4 %collective-permute-start.62 = (f32[2,16,1024]{2,1,0:T(8,128)}, f32[2,16,1024]{2,1,0:T(8,128)S(1)}, u32[]{:S(2)}, u32[]{:S(2)}) collective-permute-start(f32[2,16,1024]{2,1,0:T(8,128)} %get-tuple-element.99), channel_id=1, source_target_pairs={{0,1},{1,64},{2,3},{3,66},{4,5},{5,68},{6,7},{7,70},{8,9},{9,72},{... | collective-permute-start | bytes 393224 | tf_op jit(solution)/shard_map/ppermute | solution.py:69
  211.2 45.1 %collective-permute-start.47 = (f32[64,1024]{1,0:T(8,128)S(1)}, f32[64,1024]{1,0:T(8,128)S(1)}, u32[]{:S(2)}, u32[]{:S(2)}) collective-permute-start(f32[64,1024]{1,0:T(8,128)S(1)} %constant_dynamic-slice_fusion.1), channel_id=1, source_target_pairs={{0,1},{2,3},{4,5},{6,7},{8,9},{10,11},{12,13},{14,15},{16,17},{18,... | collective-permute-start | bytes 786440 | tf_op jit(solution)/shard_map/ppermute | solution.py:69
  (54 other events, 219.0 us)

commit v5 on v4

--- a/solution.py
+++ b/solution.py
@@ -85,7 +85,7 @@
     return rule
 
 
-def gram_kernel(order_ref, ids_ref, a_ref, s0_ref, s1_ref, own_ref, send_ref, acc):
+def gram_kernel(order_ref, ids_ref, a_ref, s0_ref, s1_ref, own_ref, send_ref, acc, level_ref):
     n = pl.program_id(0)
     d = pl.program_id(1)
     rows = s0_ref.shape[0]
@@ -93,18 +93,20 @@
     ray = jnp.sum(tile.astype(F32), axis=0, keepdims=True)
     inverse = 1.0 / ray
     lhs = []
-    low = []
-    for ref in (s0_ref, s1_ref):
+    for t, ref in enumerate((s0_ref, s1_ref)):
         scaled = ref[...].astype(F32) * inverse
-        high = scaled.astype(BF16)
-        lhs.append(high)
-        low.append((scaled - high.astype(F32)).astype(BF16))
+
+        @pl.when(d == 0)
+        def _():
+            mean = jnp.sum(scaled, axis=1, keepdims=True) / CHUNK
+            level_ref[t] = jnp.broadcast_to(mean, level_ref.shape[1:])
+
+        lhs.append((scaled - level_ref[t, :, 0:1]).astype(BF16))
     mine = a_ref[pl.ds(pl.multiple_of(ids_ref[1] * rows, rows), rows), :]
     lhs.append((mine.astype(F32) * inverse).astype(BF16))
     lhs.append(jnp.ones((16, CHUNK), BF16))
-    stack = jnp.concatenate(lhs + low, axis=0)
+    stack = jnp.concatenate(lhs, axis=0)
     product = lax.dot_general(stack, tile, (((1,), (1,)), ((), ())), preferred_element_type=F32)
-    top = 3 * rows + 16
 
     @pl.when(d == 0)
     def _():
@@ -124,9 +126,10 @@
                 @pl.when(ids_ref[4] == who)
                 def _():
                     for quarter in range(QUARTERS):
-                        lo = t * rows + quarter * part
+                        lo = quarter * part
                         ref[jnp.bitwise_xor(ids_ref[2], quarter), at, :] = (
-                            acc[lo : lo + part] + acc[top + lo : top + lo + part]
+                            acc[t * rows + lo : t * rows + lo + part]
+                            + level_ref[t, lo : lo + part, 0:1] * acc[3 * rows : 3 * rows + 1]
                         )
 
         for ref, mine_too in ((own_ref, True), (send_ref, False)):
@@ -166,7 +169,7 @@
                 pl.BlockSpec((None, None, rows, CHUNK), lambda n, d, o, s: (1, o[n], 0, d)),
             ],
             out_specs=(out, out),
-            scratch_shapes=[pltpu.VMEM((5 * rows + 16, pixels), F32)],
+            scratch_shapes=[pltpu.VMEM((3 * rows + 16, pixels), F32), pltpu.VMEM((FRAMES, rows, RY), F32)],
         ),
         compiler_params=params(24),
         name="gram_products",
@@ -219,8 +222,15 @@
     height, pixels = x_ref.shape
     blocks = pixels // RY
     lane = lax.broadcasted_iota(jnp.int32, (height, RY), 1)
-    zindex = first + lax.broadcasted_iota(jnp.int32, (height, RY), 0)
-    inside = ((zindex >= 0) & (zindex < depth - 1)).astype(F32)
+
+    @pl.when(first < 0)
+    def _():
+        x_ref[HALO - 1 : HALO, :] = x_ref[HALO : HALO + 1, :]
+
+    @pl.when(first + height > depth)
+    def _():
+        x_ref[height - HALO : height - HALO + 1, :] = x_ref[height - HALO - 1 : height - HALO, :]
+
     column = (lane < RY - 1).astype(F32)
     flux_ref[...] = jnp.zeros_like(flux_ref)
 
@@ -228,12 +238,12 @@
         here_at = pl.ds(pl.multiple_of(i * RY, RY), RY)
         next_at = pl.ds(pl.multiple_of(jnp.minimum(i + 1, blocks - 1) * RY, RY), RY)
         here = x_ref[:, here_at]
-        dz = (pltpu.roll(here, height - 1, 0) - here) * inside
+        dz = pltpu.roll(here, height - 1, 0) - here
         dc = (pltpu.roll(here, RY - 1, 1) - here) * column
         di = x_ref[:, next_at] - here
         square = dz * dz + dc * dc + di * di + SMOOTHING
         r = lax.rsqrt(square)
-        r = r * (1.5 - 0.5 * square * r * r)
+        r = r * (1.5 - (0.5 * square) * (r * r))
         fz = dz * r
         fc = dc * r
         fi = di * r
@@ -256,8 +266,9 @@
     return x_ref[...] - factor * g_ref[...]
 
 
-def first_kernel(ids_ref, x_ref, g_ref, ss_ref, flux, *, depth):
-    tv_into(x_ref, g_ref, ss_ref, flux, ids_ref[0], depth)
+def first_kernel(ids_ref, x_ref, x_out, g_ref, ss_ref, flux, *, depth):
+    x_out[...] = x_ref[...]
+    tv_into(x_out, g_ref, ss_ref, flux, ids_ref[0], depth)
 
 
 def second_kernel(ids_ref, x_ref, g_ref, s0, s1, s2, s3, x_out, g_out, ss_out, flux, *, depth, step, cells):
@@ -317,9 +328,7 @@
         return jnp.where(h == 0, jnp.stack([unit, across]), jnp.stack([across, unit]))
 
     def strip_of(pair):
-        one = move(pair, flip(dy=1), keeps)
-        two = move(pair, flip(dy=2), keeps)
-        three = move(pair, flip(dy=3), keeps)
+        one, two, three = (move(pair, flip(dy=k), keeps) for k in range(1, 4))
         same = jnp.where(keeper, pair, two)
         flipped = jnp.where(keeper, one, three)
         return jnp.where(
@@ -332,20 +341,17 @@
         high = move(lax.slice_in_dim(array, 0, HALO, axis=dim), strip_step(-1))
         return jnp.concatenate([low, array, high], axis=dim)
 
+    warm_pair = pair_of(warm_volume)
     own, send = gram_products(view_order, ids, projector, sinogram)
     both = own + move(send, flip(dc=1))
     terms = [both[0]] + [move(both[k], flip(dz=k)) for k in range(1, QUARTERS)]
     b_unit, piece, aux = call(
-        reduce_kernel,
-        [((2, part, pixels), F32), ((part, pixels), BF16), ((8, pixels), F32)],
-        ids,
-        *terms,
+        reduce_kernel, [((2, part, pixels), F32), ((part, pixels), BF16), ((8, pixels), F32)], ids, *terms
     )
 
     line = jnp.stack([piece] + [move(piece, flip(dz=k)) for k in range(1, 4)])
-    plane = jnp.concatenate(
-        [line, move(line, flip(dh=1)), move(line, flip(dtm=1)), move(line, flip(dtm=1, dh=1))]
-    )
+    flips = (flip(dh=1), flip(dtm=1), flip(dtm=1, dh=1))
+    plane = jnp.concatenate([line] + [move(line, f) for f in flips])
     spread = [move(plane, flip(dy=k)) for k in range(1, 4)]
 
     def along_z(strip):
@@ -357,7 +363,8 @@
 
     strip = strip_of(pair_of(b_unit))
     quarters = along_z(strip)
-    later = pair_of(move(after(b_unit, strip), flip(dc=1), lambda d: not keeps(d)))
+    later = move(after(b_unit, strip), flip(dc=1), lambda d: not keeps(d))
+    later = along_z(strip_of(pair_of(later)))
 
     big = ((height, pixels), F32)
     small = ((8, RY), F32)
@@ -371,11 +378,9 @@
             move(sums, flip(dtm=1, dc=1)),
         ]
 
-    x = widen(strip_of(pair_of(after(warm_volume, both))).reshape(inner, pixels), 0)
+    x = widen(strip_of(after(warm_pair, both)).reshape(inner, pixels), 0)
     x = after(x, strip)
-    g, sums = call(
-        functools.partial(first_kernel, depth=depth), [big, small], ids, x, scratch=[flux]
-    )
+    x, g, sums = call(functools.partial(first_kernel, depth=depth), [big, big, small], ids, x, scratch=[flux])
     b_wide = [None, None]
     finished = []
     for frame in range(FRAMES):
@@ -391,18 +396,10 @@
                 scratch=[flux],
             )
             if frame == 0 and sweep == 0:
-                (mine,) = call(
-                    place_gram_kernel,
-                    [((slices * 16, pixels), BF16)],
-                    ids,
-                    after(plane, sums),
-                    *spread,
-                )
+                (mine,) = call(place_gram_kernel, [((slices * 16, pixels), BF16)], ids, after(plane, sums), *spread)
                 other = move(mine, flip(dc=1))
                 b_wide[0] = b_rows(quarters)
-            if frame == 0 and sweep == 1:
-                later = along_z(after(later, x))
-            if frame == 1 and sweep == 0:
+            if frame == 0 and sweep == 2:
                 b_wide[1] = b_rows([after(later[0], x)] + later[1:])
             final = sweep == SWEEPS - 1 and frame == FRAMES - 1
             outs = call(
@@ -422,8 +419,6 @@
                 x = outs[0]
             else:
                 x, g, sums = outs
-            if frame == 0 and sweep == 0:
-                later = strip_of(after(later, x))
         start = HALO + (gz % 4) * slices
         local = lax.dynamic_slice_in_dim(x, start, slices, axis=0)
         passed = move(local, flip(dc=1), keeps)

time: 260 us -> 267 us (1.027)
  waiting for transfers between devices: 73.8 us -> 82.1 us
  starting transfers between devices: 113 us -> 108 us
  local copies, waits for them, and re-layouts: 5.31 us -> 8.63 us
    ppermute x77, waiting for transfers between devices: 73.8 us -> 82.1 us  [move(): return lax.ppermute(array, AXES, pairs)]
    ppermute x77, starting transfers between devices: 113 us -> 108 us  [move(): return lax.ppermute(array, AXES, pairs)]
    unnamed x24 -> x28, local copies, waits for them, and re-layouts: 4.33 us -> 7.66 us
  transfers between devices with their start and end apart: 77 -> 77, of which waited for: 35 -> 40; matrix products, arithmetic and copies ran while one was open for 1% -> 1% of each run, Pallas kernels for 16% -> 18%
where the time goes in v5:
time: 267 us; the launch traced here: 265 us
  starting transfers between devices  108 us (40%)
  waiting for transfers between devices  82.1 us (31%)
  Pallas kernels  62.4 us (23%)
  local copies, waits for them, and re-layouts  8.63 us (3%)
  other arithmetic  3.25 us (1%)
    ppermute x77, starting transfers between devices, move(): return lax.ppermute(array, AXES, pairs)  108 us
    ppermute x77, waiting for transfers between devices, move(): return lax.ppermute(array, AXES, pairs)  82.1 us
    pallas_call x17, Pallas kernels, call(): pl.pallas_call(kernel, out_shape=tuple((pltpu.VMEM(shape, dtype) for shap...  49.4 us
    pallas_call x1, Pallas kernels, gram_products(): pl.pallas_call(gram_kernel, out_shape=(jax.ShapeDtypeStruct(shape, F32),)...  12.9 us
    unnamed x28, local copies, waits for them, and re-layouts  7.66 us
  transfers between devices with their start and end apart: 77, of which 40 were waited for; matrix products, arithmetic and copies ran while one was open for 1% of the time, Pallas kernels for 18%

profile of v5, /device:TPU:0, one launch (start us, length us, event | category | flops | bytes accessed | tf_op | source)
XLA Modules:
  0.0 264.8 jit_solution(5701841906649015230)
XLA Ops:
  0.7 12.9 %gram_products.1 = (f32[4,56,1024]{2,1,0:T(8,128)S(1)}, f32[4,56,1024]{2,1,0:T(8,128)S(1)}) custom-call(s32[2]{0:T(128)S(1)} %copy-done.9, s32[8]{0:T(128)S(1)} %stack.105.ids_ref, bf16[2,1024,2560]{2,1,0:T(8,128)(2,1)} %a_ref.1, bf16[2,2,64,2560]{3,2,1,0:T(8,128)(2,1)} %s1_ref.1, bf16[2,2,64,2560]{3,2,1,0:T(8,128)(2,1)} %s1_ref.1), custom_call_target="tpu_custom_call" | custom-call | tf_op jit(solution)/shard_map/gram_products/pallas_call | solution.py:160
  13.8 5.0 %collective-permute-start = (f32[64,1024]{1,0:T(8,128)S(1)}, f32[64,1024]{1,0:T(8,128)S(1)}, u32[]{:S(2)}, u32[]{:S(2)}) collective-permute-start(f32[64,1024]{1,0:T(8,128)S(1)} %copy-done.10), channel_id=1, source_target_pairs={{0,8},{2,10},{4,12},{6,14},{8,0},{10,2},{12,4},{14,6},{16,24},{18,... | collective-permute-start | bytes 786440 | tf_op jit(solution)/shard_map/ppermute | solution.py:69
  21.1 3.6 %collective-permute-start.8 = (f32[56,1024]{1,0:T(8,128)S(1)}, f32[56,1024]{1,0:T(8,128)S(1)}, u32[]{:S(2)}, u32[]{:S(2)}) collective-permute-start(f32[56,1024]{1,0:T(8,128)S(1)} %get-tuple-element.104), channel_id=1, source_target_pairs={{0,4},{1,5},{2,6},{3,7},{4,0},{5,1},{6,2},{7,3},{8,12},{9,13},{10,... | collective-permute-start | bytes 688136 | tf_op jit(solution)/shard_map/ppermute | solution.py:69
  29.9 2.7 %collective-permute-done.8.a2 = f32[56,1024]{1,0:T(8,128)S(1)} collective-permute-done((f32[56,1024]{1,0:T(8,128)S(1)}, f32[56,1024]{1,0:T(8,128)S(1)}, u32[]{:S(2)}, u32[]{:S(2)}) %collective-permute-start.8) | collective-permute-done | bytes 229408 | tf_op jit(solution)/shard_map/ppermute | solution.py:69
  37.3 3.3 %collective-permute-start.22 = (bf16[16,1024]{1,0:T(8,128)(2,1)S(1)}, bf16[16,1024]{1,0:T(8,128)(2,1)S(1)}, u32[]{:S(2)}, u32[]{:S(2)}) collective-permute-start(bf16[16,1024]{1,0:T(8,128)(2,1)S(1)} %get-tuple-element.62), channel_id=1, source_target_pairs={{0,6},{1,7},{2,4},{3,5},{4,2},{5,3},{6,0},{7,1},{8,14},{9,15},{10,... | collective-permute-start | bytes 98312 | tf_op jit(solution)/shard_map/ppermute | solution.py:69
  40.6 5.9 %collective-permute-start.4 = (f32[2,64,1024]{2,1,0:T(8,128)S(1)}, f32[2,64,1024]{2,1,0:T(8,128)S(1)}, u32[]{:S(2)}, u32[]{:S(2)}) collective-permute-start(f32[2,64,1024]{2,1,0:T(8,128)S(1)} %maximum_select_fusion.1), channel_id=1, source_target_pairs={{0,48},{2,50},{4,52},{6,54},{8,56},{10,58},{12,60},{14,62},{16,32}... | collective-permute-start | bytes 1572872 | tf_op jit(solution)/shard_map/ppermute | solution.py:69
  46.5 4.2 %collective-permute-start.10 = (f32[2,16,1024]{2,1,0:T(8,128)S(1)}, f32[2,16,1024]{2,1,0:T(8,128)S(1)}, u32[]{:S(2)}, u32[]{:S(2)}) collective-permute-start(f32[2,16,1024]{2,1,0:T(8,128)S(1)} %get-tuple-element.83), channel_id=1, source_target_pairs={{0,8},{2,10},{4,12},{6,14},{8,0},{10,2},{12,4},{14,6},{16,24},{18,... | collective-permute-start | bytes 393224 | tf_op jit(solution)/shard_map/ppermute | solution.py:69
  52.1 2.8 %collective-permute-done.10 = f32[2,16,1024]{2,1,0:T(8,128)S(1)} collective-permute-done((f32[2,16,1024]{2,1,0:T(8,128)S(1)}, f32[2,16,1024]{2,1,0:T(8,128)S(1)}, u32[]{:S(2)}, u32[]{:S(2)}) %collective-permute-start.10) | collective-permute-done | bytes 131104 | tf_op jit(solution)/shard_map/ppermute | solution.py:69
  71.4 4.6 %collective-permute-start.28 = (bf16[16,16,1024]{2,1,0:T(8,128)(2,1)S(1)}, bf16[16,16,1024]{2,1,0:T(8,128)(2,1)S(1)}, u32[]{:S(2)}, u32[]{:S(2)}) collective-permute-start(bf16[16,16,1024]{2,1,0:T(8,128)(2,1)S(1)} %constant_dynamic-update-slice_fusion.y0), channel_id=1, source_target_pairs={{0,48},{1,49},{2,50},{3,51},{4,52},{5,53},{6,54},{7,55},{8,56},{9,... | collective-permute-start | bytes 1572872 | tf_op jit(solution)/shard_map/ppermute | solution.py:69
  78.6 2.7 %collective-permute-start.14 = (f32[8,128]{1,0:T(8,128)S(1)}, f32[8,128]{1,0:T(8,128)S(1)}, u32[]{:S(2)}, u32[]{:S(2)}) collective-permute-start(f32[8,128]{1,0:T(8,128)S(1)} %get-tuple-element.58.s0), channel_id=1, source_target_pairs={{0,1},{1,0},{2,3},{3,2},{4,5},{5,4},{6,7},{7,6},{8,9},{9,8},{10,11... | collective-permute-start | bytes 12296 | tf_op jit(solution)/shard_map/ppermute | solution.py:69
  87.9 4.1 %collective-permute-done.27.y2 = bf16[16,16,1024]{2,1,0:T(8,128)(2,1)S(1)} collective-permute-done((bf16[16,16,1024]{2,1,0:T(8,128)(2,1)S(1)}, bf16[16,16,1024]{2,1,0:T(8,128)(2,1)S(1)}, u32[]{:S(2)}, u32[]{:S(2)}) %collective-permute-start.27) | collective-permute-done | bytes 524320 | tf_op jit(solution)/shard_map/ppermute | solution.py:69
  92.0 5.8 %collective-permute-done.28.y3 = bf16[16,16,1024]{2,1,0:T(8,128)(2,1)S(1)} collective-permute-done((bf16[16,16,1024]{2,1,0:T(8,128)(2,1)S(1)}, bf16[16,16,1024]{2,1,0:T(8,128)(2,1)S(1)}, u32[]{:S(2)}, u32[]{:S(2)}) %collective-permute-start.28) | collective-permute-done | bytes 524320 | tf_op jit(solution)/shard_map/ppermute | solution.py:69
  104.6 4.5 %collective-permute-start.55 = (f32[2,16,1024]{2,1,0:T(8,128)S(1)}, f32[2,16,1024]{2,1,0:T(8,128)S(1)}, u32[]{:S(2)}, u32[]{:S(2)}) collective-permute-start(f32[2,16,1024]{2,1,0:T(8,128)S(1)} %collective-permute-done.54), channel_id=1, source_target_pairs={{0,8},{2,10},{4,12},{6,14},{8,0},{10,2},{12,4},{14,6},{16,24},{18,... | collective-permute-start | bytes 393224 | tf_op jit(solution)/shard_map/ppermute | solution.py:69
  109.1 3.9 %collective-permute-done.55 = f32[2,16,1024]{2,1,0:T(8,128)S(1)} collective-permute-done((f32[2,16,1024]{2,1,0:T(8,128)S(1)}, f32[2,16,1024]{2,1,0:T(8,128)S(1)}, u32[]{:S(2)}, u32[]{:S(2)}) %collective-permute-start.55) | collective-permute-done | bytes 131104 | tf_op jit(solution)/shard_map/ppermute | solution.py:69
  119.1 3.5 %collective-permute-done.57 = f32[2,2,16,1024]{3,2,1,0:T(8,128)S(1)} collective-permute-done((f32[2,2,16,1024]{3,2,1,0:T(8,128)S(1)}, f32[2,2,16,1024]{3,2,1,0:T(8,128)S(1)}, u32[]{:S(2)}, u32[]{:S(2)}) %collective-permute-start.57) | collective-permute-done | bytes 262176 | tf_op jit(solution)/shard_map/ppermute | solution.py:69
  123.6 7.2 %collective-permute-done.30.z1 = f32[4,2,16,1024]{3,2,1,0:T(8,128)S(1)} collective-permute-done((f32[4,2,16,1024]{3,2,1,0:T(8,128)S(1)}, f32[4,2,16,1024]{3,2,1,0:T(8,128)S(1)}, u32[]{:S(2)}, u32[]{:S(2)}) %collective-permute-start.30) | collective-permute-done | bytes 524320 | tf_op jit(solution)/shard_map/ppermute | solution.py:69
  131.1 9.8 %collective-permute-done.31.z2 = f32[4,2,16,1024]{3,2,1,0:T(8,128)S(1)} collective-permute-done((f32[4,2,16,1024]{3,2,1,0:T(8,128)S(1)}, f32[4,2,16,1024]{3,2,1,0:T(8,128)S(1)}, u32[]{:S(2)}, u32[]{:S(2)}) %collective-permute-start.31) | collective-permute-done | bytes 524320 | tf_op jit(solution)/shard_map/ppermute | solution.py:69
  140.9 3.4 %collective-permute-done.32.z3 = f32[4,2,16,1024]{3,2,1,0:T(8,128)S(1)} collective-permute-done((f32[4,2,16,1024]{3,2,1,0:T(8,128)S(1)}, f32[4,2,16,1024]{3,2,1,0:T(8,128)S(1)}, u32[]{:S(2)}, u32[]{:S(2)}) %collective-permute-start.32) | collective-permute-done | bytes 524320 | tf_op jit(solution)/shard_map/ppermute | solution.py:69
  151.3 3.5 %collective-permute-done.34 = f32[2,16,1024]{2,1,0:T(8,128)S(1)} collective-permute-done((f32[2,16,1024]{2,1,0:T(8,128)S(1)}, f32[2,16,1024]{2,1,0:T(8,128)S(1)}, u32[]{:S(2)}, u32[]{:S(2)}) %collective-permute-start.34) | collective-permute-done | bytes 131104 | tf_op jit(solution)/shard_map/ppermute | solution.py:69
  158.6 5.0 %shard_map.51 = (f32[288,1024]{1,0:T(8,128)S(1)}, f32[288,1024]{1,0:T(8,128)S(1)}, f32[8,128]{1,0:T(8,128)S(1)}) custom-call(s32[8]{0:T(128)S(1)} %stack.105.ids_ref, f32[288,1024]{1,0:T(8,128)S(1)} %get-tuple-element.59.x_ref, f32[288,1024]{1,0:T(8,128)S(1)} %get-tuple-element.60.g_ref, f32[8,128]{1,0:T(8,128)S(1)} %get-tuple-element.61.s0, ...), custom_call_target="tpu_custom_call" | custom-call | tf_op jit(solution)/shard_map/pallas_call | solution.py:40
  163.7 4.1 %collective-permute-start.35 = (f32[8,128]{1,0:T(8,128)S(1)}, f32[8,128]{1,0:T(8,128)S(1)}, u32[]{:S(2)}, u32[]{:S(2)}) collective-permute-start(f32[8,128]{1,0:T(8,128)S(1)} %get-tuple-element.67.s0), channel_id=1, source_target_pairs={{0,1},{1,0},{2,3},{3,2},{4,5},{5,4},{6,7},{7,6},{8,9},{9,8},{10,11... | collective-permute-start | bytes 12296 | tf_op jit(solution)/shard_map/ppermute | solution.py:69
  171.6 2.6 shard_map.52
  178.8 5.0 %shard_map.53 = (f32[288,1024]{1,0:T(8,128)S(1)}, f32[288,1024]{1,0:T(8,128)S(1)}, f32[8,128]{1,0:T(8,128)S(1)}) custom-call(s32[8]{0:T(128)S(1)} %stack.105.ids_ref, f32[288,1024]{1,0:T(8,128)S(1)} %get-tuple-element.68.x_ref, f32[288,1024]{1,0:T(8,128)S(1)} %get-tuple-element.69.g_ref, f32[8,128]{1,0:T(8,128)S(1)} %get-tuple-element.70.s0, ...), custom_call_target="tpu_custom_call" | custom-call | tf_op jit(solution)/shard_map/pallas_call | solution.py:40
  188.2 2.6 shard_map.54
  201.4 3.0 %collective-permute-done.45.s2 = f32[8,128]{1,0:T(8,128)S(1)} collective-permute-done((f32[8,128]{1,0:T(8,128)S(1)}, f32[8,128]{1,0:T(8,128)S(1)}, u32[]{:S(2)}, u32[]{:S(2)}) %collective-permute-start.45) | collective-permute-done | bytes 4128 | tf_op jit(solution)/shard_map/ppermute | solution.py:69
  209.0 5.0 %shard_map.55 = (f32[288,1024]{1,0:T(8,128)S(1)}, f32[288,1024]{1,0:T(8,128)S(1)}, f32[8,128]{1,0:T(8,128)S(1)}) custom-call(s32[8]{0:T(128)S(1)} %stack.105.ids_ref, f32[288,1024]{1,0:T(8,128)S(1)} %get-tuple-element.74.x_ref, f32[288,1024]{1,0:T(8,128)S(1)} %copy-done.8, f32[8,128]{1,0:T(8,128)S(1)} %get-tuple-element.76.s0, ...), custom_call_target="tpu_custom_call" | custom-call | tf_op jit(solution)/shard_map/pallas_call | solution.py:40
  218.3 2.6 shard_map.56
  225.1 5.0 %shard_map.58 = (f32[288,1024]{1,0:T(8,128)S(1)}, f32[288,1024]{1,0:T(8,128)S(1)}, f32[8,128]{1,0:T(8,128)S(1)}) custom-call(s32[8]{0:T(128)S(1)} %stack.105.ids_ref, f32[288,1024]{1,0:T(8,128)S(1)} %get-tuple-element.80.x_ref, f32[288,1024]{1,0:T(8,128)S(1)} %get-tuple-element.81.g_ref, f32[8,128]{1,0:T(8,128)S(1)} %get-tuple-element.82.s0, ...), custom_call_target="tpu_custom_call" | custom-call | tf_op jit(solution)/shard_map/pallas_call | solution.py:40
  234.5 2.6 shard_map.59
  241.3 5.0 %shard_map.60 = (f32[288,1024]{1,0:T(8,128)S(1)}, f32[288,1024]{1,0:T(8,128)S(1)}, f32[8,128]{1,0:T(8,128)S(1)}) custom-call(s32[8]{0:T(128)S(1)} %stack.105.ids_ref, f32[288,1024]{1,0:T(8,128)S(1)} %get-tuple-element.88.x_ref, f32[288,1024]{1,0:T(8,128)S(1)} %get-tuple-element.89.g_ref, f32[8,128]{1,0:T(8,128)S(1)} %get-tuple-element.90.s0, ...), custom_call_target="tpu_custom_call" | custom-call | tf_op jit(solution)/shard_map/pallas_call | solution.py:40
  250.7 2.6 shard_map.61
  257.5 3.3 %shard_map.62 = f32[288,1024]{1,0:T(8,128)S(1)} custom-call(s32[8]{0:T(128)S(1)} %stack.105.ids_ref, f32[288,1024]{1,0:T(8,128)S(1)} %get-tuple-element.94.x_ref, f32[288,1024]{1,0:T(8,128)S(1)} %get-tuple-element.95.g_ref, f32[8,128]{1,0:T(8,128)S(1)} %get-tuple-element.96.s0, f32[8,128]{1,0:T(8,128)S(1)} %collective-permute-done.73.s1, ...), custom_call_target="tpu_custom_call" | custom-call | tf_op jit(solution)/shard_map/pallas_call | solution.py:40
  (196 shorter events, 121.8 us)
Async XLA Ops:
  13.8 10.9 %collective-permute-start = (f32[64,1024]{1,0:T(8,128)S(1)}, f32[64,1024]{1,0:T(8,128)S(1)}, u32[]{:S(2)}, u32[]{:S(2)}) collective-permute-start(f32[64,1024]{1,0:T(8,128)S(1)} %copy-done.10), channel_id=1, source_target_pairs={{0,8},{2,10},{4,12},{6,14},{8,0},{10,2},{12,4},{14,6},{16,24},{18,... | collective-permute-start | bytes 786440 | tf_op jit(solution)/shard_map/ppermute | solution.py:69
  19.1 10.9 %collective-permute-start.7 = (f32[56,1024]{1,0:T(8,128)S(1)}, f32[56,1024]{1,0:T(8,128)S(1)}, u32[]{:S(2)}, u32[]{:S(2)}) collective-permute-start(f32[56,1024]{1,0:T(8,128)S(1)} %get-tuple-element.105), channel_id=1, source_target_pairs={{0,2},{1,3},{2,0},{3,1},{4,6},{5,7},{6,4},{7,5},{8,10},{9,11},{10,... | collective-permute-start | bytes 688136 | tf_op jit(solution)/shard_map/ppermute | solution.py:69
  21.1 11.6 %collective-permute-start.8 = (f32[56,1024]{1,0:T(8,128)S(1)}, f32[56,1024]{1,0:T(8,128)S(1)}, u32[]{:S(2)}, u32[]{:S(2)}) collective-permute-start(f32[56,1024]{1,0:T(8,128)S(1)} %get-tuple-element.104), channel_id=1, source_target_pairs={{0,4},{1,5},{2,6},{3,7},{4,0},{5,1},{6,2},{7,3},{8,12},{9,13},{10,... | collective-permute-start | bytes 688136 | tf_op jit(solution)/shard_map/ppermute | solution.py:69
  24.6 10.5 %collective-permute-start.9 = (f32[56,1024]{1,0:T(8,128)S(1)}, f32[56,1024]{1,0:T(8,128)S(1)}, u32[]{:S(2)}, u32[]{:S(2)}) collective-permute-start(f32[56,1024]{1,0:T(8,128)S(1)} %get-tuple-element.103), channel_id=1, source_target_pairs={{0,6},{1,7},{2,4},{3,5},{4,2},{5,3},{6,0},{7,1},{8,14},{9,15},{10,... | collective-permute-start | bytes 688136 | tf_op jit(solution)/shard_map/ppermute | solution.py:69
  24.7 36.5 %collective-permute-start.2 = (f32[2,64,1024]{2,1,0:T(8,128)S(1)}, f32[2,64,1024]{2,1,0:T(8,128)S(1)}, u32[]{:S(2)}, u32[]{:S(2)}) collective-permute-start(f32[2,64,1024]{2,1,0:T(8,128)S(1)} %maximum_select_fusion.1), channel_id=1, source_target_pairs={{0,32},{2,34},{4,36},{6,38},{8,40},{10,42},{12,44},{14,46},{16,48}... | collective-permute-start | bytes 1572872 | tf_op jit(solution)/shard_map/ppermute | solution.py:69
  27.3 36.0 %collective-permute-start.3 = (f32[2,64,1024]{2,1,0:T(8,128)S(1)}, f32[2,64,1024]{2,1,0:T(8,128)S(1)}, u32[]{:S(2)}, u32[]{:S(2)}) collective-permute-start(f32[2,64,1024]{2,1,0:T(8,128)S(1)} %maximum_select_fusion.1), channel_id=1, source_target_pairs={{0,16},{2,18},{4,20},{6,22},{8,24},{10,26},{12,28},{14,30},{16,0},... | collective-permute-start | bytes 1572872 | tf_op jit(solution)/shard_map/ppermute | solution.py:69
  35.9 10.6 %collective-permute-start.21 = (bf16[16,1024]{1,0:T(8,128)(2,1)S(1)}, bf16[16,1024]{1,0:T(8,128)(2,1)S(1)}, u32[]{:S(2)}, u32[]{:S(2)}) collective-permute-start(bf16[16,1024]{1,0:T(8,128)(2,1)S(1)} %get-tuple-element.62), channel_id=1, source_target_pairs={{0,4},{1,5},{2,6},{3,7},{4,0},{5,1},{6,2},{7,3},{8,12},{9,13},{10,... | collective-permute-start | bytes 98312 | tf_op jit(solution)/shard_map/ppermute | solution.py:69
  37.3 13.5 %collective-permute-start.22 = (bf16[16,1024]{1,0:T(8,128)(2,1)S(1)}, bf16[16,1024]{1,0:T(8,128)(2,1)S(1)}, u32[]{:S(2)}, u32[]{:S(2)}) collective-permute-start(bf16[16,1024]{1,0:T(8,128)(2,1)S(1)} %get-tuple-element.62), channel_id=1, source_target_pairs={{0,6},{1,7},{2,4},{3,5},{4,2},{5,3},{6,0},{7,1},{8,14},{9,15},{10,... | collective-permute-start | bytes 98312 | tf_op jit(solution)/shard_map/ppermute | solution.py:69
  40.6 24.1 %collective-permute-start.4 = (f32[2,64,1024]{2,1,0:T(8,128)S(1)}, f32[2,64,1024]{2,1,0:T(8,128)S(1)}, u32[]{:S(2)}, u32[]{:S(2)}) collective-permute-start(f32[2,64,1024]{2,1,0:T(8,128)S(1)} %maximum_select_fusion.1), channel_id=1, source_target_pairs={{0,48},{2,50},{4,52},{6,54},{8,56},{10,58},{12,60},{14,62},{16,32}... | collective-permute-start | bytes 1572872 | tf_op jit(solution)/shard_map/ppermute | solution.py:69
  46.5 8.4 %collective-permute-start.10 = (f32[2,16,1024]{2,1,0:T(8,128)S(1)}, f32[2,16,1024]{2,1,0:T(8,128)S(1)}, u32[]{:S(2)}, u32[]{:S(2)}) collective-permute-start(f32[2,16,1024]{2,1,0:T(8,128)S(1)} %get-tuple-element.83), channel_id=1, source_target_pairs={{0,8},{2,10},{4,12},{6,14},{8,0},{10,2},{12,4},{14,6},{16,24},{18,... | collective-permute-start | bytes 393224 | tf_op jit(solution)/shard_map/ppermute | solution.py:69
  50.8 6.6 %collective-permute-start.23 = (bf16[4,16,1024]{2,1,0:T(8,128)(2,1)S(1)}, bf16[4,16,1024]{2,1,0:T(8,128)(2,1)S(1)}, u32[]{:S(2)}, u32[]{:S(2)}) collective-permute-start(bf16[4,16,1024]{2,1,0:T(8,128)(2,1)S(1)} %pad_maximum_fusion.4), channel_id=1, source_target_pairs={{0,8},{1,9},{2,10},{3,11},{4,12},{5,13},{6,14},{7,15},{8,0},{9,1},... | collective-permute-start | bytes 393224 | tf_op jit(solution)/shard_map/ppermute | solution.py:69
  57.3 8.8 %collective-permute-start.25 = (bf16[4,16,1024]{2,1,0:T(8,128)(2,1)S(1)}, bf16[4,16,1024]{2,1,0:T(8,128)(2,1)S(1)}, u32[]{:S(2)}, u32[]{:S(2)}) collective-permute-start(bf16[4,16,1024]{2,1,0:T(8,128)(2,1)S(1)} %pad_maximum_fusion.4), channel_id=1, source_target_pairs={{0,72},{1,73},{2,74},{3,75},{4,76},{5,77},{6,78},{7,79},{8,64},{9,... | collective-permute-start | bytes 393224 | tf_op jit(solution)/shard_map/ppermute | solution.py:69
  59.9 11.6 %collective-permute-start.11 = (f32[2,2,16,1024]{3,2,1,0:T(8,128)S(1)}, f32[2,2,16,1024]{3,2,1,0:T(8,128)S(1)}, u32[]{:S(2)}, u32[]{:S(2)}) collective-permute-start(f32[2,2,16,1024]{3,2,1,0:T(8,128)S(1)} %maximum_select_fusion.4), channel_id=1, source_target_pairs={{0,32},{2,34},{4,36},{6,38},{8,40},{10,42},{12,44},{14,46},{16,48}... | collective-permute-start | bytes 786440 | tf_op jit(solution)/shard_map/ppermute | solution.py:69
  61.2 14.9 %collective-permute-start.12 = (f32[2,2,16,1024]{3,2,1,0:T(8,128)S(1)}, f32[2,2,16,1024]{3,2,1,0:T(8,128)S(1)}, u32[]{:S(2)}, u32[]{:S(2)}) collective-permute-start(f32[2,2,16,1024]{3,2,1,0:T(8,128)S(1)} %maximum_select_fusion.4), channel_id=1, source_target_pairs={{0,16},{2,18},{4,20},{6,22},{8,24},{10,26},{12,28},{14,30},{16,0},... | collective-permute-start | bytes 786440 | tf_op jit(solution)/shard_map/ppermute | solution.py:69
  63.3 12.8 %collective-permute-start.13 = (f32[2,2,16,1024]{3,2,1,0:T(8,128)S(1)}, f32[2,2,16,1024]{3,2,1,0:T(8,128)S(1)}, u32[]{:S(2)}, u32[]{:S(2)}) collective-permute-start(f32[2,2,16,1024]{3,2,1,0:T(8,128)S(1)} %maximum_select_fusion.4), channel_id=1, source_target_pairs={{0,48},{2,50},{4,52},{6,54},{8,56},{10,58},{12,60},{14,62},{16,32}... | collective-permute-start | bytes 786440 | tf_op jit(solution)/shard_map/ppermute | solution.py:69
  67.5 20.4 %collective-permute-start.26 = (bf16[16,16,1024]{2,1,0:T(8,128)(2,1)S(1)}, bf16[16,16,1024]{2,1,0:T(8,128)(2,1)S(1)}, u32[]{:S(2)}, u32[]{:S(2)}) collective-permute-start(bf16[16,16,1024]{2,1,0:T(8,128)(2,1)S(1)} %constant_dynamic-update-slice_fusion.y0), channel_id=1, source_target_pairs={{0,16},{1,17},{2,18},{3,19},{4,20},{5,21},{6,22},{7,23},{8,24},{9,... | collective-permute-start | bytes 1572872 | tf_op jit(solution)/shard_map/ppermute | solution.py:69
  71.3 20.6 %collective-permute-start.27 = (bf16[16,16,1024]{2,1,0:T(8,128)(2,1)S(1)}, bf16[16,16,1024]{2,1,0:T(8,128)(2,1)S(1)}, u32[]{:S(2)}, u32[]{:S(2)}) collective-permute-start(bf16[16,16,1024]{2,1,0:T(8,128)(2,1)S(1)} %constant_dynamic-update-slice_fusion.y0), channel_id=1, source_target_pairs={{0,32},{1,33},{2,34},{3,35},{4,36},{5,37},{6,38},{7,39},{8,40},{9,... | collective-permute-start | bytes 1572872 | tf_op jit(solution)/shard_map/ppermute | solution.py:69
  71.4 26.4 %collective-permute-start.28 = (bf16[16,16,1024]{2,1,0:T(8,128)(2,1)S(1)}, bf16[16,16,1024]{2,1,0:T(8,128)(2,1)S(1)}, u32[]{:S(2)}, u32[]{:S(2)}) collective-permute-start(bf16[16,16,1024]{2,1,0:T(8,128)(2,1)S(1)} %constant_dynamic-update-slice_fusion.y0), channel_id=1, source_target_pairs={{0,48},{1,49},{2,50},{3,51},{4,52},{5,53},{6,54},{7,55},{8,56},{9,... | collective-permute-start | bytes 1572872 | tf_op jit(solution)/shard_map/ppermute | solution.py:69
  98.6 60.1 %collective-permute-start.29 = (bf16[1024,1024]{1,0:T(8,128)(2,1)S(1)}, bf16[1024,1024]{1,0:T(8,128)(2,1)S(1)}, u32[]{:S(2)}, u32[]{:S(2)}) collective-permute-start(bf16[1024,1024]{1,0:T(8,128)(2,1)S(1)} %shard_map.49.mine_ref), channel_id=1, source_target_pairs={{0,1},{1,0},{2,3},{3,2},{4,5},{5,4},{6,7},{7,6},{8,9},{9,8},{10,11... | collective-permute-start | bytes 6291464 | tf_op jit(solution)/shard_map/ppermute | solution.py:69
  104.6 8.4 %collective-permute-start.55 = (f32[2,16,1024]{2,1,0:T(8,128)S(1)}, f32[2,16,1024]{2,1,0:T(8,128)S(1)}, u32[]{:S(2)}, u32[]{:S(2)}) collective-permute-start(f32[2,16,1024]{2,1,0:T(8,128)S(1)} %collective-permute-done.54), channel_id=1, source_target_pairs={{0,8},{2,10},{4,12},{6,14},{8,0},{10,2},{12,4},{14,6},{16,24},{18,... | collective-permute-start | bytes 393224 | tf_op jit(solution)/shard_map/ppermute | solution.py:69
  114.3 8.3 %collective-permute-start.57 = (f32[2,2,16,1024]{3,2,1,0:T(8,128)S(1)}, f32[2,2,16,1024]{3,2,1,0:T(8,128)S(1)}, u32[]{:S(2)}, u32[]{:S(2)}) collective-permute-start(f32[2,2,16,1024]{3,2,1,0:T(8,128)S(1)} %maximum_select_fusion.5), channel_id=1, source_target_pairs={{0,16},{2,18},{4,20},{6,22},{8,24},{10,26},{12,28},{14,30},{16,0},... | collective-permute-start | bytes 786440 | tf_op jit(solution)/shard_map/ppermute | solution.py:69
  117.5 13.3 %collective-permute-start.30 = (f32[4,2,16,1024]{3,2,1,0:T(8,128)S(1)}, f32[4,2,16,1024]{3,2,1,0:T(8,128)S(1)}, u32[]{:S(2)}, u32[]{:S(2)}) collective-permute-start(f32[4,2,16,1024]{3,2,1,0:T(8,128)S(1)} %maximum_select_fusion.2.z0), channel_id=1, source_target_pairs={{0,2},{1,3},{2,0},{3,1},{4,6},{5,7},{6,4},{7,5},{8,10},{9,11},{10,... | collective-permute-start | bytes 1572872 | tf_op jit(solution)/shard_map/ppermute | solution.py:69
  118.1 22.8 %collective-permute-start.31 = (f32[4,2,16,1024]{3,2,1,0:T(8,128)S(1)}, f32[4,2,16,1024]{3,2,1,0:T(8,128)S(1)}, u32[]{:S(2)}, u32[]{:S(2)}) collective-permute-start(f32[4,2,16,1024]{3,2,1,0:T(8,128)S(1)} %maximum_select_fusion.2.z0), channel_id=1, source_target_pairs={{0,4},{1,5},{2,6},{3,7},{4,0},{5,1},{6,2},{7,3},{8,12},{9,13},{10,... | collective-permute-start | bytes 1572872 | tf_op jit(solution)/shard_map/ppermute | solution.py:69
  122.5 21.8 %collective-permute-start.32 = (f32[4,2,16,1024]{3,2,1,0:T(8,128)S(1)}, f32[4,2,16,1024]{3,2,1,0:T(8,128)S(1)}, u32[]{:S(2)}, u32[]{:S(2)}) collective-permute-start(f32[4,2,16,1024]{3,2,1,0:T(8,128)S(1)} %maximum_select_fusion.2.z0), channel_id=1, source_target_pairs={{0,6},{1,7},{2,4},{3,5},{4,2},{5,3},{6,0},{7,1},{8,14},{9,15},{10,... | collective-permute-start | bytes 1572872 | tf_op jit(solution)/shard_map/ppermute | solution.py:69
  122.6 23.6 %collective-permute-start.17 = (f32[8,128]{1,0:T(8,128)S(1)}, f32[8,128]{1,0:T(8,128)S(1)}, u32[]{:S(2)}, u32[]{:S(2)}) collective-permute-start(f32[8,128]{1,0:T(8,128)S(1)} %get-tuple-element.61.s0), channel_id=1, source_target_pairs={{0,1},{1,0},{2,3},{3,2},{4,5},{5,4},{6,7},{7,6},{8,9},{9,8},{10,11... | collective-permute-start | bytes 12296 | tf_op jit(solution)/shard_map/ppermute | solution.py:69
  130.8 16.9 %collective-permute-start.18 = (f32[8,128]{1,0:T(8,128)S(1)}, f32[8,128]{1,0:T(8,128)S(1)}, u32[]{:S(2)}, u32[]{:S(2)}) collective-permute-start(f32[8,128]{1,0:T(8,128)S(1)} %get-tuple-element.61.s0), channel_id=1, source_target_pairs={{0,64},{1,65},{2,66},{3,67},{4,68},{5,69},{6,70},{7,71},{8,72},{9,... | collective-permute-start | bytes 12296 | tf_op jit(solution)/shard_map/ppermute | solution.py:69
  140.9 51.0 %collective-permute-start.59 = (f32[4,2,16,1024]{3,2,1,0:T(8,128)S(1)}, f32[4,2,16,1024]{3,2,1,0:T(8,128)S(1)}, u32[]{:S(2)}, u32[]{:S(2)}) collective-permute-start(f32[4,2,16,1024]{3,2,1,0:T(8,128)S(1)} %maximum_select_fusion.3.z0), channel_id=1, source_target_pairs={{0,2},{1,3},{2,0},{3,1},{4,6},{5,7},{6,4},{7,5},{8,10},{9,11},{10,... | collective-permute-start | bytes 1572872 | tf_op jit(solution)/shard_map/ppermute | solution.py:69
  144.3 47.6 %collective-permute-start.60 = (f32[4,2,16,1024]{3,2,1,0:T(8,128)S(1)}, f32[4,2,16,1024]{3,2,1,0:T(8,128)S(1)}, u32[]{:S(2)}, u32[]{:S(2)}) collective-permute-start(f32[4,2,16,1024]{3,2,1,0:T(8,128)S(1)} %maximum_select_fusion.3.z0), channel_id=1, source_target_pairs={{0,4},{1,5},{2,6},{3,7},{4,0},{5,1},{6,2},{7,3},{8,12},{9,13},{10,... | collective-permute-start | bytes 1572872 | tf_op jit(solution)/shard_map/ppermute | solution.py:69
  146.2 45.7 %collective-permute-start.61 = (f32[4,2,16,1024]{3,2,1,0:T(8,128)S(1)}, f32[4,2,16,1024]{3,2,1,0:T(8,128)S(1)}, u32[]{:S(2)}, u32[]{:S(2)}) collective-permute-start(f32[4,2,16,1024]{3,2,1,0:T(8,128)S(1)} %maximum_select_fusion.3.z0), channel_id=1, source_target_pairs={{0,6},{1,7},{2,4},{3,5},{4,2},{5,3},{6,0},{7,1},{8,14},{9,15},{10,... | collective-permute-start | bytes 1572872 | tf_op jit(solution)/shard_map/ppermute | solution.py:69
  194.7 27.4 %collective-permute-start.62 = (f32[2,16,1024]{2,1,0:T(8,128)}, f32[2,16,1024]{2,1,0:T(8,128)S(1)}, u32[]{:S(2)}, u32[]{:S(2)}) collective-permute-start(f32[2,16,1024]{2,1,0:T(8,128)} %get-tuple-element.97), channel_id=1, source_target_pairs={{0,1},{1,64},{2,3},{3,66},{4,5},{5,68},{6,7},{7,70},{8,9},{9,72},{... | collective-permute-start | bytes 393224 | tf_op jit(solution)/shard_map/ppermute | solution.py:69
  196.7 26.2 %collective-permute-start.63 = (f32[2,16,1024]{2,1,0:T(8,128)}, f32[2,16,1024]{2,1,0:T(8,128)}, u32[]{:S(2)}, u32[]{:S(2)}) collective-permute-start(f32[2,16,1024]{2,1,0:T(8,128)} %get-tuple-element.98), channel_id=1, source_target_pairs={{1,0},{3,2},{5,4},{7,6},{9,8},{11,10},{13,12},{15,14},{17,16},{19,... | collective-permute-start | bytes 393224 | tf_op jit(solution)/shard_map/ppermute | solution.py:69
  215.9 46.9 %collective-permute-start.47 = (f32[64,1024]{1,0:T(8,128)S(1)}, f32[64,1024]{1,0:T(8,128)S(1)}, u32[]{:S(2)}, u32[]{:S(2)}) collective-permute-start(f32[64,1024]{1,0:T(8,128)S(1)} %constant_dynamic-slice_fusion.1), channel_id=1, source_target_pairs={{0,1},{2,3},{4,5},{6,7},{8,9},{10,11},{12,13},{14,15},{16,17},{18,... | collective-permute-start | bytes 786440 | tf_op jit(solution)/shard_map/ppermute | solution.py:69
  (56 other events, 224.0 us)

commit v6 on v5

--- a/solution.py
+++ b/solution.py
@@ -12,7 +12,8 @@
 SWEEPS = 3
 TV_STEPS = 2
 HALO = 16
-CHUNK = 512
+CHUNK = 1280
+ROWS = 32
 QUARTERS = 4
 AXES = ("tm", "gz", "view")
 
@@ -87,66 +88,67 @@
 
 def gram_kernel(order_ref, ids_ref, a_ref, s0_ref, s1_ref, own_ref, send_ref, acc, level_ref):
     n = pl.program_id(0)
-    d = pl.program_id(1)
-    rows = s0_ref.shape[0]
-    tile = a_ref[...]
-    ray = jnp.sum(tile.astype(F32), axis=0, keepdims=True)
-    inverse = 1.0 / ray
-    lhs = []
-    for t, ref in enumerate((s0_ref, s1_ref)):
-        scaled = ref[...].astype(F32) * inverse
-
-        @pl.when(d == 0)
-        def _():
-            mean = jnp.sum(scaled, axis=1, keepdims=True) / CHUNK
-            level_ref[t] = jnp.broadcast_to(mean, level_ref.shape[1:])
-
-        lhs.append((scaled - level_ref[t, :, 0:1]).astype(BF16))
-    mine = a_ref[pl.ds(pl.multiple_of(ids_ref[1] * rows, rows), rows), :]
-    lhs.append((mine.astype(F32) * inverse).astype(BF16))
-    lhs.append(jnp.ones((16, CHUNK), BF16))
-    stack = jnp.concatenate(lhs, axis=0)
-    product = lax.dot_general(stack, tile, (((1,), (1,)), ((), ())), preferred_element_type=F32)
-
-    @pl.when(d == 0)
-    def _():
-        acc[...] = product
-
-    @pl.when(d > 0)
-    def _():
-        acc[...] += product
-
-    @pl.when(d == pl.num_programs(1) - 1)
-    def _():
-        part = rows // QUARTERS
-        at = pl.ds(pl.multiple_of(n * part, part), part)
-        for t in range(FRAMES):
-            for ref, who in ((own_ref, 1 - t), (send_ref, t)):
-
-                @pl.when(ids_ref[4] == who)
-                def _():
-                    for quarter in range(QUARTERS):
-                        lo = quarter * part
-                        ref[jnp.bitwise_xor(ids_ref[2], quarter), at, :] = (
-                            acc[t * rows + lo : t * rows + lo + part]
-                            + level_ref[t, lo : lo + part, 0:1] * acc[3 * rows : 3 * rows + 1]
-                        )
-
-        for ref, mine_too in ((own_ref, True), (send_ref, False)):
-
-            @pl.when((ids_ref[3] == n) == mine_too)
+    rows, det = s0_ref.shape
+    my_rows = pl.ds(pl.multiple_of(ids_ref[1] * rows, rows), rows)
+
+    def chunk(d, first):
+        at = pl.ds(d * CHUNK, CHUNK) if first else pl.ds(pl.multiple_of(d * CHUNK, CHUNK), CHUNK)
+        tile = a_ref[:, at]
+        ray = jnp.sum(tile.astype(F32), axis=0, keepdims=True)
+        inverse = 1.0 / ray
+        lhs = []
+        for t, ref in enumerate((s0_ref, s1_ref)):
+            scaled = ref[:, at].astype(F32) * inverse
+            if first:
+                mean = jnp.sum(scaled, axis=1, keepdims=True) / CHUNK
+                level_ref[t] = jnp.broadcast_to(mean, level_ref.shape[1:])
+            lhs.append((scaled - level_ref[t, :, 0:1]).astype(BF16))
+        lhs.append((a_ref[my_rows, at].astype(F32) * inverse).astype(BF16))
+        lhs.append(jnp.ones((16, CHUNK), BF16))
+        stack = jnp.concatenate(lhs, axis=0)
+        product = lax.dot_general(stack, tile, (((1,), (1,)), ((), ())), preferred_element_type=F32)
+        if first:
+            acc[...] = product
+        else:
+            acc[...] += product
+
+    chunk(0, True)
+
+    def further(d, carry):
+        chunk(d, False)
+        return carry
+
+    lax.fori_loop(1, det // CHUNK, further, 0)
+
+    part = rows // QUARTERS
+    at = pl.ds(pl.multiple_of(n * part, part), part)
+    for t in range(FRAMES):
+        for ref, who in ((own_ref, 1 - t), (send_ref, t)):
+
+            @pl.when(ids_ref[4] == who)
             def _():
                 for quarter in range(QUARTERS):
-                    lo = 2 * rows + quarter * part
-                    ref[jnp.bitwise_xor(ids_ref[2], quarter), 2 * part : 3 * part, :] = acc[lo : lo + part]
-
-            for half in range(2):
-
-                @pl.when(n == half)
-                def _():
-                    cover = acc[3 * rows : 3 * rows + 8]
-                    for k in range(QUARTERS):
-                        ref[k, 3 * part + half : 3 * part + 8, :] = cover[half:8]
+                    lo = quarter * part
+                    ref[jnp.bitwise_xor(ids_ref[2], quarter), at, :] = (
+                        acc[t * rows + lo : t * rows + lo + part]
+                        + level_ref[t, lo : lo + part, 0:1] * acc[3 * rows : 3 * rows + 1]
+                    )
+
+    for ref, mine_too in ((own_ref, True), (send_ref, False)):
+
+        @pl.when((ids_ref[3] == n) == mine_too)
+        def _():
+            for quarter in range(QUARTERS):
+                lo = 2 * rows + quarter * part
+                ref[jnp.bitwise_xor(ids_ref[2], quarter), 2 * part : 3 * part, :] = acc[lo : lo + part]
+
+        for half in range(2):
+
+            @pl.when(n == half)
+            def _():
+                cover = acc[3 * rows : 3 * rows + 8]
+                for k in range(QUARTERS):
+                    ref[k, 3 * part + half : 3 * part + 8, :] = cover[half:8]
 
 
 def gram_products(order, ids, projector, measured):
@@ -154,7 +156,7 @@
     rows = measured.shape[2]
     part = rows // QUARTERS
     shape = (QUARTERS, 3 * part + 8, pixels)
-    out = pl.BlockSpec(shape, lambda n, d, o, s: (0, 0, 0))
+    out = pl.BlockSpec(shape, lambda n, o, s: (0, 0, 0))
     projector = pltpu.with_memory_space_constraint(projector, pltpu.HBM)
     measured = pltpu.with_memory_space_constraint(measured, pltpu.HBM)
     return pl.pallas_call(
@@ -162,11 +164,11 @@
         out_shape=(jax.ShapeDtypeStruct(shape, F32),) * 2,
         grid_spec=pltpu.PrefetchScalarGridSpec(
             num_scalar_prefetch=2,
-            grid=(2, det // CHUNK),
+            grid=(2,),
             in_specs=[
-                pl.BlockSpec((None, pixels, CHUNK), lambda n, d, o, s: (o[n], 0, d)),
-                pl.BlockSpec((None, None, rows, CHUNK), lambda n, d, o, s: (0, o[n], 0, d)),
-                pl.BlockSpec((None, None, rows, CHUNK), lambda n, d, o, s: (1, o[n], 0, d)),
+                pl.BlockSpec((None, pixels, det), lambda n, o, s: (o[n], 0, 0)),
+                pl.BlockSpec((None, None, rows, det), lambda n, o, s: (0, o[n], 0, 0)),
+                pl.BlockSpec((None, None, rows, det), lambda n, o, s: (1, o[n], 0, 0)),
             ],
             out_specs=(out, out),
             scratch_shapes=[pltpu.VMEM((3 * rows + 16, pixels), F32), pltpu.VMEM((FRAMES, rows, RY), F32)],
@@ -174,6 +176,11 @@
         compiler_params=params(24),
         name="gram_products",
     )(order, ids, projector, measured, measured)
+
+
+def chip_sum_kernel(ids_ref, own_ref, got_ref, *outs):
+    for k, out in enumerate(outs):
+        out[...] = own_ref[k] + got_ref[k]
 
 
 def reduce_kernel(ids_ref, a0, a1, a2, a3, b_ref, gram_ref, aux_ref):
@@ -207,7 +214,7 @@
                 out_ref[pl.ds(pl.multiple_of(row, part), part), :] = ref[dx * QUARTERS + k]
 
 
-def place_rows_kernel(ids_ref, z0, z1, z2, z3, out_ref):
+def place_rows_kernel(ids_ref, z0, z1, z2, z3, out_ref, head_ref, tail_ref):
     z = ids_ref[2]
     part = z0.shape[2]
     for k, ref in enumerate((z0, z1, z2, z3)):
@@ -216,12 +223,13 @@
             for n in range(2):
                 row = slab * (QUARTERS * part) + start
                 out_ref[n, pl.ds(pl.multiple_of(row, part), part), :] = ref[slab, n]
+    head_ref[...] = out_ref[:, :HALO]
+    tail_ref[...] = out_ref[:, out_ref.shape[1] - HALO :]
 
 
 def tv_into(x_ref, g_ref, ss_ref, flux_ref, first, depth):
     height, pixels = x_ref.shape
     blocks = pixels // RY
-    lane = lax.broadcasted_iota(jnp.int32, (height, RY), 1)
 
     @pl.when(first < 0)
     def _():
@@ -231,29 +239,35 @@
     def _():
         x_ref[height - HALO : height - HALO + 1, :] = x_ref[height - HALO - 1 : height - HALO, :]
 
-    column = (lane < RY - 1).astype(F32)
+    column = (lax.broadcasted_iota(jnp.int32, (ROWS, RY), 1) < RY - 1).astype(F32)
     flux_ref[...] = jnp.zeros_like(flux_ref)
 
     def block(i, folded):
         here_at = pl.ds(pl.multiple_of(i * RY, RY), RY)
         next_at = pl.ds(pl.multiple_of(jnp.minimum(i + 1, blocks - 1) * RY, RY), RY)
-        here = x_ref[:, here_at]
-        dz = pltpu.roll(here, height - 1, 0) - here
-        dc = (pltpu.roll(here, RY - 1, 1) - here) * column
-        di = x_ref[:, next_at] - here
-        square = dz * dz + dc * dc + di * di + SMOOTHING
-        r = lax.rsqrt(square)
-        r = r * (1.5 - (0.5 * square) * (r * r))
-        fz = dz * r
-        fc = dc * r
-        fi = di * r
-        g = (pltpu.roll(fz, 1, 0) - fz) + (flux_ref[...] - fi) + (pltpu.roll(fc, 1, 1) - fc)
-        flux_ref[...] = fi
-        g_ref[:, here_at] = g
-        inner = g[HALO : height - HALO]
-        piece = inner * inner
-        for k in range(piece.shape[0] // 8):
-            folded = folded + piece[8 * k : 8 * k + 8]
+        above = jnp.zeros((8, RY), F32)
+        for lo in range(0, height, ROWS):
+            hi = lo + ROWS
+            here = x_ref[lo:hi, here_at]
+            tail = x_ref[hi : hi + 8, here_at] if hi < height else here[ROWS - 8 :]
+            below = pltpu.roll(jnp.concatenate([here, tail]), ROWS + 7, 0)[:ROWS]
+            dz = below - here
+            dc = (pltpu.roll(here, RY - 1, 1) - here) * column
+            di = x_ref[lo:hi, next_at] - here
+            square = dz * dz + dc * dc + di * di + SMOOTHING
+            r = lax.rsqrt(square)
+            r = r * (1.5 - (0.5 * square) * (r * r))
+            fz = dz * r
+            fc = dc * r
+            fi = di * r
+            over = pltpu.roll(jnp.concatenate([above, fz]), 1, 0)[8:]
+            above = fz[ROWS - 8 :]
+            g = (over - fz) + (flux_ref[lo:hi] - fi) + (pltpu.roll(fc, 1, 1) - fc)
+            flux_ref[lo:hi] = fi
+            g_ref[lo:hi, here_at] = g
+            for k in range(0, ROWS, 8):
+                if HALO <= lo + k < height - HALO:
+                    folded = folded + g[k : k + 8] * g[k : k + 8]
         return folded
 
     ss_ref[...] = lax.fori_loop(0, blocks, block, jnp.zeros((8, RY), F32))
@@ -277,10 +291,12 @@
 
 
 def subset_kernel(
-    ids_ref, x_ref, g_ref, s0, s1, s2, s3, mine_ref, other_ref, b_ref, aux_ref, *rest, depth, step, cells, final
+    ids_ref, x_ref, g_ref, s0, s1, s2, s3, mine_ref, other_ref, low_ref, b_ref, high_ref, aux_ref, *rest, depth, step, cells, last, final
 ):
     flux, product = rest[-2:]
     x_out = rest[0]
+    height = x_ref.shape[0]
+    parts = ((low_ref, 0, HALO), (b_ref, HALO, height - HALO), (high_ref, height - HALO, height))
     x_out[...] = descend(x_ref, g_ref, (s0, s1, s2, s3), step, cells)
     core = ids_ref[3]
 
@@ -296,13 +312,20 @@
             product[...] = jnp.dot(rounded, other_ref[...], preferred_element_type=F32)
 
         along = jnp.sum(rounded.astype(F32) * aux_ref[pl.ds(n, 1), :], axis=1, keepdims=True)
-        change = b_ref[n] - product[...] * aux_ref[pl.ds(2 + n, 1), :] - along
-        x_out[...] = jnp.maximum(x_out[...] + change, 0.0)
+        scale = aux_ref[pl.ds(2 + n, 1), :]
+        for ref, lo, hi in parts:
+            change = ref[n] - product[lo:hi] * scale - along[lo:hi]
+            x_out[lo:hi] = jnp.maximum(x_out[lo:hi] + change, 0.0)
         return carry
 
     lax.fori_loop(0, 2, subset, 0)
+    if last:
+        slab_out = rest[1]
+        rows = slab_out.shape[0]
+        start = HALO + jnp.bitwise_and(ids_ref[1], 3) * rows
+        slab_out[...] = x_out[pl.ds(pl.multiple_of(start, HALO), rows), :]
     if not final:
-        g_out, ss_out = rest[1:3]
+        g_out, ss_out = rest[1 + last : 3 + last]
         tv_into(x_out, g_out, ss_out, flux, ids_ref[0], depth)
 
 
@@ -341,12 +364,17 @@
         high = move(lax.slice_in_dim(array, 0, HALO, axis=dim), strip_step(-1))
         return jnp.concatenate([low, array, high], axis=dim)
 
-    warm_pair = pair_of(warm_volume)
     own, send = gram_products(view_order, ids, projector, sinogram)
-    both = own + move(send, flip(dc=1))
-    terms = [both[0]] + [move(both[k], flip(dz=k)) for k in range(1, QUARTERS)]
+    passed = move(send, flip(dc=1))
+    warm_pair = pair_of(after(warm_volume, send))
+    block = (own.shape[1:], F32)
+    terms = call(chip_sum_kernel, [block] * QUARTERS, ids, own, passed)
+    terms = [terms[0]] + [move(terms[k], flip(dz=k)) for k in range(1, QUARTERS)]
     b_unit, piece, aux = call(
-        reduce_kernel, [((2, part, pixels), F32), ((part, pixels), BF16), ((8, pixels), F32)], ids, *terms
+        reduce_kernel,
+        [((2, part, pixels), F32), ((part, pixels), BF16), ((8, pixels), F32)],
+        ids,
+        *terms,
     )
 
     line = jnp.stack([piece] + [move(piece, flip(dz=k)) for k in range(1, 4)])
@@ -358,8 +386,11 @@
         return [strip] + [move(strip, flip(dz=k)) for k in range(1, 4)]
 
     def b_rows(quarters):
-        (rows,) = call(place_rows_kernel, [((2, inner, pixels), F32)], ids, *quarters)
-        return widen(rows, 1)
+        edge = ((2, HALO, pixels), F32)
+        rows, head, tail = call(
+            place_rows_kernel, [((2, inner, pixels), F32), edge, edge], ids, *quarters
+        )
+        return move(tail, strip_step(1)), rows, move(head, strip_step(-1))
 
     strip = strip_of(pair_of(b_unit))
     quarters = along_z(strip)
@@ -378,9 +409,11 @@
             move(sums, flip(dtm=1, dc=1)),
         ]
 
-    x = widen(strip_of(after(warm_pair, both)).reshape(inner, pixels), 0)
+    x = widen(strip_of(after(warm_pair, terms[0])).reshape(inner, pixels), 0)
     x = after(x, strip)
-    x, g, sums = call(functools.partial(first_kernel, depth=depth), [big, big, small], ids, x, scratch=[flux])
+    x, g, sums = call(
+        functools.partial(first_kernel, depth=depth), [big, big, small], ids, x, scratch=[flux]
+    )
     b_wide = [None, None]
     finished = []
     for frame in range(FRAMES):
@@ -396,31 +429,41 @@
                 scratch=[flux],
             )
             if frame == 0 and sweep == 0:
-                (mine,) = call(place_gram_kernel, [((slices * 16, pixels), BF16)], ids, after(plane, sums), *spread)
+                (mine,) = call(
+                    place_gram_kernel,
+                    [((slices * 16, pixels), BF16)],
+                    ids,
+                    after(plane, sums),
+                    *spread,
+                )
                 other = move(mine, flip(dc=1))
                 b_wide[0] = b_rows(quarters)
             if frame == 0 and sweep == 2:
                 b_wide[1] = b_rows([after(later[0], x)] + later[1:])
-            final = sweep == SWEEPS - 1 and frame == FRAMES - 1
+            last = sweep == SWEEPS - 1
+            final = last and frame == FRAMES - 1
+            outs = [big] + [((slices, pixels), F32)] * last
+            if not final:
+                outs += [big, small]
             outs = call(
-                functools.partial(subset_kernel, depth=depth, step=step + 1, cells=cells, final=final),
-                [big] if final else [big, big, small],
+                functools.partial(
+                    subset_kernel, depth=depth, step=step + 1, cells=cells, last=last, final=final
+                ),
+                outs,
                 ids,
                 x,
                 g,
                 *everyone(sums),
                 mine,
                 other,
-                b_wide[frame],
+                *b_wide[frame],
                 aux,
                 scratch=[flux, pltpu.VMEM((height, pixels), F32)],
             )
-            if final:
-                x = outs[0]
-            else:
-                x, g, sums = outs
-        start = HALO + (gz % 4) * slices
-        local = lax.dynamic_slice_in_dim(x, start, slices, axis=0)
+            x = outs[0]
+            if not final:
+                g, sums = outs[-2:]
+        local = outs[1]
         passed = move(local, flip(dc=1), keeps)
         finished.append(jnp.where(keeper, local, passed))
     return jnp.stack(finished, axis=0)

time: 267 us -> 256 us (0.959)
  starting transfers between devices: 108 us -> 122 us
  waiting for transfers between devices: 82.1 us -> 69.2 us
  local copies, waits for them, and re-layouts: 8.63 us -> 0.8 us
    ppermute x77, starting transfers between devices: 108 us -> 122 us  [move(): return lax.ppermute(array, AXES, pairs)]
    ppermute x77, waiting for transfers between devices: 82.1 us -> 69.2 us  [move(): return lax.ppermute(array, AXES, pairs)]
    unnamed x28 -> x10, local copies, waits for them, and re-layouts: 7.66 us -> 0.69 us
    pallas_call x1, Pallas kernels: 12.9 us -> 8.68 us  [gram_products(): pl.pallas_call(gram_kernel, out_shape=(jax.ShapeDtypeStruct(shape, F32),)...]
    pallas_call x17 -> x18, Pallas kernels: 49.4 us -> 51.3 us  [call(): pl.pallas_call(kernel, out_shape=tuple((pltpu.VMEM(shape, dtype) for shap...]
  transfers between devices with their start and end apart: 77 -> 77, of which waited for: 40 -> 42; matrix products, arithmetic and copies ran while one was open for 1% -> 0% of each run, Pallas kernels for 18% -> 20%
where the time goes in v6:
time: 256 us; the launch traced here: 254 us
  starting transfers between devices  122 us (48%)
  waiting for transfers between devices  69.2 us (27%)
  Pallas kernels  59.9 us (23%)
    ppermute x77, starting transfers between devices, move(): return lax.ppermute(array, AXES, pairs)  122 us
    ppermute x77, waiting for transfers between devices, move(): return lax.ppermute(array, AXES, pairs)  69.2 us
    pallas_call x18, Pallas kernels, call(): pl.pallas_call(kernel, out_shape=tuple((pltpu.VMEM(shape, dtype) for shap...  51.3 us
    pallas_call x1, Pallas kernels, gram_products(): pl.pallas_call(gram_kernel, out_shape=(jax.ShapeDtypeStruct(shape, F32),)...  8.68 us
  transfers between devices with their start and end apart: 77, of which 42 were waited for; matrix products, arithmetic and copies ran while one was open for 0% of the time, Pallas kernels for 20%

profile of v6, /device:TPU:0, one launch (start us, length us, event | category | flops | bytes accessed | tf_op | source)
XLA Modules:
  0.0 254.2 jit_solution(18026581899080458743)
XLA Ops:
  0.7 8.7 %gram_products.1 = (f32[4,56,1024]{2,1,0:T(8,128)S(1)}, f32[4,56,1024]{2,1,0:T(8,128)S(1)}) custom-call(s32[2]{0:T(128)S(1)} %copy-done, s32[8]{0:T(128)S(1)} %stack.105.ids_ref, bf16[2,1024,2560]{2,1,0:T(8,128)(2,1)} %a_ref.1, bf16[2,2,64,2560]{3,2,1,0:T(8,128)(2,1)} %s1_ref.1, bf16[2,2,64,2560]{3,2,1,0:T(8,128)(2,1)} %s1_ref.1), custom_call_target="tpu_custom_call" | custom-call | tf_op jit(solution)/shard_map/gram_products/pallas_call | solution.py:162
  9.5 5.1 %collective-permute-start = (f32[64,1024]{1,0:T(8,128)S(1)}, f32[64,1024]{1,0:T(8,128)S(1)}, u32[]{:S(2)}, u32[]{:S(2)}) collective-permute-start(f32[64,1024]{1,0:T(8,128)S(1)} %copy-done.1), channel_id=1, source_target_pairs={{0,8},{2,10},{4,12},{6,14},{8,0},{10,2},{12,4},{14,6},{16,24},{18,... | collective-permute-start | bytes 786440 | tf_op jit(solution)/shard_map/ppermute | solution.py:70
  17.3 3.6 %collective-permute-start.8 = (f32[56,1024]{1,0:T(8,128)S(1)}, f32[56,1024]{1,0:T(8,128)S(1)}, u32[]{:S(2)}, u32[]{:S(2)}) collective-permute-start(f32[56,1024]{1,0:T(8,128)S(1)} %get-tuple-element.70), channel_id=1, source_target_pairs={{0,4},{1,5},{2,6},{3,7},{4,0},{5,1},{6,2},{7,3},{8,12},{9,13},{10,... | collective-permute-start | bytes 688136 | tf_op jit(solution)/shard_map/ppermute | solution.py:70
  20.9 2.7 %collective-permute-start.2 = (f32[2,64,1024]{2,1,0:T(8,128)S(1)}, f32[2,64,1024]{2,1,0:T(8,128)S(1)}, u32[]{:S(2)}, u32[]{:S(2)}) collective-permute-start(f32[2,64,1024]{2,1,0:T(8,128)S(1)} %maximum_select_fusion.1), channel_id=1, source_target_pairs={{0,32},{2,34},{4,36},{6,38},{8,40},{10,42},{12,44},{14,46},{16,48}... | collective-permute-start | bytes 1572872 | tf_op jit(solution)/shard_map/ppermute | solution.py:70
  26.2 2.7 %collective-permute-done.8.a2 = f32[56,1024]{1,0:T(8,128)S(1)} collective-permute-done((f32[56,1024]{1,0:T(8,128)S(1)}, f32[56,1024]{1,0:T(8,128)S(1)}, u32[]{:S(2)}, u32[]{:S(2)}) %collective-permute-start.8) | collective-permute-done | bytes 229408 | tf_op jit(solution)/shard_map/ppermute | solution.py:70
  33.5 3.3 %collective-permute-start.22 = (bf16[16,1024]{1,0:T(8,128)(2,1)S(1)}, bf16[16,1024]{1,0:T(8,128)(2,1)S(1)}, u32[]{:S(2)}, u32[]{:S(2)}) collective-permute-start(bf16[16,1024]{1,0:T(8,128)(2,1)S(1)} %get-tuple-element.80), channel_id=1, source_target_pairs={{0,6},{1,7},{2,4},{3,5},{4,2},{5,3},{6,0},{7,1},{8,14},{9,15},{10,... | collective-permute-start | bytes 98312 | tf_op jit(solution)/shard_map/ppermute | solution.py:70
  36.8 6.0 %collective-permute-start.4 = (f32[2,64,1024]{2,1,0:T(8,128)S(1)}, f32[2,64,1024]{2,1,0:T(8,128)S(1)}, u32[]{:S(2)}, u32[]{:S(2)}) collective-permute-start(f32[2,64,1024]{2,1,0:T(8,128)S(1)} %maximum_select_fusion.1), channel_id=1, source_target_pairs={{0,48},{2,50},{4,52},{6,54},{8,56},{10,58},{12,60},{14,62},{16,32}... | collective-permute-start | bytes 1572872 | tf_op jit(solution)/shard_map/ppermute | solution.py:70
  42.8 4.2 %collective-permute-start.10 = (f32[2,16,1024]{2,1,0:T(8,128)S(1)}, f32[2,16,1024]{2,1,0:T(8,128)S(1)}, u32[]{:S(2)}, u32[]{:S(2)}) collective-permute-start(f32[2,16,1024]{2,1,0:T(8,128)S(1)} %get-tuple-element.105), channel_id=1, source_target_pairs={{0,8},{2,10},{4,12},{6,14},{8,0},{10,2},{12,4},{14,6},{16,24},{18,... | collective-permute-start | bytes 393224 | tf_op jit(solution)/shard_map/ppermute | solution.py:70
  48.3 2.8 %collective-permute-done.10 = f32[2,16,1024]{2,1,0:T(8,128)S(1)} collective-permute-done((f32[2,16,1024]{2,1,0:T(8,128)S(1)}, f32[2,16,1024]{2,1,0:T(8,128)S(1)}, u32[]{:S(2)}, u32[]{:S(2)}) %collective-permute-start.10) | collective-permute-done | bytes 131104 | tf_op jit(solution)/shard_map/ppermute | solution.py:70
  67.7 4.6 %collective-permute-start.28 = (bf16[16,16,1024]{2,1,0:T(8,128)(2,1)S(1)}, bf16[16,16,1024]{2,1,0:T(8,128)(2,1)S(1)}, u32[]{:S(2)}, u32[]{:S(2)}) collective-permute-start(bf16[16,16,1024]{2,1,0:T(8,128)(2,1)S(1)} %constant_dynamic-update-slice_fusion.y0), channel_id=1, source_target_pairs={{0,48},{1,49},{2,50},{3,51},{4,52},{5,53},{6,54},{7,55},{8,56},{9,... | collective-permute-start | bytes 1572872 | tf_op jit(solution)/shard_map/ppermute | solution.py:70
  74.9 2.7 %collective-permute-start.14 = (f32[8,128]{1,0:T(8,128)S(1)}, f32[8,128]{1,0:T(8,128)S(1)}, u32[]{:S(2)}, u32[]{:S(2)}) collective-permute-start(f32[8,128]{1,0:T(8,128)S(1)} %get-tuple-element.76.s0), channel_id=1, source_target_pairs={{0,1},{1,0},{2,3},{3,2},{4,5},{5,4},{6,7},{7,6},{8,9},{9,8},{10,11... | collective-permute-start | bytes 12296 | tf_op jit(solution)/shard_map/ppermute | solution.py:70
  81.5 2.6 %shard_map.49 = (f32[288,1024]{1,0:T(8,128)S(1)}, f32[288,1024]{1,0:T(8,128)S(1)}, f32[8,128]{1,0:T(8,128)S(1)}) custom-call(s32[8]{0:T(128)S(1)} %stack.105.ids_ref, f32[288,1024]{1,0:T(8,128)S(1)} %get-tuple-element.74.x_ref, f32[288,1024]{1,0:T(8,128)S(1)} %get-tuple-element.75.g_ref, f32[8,128]{1,0:T(8,128)S(1)} %get-tuple-element.76.s0, ...), custom_call_target="tpu_custom_call" | custom-call | tf_op jit(solution)/shard_map/pallas_call | solution.py:41
  84.2 4.1 %collective-permute-done.27.y2 = bf16[16,16,1024]{2,1,0:T(8,128)(2,1)S(1)} collective-permute-done((bf16[16,16,1024]{2,1,0:T(8,128)(2,1)S(1)}, bf16[16,16,1024]{2,1,0:T(8,128)(2,1)S(1)}, u32[]{:S(2)}, u32[]{:S(2)}) %collective-permute-start.27) | collective-permute-done | bytes 524320 | tf_op jit(solution)/shard_map/ppermute | solution.py:70
  88.2 5.9 %collective-permute-done.28.y3 = bf16[16,16,1024]{2,1,0:T(8,128)(2,1)S(1)} collective-permute-done((bf16[16,16,1024]{2,1,0:T(8,128)(2,1)S(1)}, bf16[16,16,1024]{2,1,0:T(8,128)(2,1)S(1)}, u32[]{:S(2)}, u32[]{:S(2)}) %collective-permute-start.28) | collective-permute-done | bytes 524320 | tf_op jit(solution)/shard_map/ppermute | solution.py:70
  100.9 4.4 %collective-permute-start.55 = (f32[2,16,1024]{2,1,0:T(8,128)S(1)}, f32[2,16,1024]{2,1,0:T(8,128)S(1)}, u32[]{:S(2)}, u32[]{:S(2)}) collective-permute-start(f32[2,16,1024]{2,1,0:T(8,128)S(1)} %collective-permute-done.54), channel_id=1, source_target_pairs={{0,8},{2,10},{4,12},{6,14},{8,0},{10,2},{12,4},{14,6},{16,24},{18,... | collective-permute-start | bytes 393224 | tf_op jit(solution)/shard_map/ppermute | solution.py:70
  105.3 3.9 %collective-permute-done.55 = f32[2,16,1024]{2,1,0:T(8,128)S(1)} collective-permute-done((f32[2,16,1024]{2,1,0:T(8,128)S(1)}, f32[2,16,1024]{2,1,0:T(8,128)S(1)}, u32[]{:S(2)}, u32[]{:S(2)}) %collective-permute-start.55) | collective-permute-done | bytes 131104 | tf_op jit(solution)/shard_map/ppermute | solution.py:70
  113.9 3.6 %collective-permute-done.57 = f32[2,2,16,1024]{3,2,1,0:T(8,128)S(1)} collective-permute-done((f32[2,2,16,1024]{3,2,1,0:T(8,128)S(1)}, f32[2,2,16,1024]{3,2,1,0:T(8,128)S(1)}, u32[]{:S(2)}, u32[]{:S(2)}) %collective-permute-start.57) | collective-permute-done | bytes 262176 | tf_op jit(solution)/shard_map/ppermute | solution.py:70
  122.3 3.6 %collective-permute-done.18.s2 = f32[8,128]{1,0:T(8,128)S(1)} collective-permute-done((f32[8,128]{1,0:T(8,128)S(1)}, f32[8,128]{1,0:T(8,128)S(1)}, u32[]{:S(2)}, u32[]{:S(2)}) %collective-permute-start.18) | collective-permute-done | bytes 4128 | tf_op jit(solution)/shard_map/ppermute | solution.py:70
  125.9 4.4 %collective-permute-start.60 = (f32[4,2,16,1024]{3,2,1,0:T(8,128)S(1)}, f32[4,2,16,1024]{3,2,1,0:T(8,128)S(1)}, u32[]{:S(2)}, u32[]{:S(2)}) collective-permute-start(f32[4,2,16,1024]{3,2,1,0:T(8,128)S(1)} %maximum_select_fusion.3.z0), channel_id=1, source_target_pairs={{0,4},{1,5},{2,6},{3,7},{4,0},{5,1},{6,2},{7,3},{8,12},{9,13},{10,... | collective-permute-start | bytes 1572872 | tf_op jit(solution)/shard_map/ppermute | solution.py:70
  130.3 4.8 %collective-permute-start.61 = (f32[4,2,16,1024]{3,2,1,0:T(8,128)S(1)}, f32[4,2,16,1024]{3,2,1,0:T(8,128)S(1)}, u32[]{:S(2)}, u32[]{:S(2)}) collective-permute-start(f32[4,2,16,1024]{3,2,1,0:T(8,128)S(1)} %maximum_select_fusion.3.z0), channel_id=1, source_target_pairs={{0,6},{1,7},{2,4},{3,5},{4,2},{5,3},{6,0},{7,1},{8,14},{9,15},{10,... | collective-permute-start | bytes 1572872 | tf_op jit(solution)/shard_map/ppermute | solution.py:70
  137.4 4.1 %collective-permute-start.19 = (f32[8,128]{1,0:T(8,128)S(1)}, f32[8,128]{1,0:T(8,128)S(1)}, u32[]{:S(2)}, u32[]{:S(2)}) collective-permute-start(f32[8,128]{1,0:T(8,128)S(1)} %get-tuple-element.79.s0), channel_id=1, source_target_pairs={{0,65},{1,64},{2,67},{3,66},{4,69},{5,68},{6,71},{7,70},{8,73},{9,... | collective-permute-start | bytes 12296 | tf_op jit(solution)/shard_map/ppermute | solution.py:70
  142.8 4.3 %collective-permute-start.33 = (f32[2,16,1024]{2,1,0:T(8,128)S(1)}, f32[2,16,1024]{2,1,0:T(8,128)S(1)}, u32[]{:S(2)}, u32[]{:S(2)}) collective-permute-start(f32[2,16,1024]{2,1,0:T(8,128)S(1)} %get-tuple-element.82), channel_id=1, source_target_pairs={{0,1},{1,64},{2,3},{3,66},{4,5},{5,68},{6,7},{7,70},{8,9},{9,72},{... | collective-permute-start | bytes 393224 | tf_op jit(solution)/shard_map/ppermute | solution.py:70
  151.8 5.1 %shard_map.52 = (f32[288,1024]{1,0:T(8,128)S(1)}, f32[288,1024]{1,0:T(8,128)S(1)}, f32[8,128]{1,0:T(8,128)S(1)}) custom-call(s32[8]{0:T(128)S(1)} %stack.105.ids_ref, f32[288,1024]{1,0:T(8,128)S(1)} %get-tuple-element.77.x_ref, f32[288,1024]{1,0:T(8,128)S(1)} %get-tuple-element.78.g_ref, f32[8,128]{1,0:T(8,128)S(1)} %get-tuple-element.79.s0, ...), custom_call_target="tpu_custom_call" | custom-call | tf_op jit(solution)/shard_map/pallas_call | solution.py:41
  156.8 4.6 %collective-permute-start.35 = (f32[8,128]{1,0:T(8,128)S(1)}, f32[8,128]{1,0:T(8,128)S(1)}, u32[]{:S(2)}, u32[]{:S(2)}) collective-permute-start(f32[8,128]{1,0:T(8,128)S(1)} %get-tuple-element.88.s0), channel_id=1, source_target_pairs={{0,1},{1,0},{2,3},{3,2},{4,5},{5,4},{6,7},{7,6},{8,9},{9,8},{10,11... | collective-permute-start | bytes 12296 | tf_op jit(solution)/shard_map/ppermute | solution.py:70
  165.3 2.6 %shard_map.53 = (f32[288,1024]{1,0:T(8,128)S(1)}, f32[288,1024]{1,0:T(8,128)S(1)}, f32[8,128]{1,0:T(8,128)S(1)}) custom-call(s32[8]{0:T(128)S(1)} %stack.105.ids_ref, f32[288,1024]{1,0:T(8,128)S(1)} %get-tuple-element.86.x_ref, f32[288,1024]{1,0:T(8,128)S(1)} %get-tuple-element.87.g_ref, f32[8,128]{1,0:T(8,128)S(1)} %get-tuple-element.88.s0, ...), custom_call_target="tpu_custom_call" | custom-call | tf_op jit(solution)/shard_map/pallas_call | solution.py:41
  172.4 5.1 %shard_map.54 = (f32[288,1024]{1,0:T(8,128)S(1)}, f32[288,1024]{1,0:T(8,128)S(1)}, f32[8,128]{1,0:T(8,128)S(1)}) custom-call(s32[8]{0:T(128)S(1)} %stack.105.ids_ref, f32[288,1024]{1,0:T(8,128)S(1)} %get-tuple-element.89.x_ref, f32[288,1024]{1,0:T(8,128)S(1)} %get-tuple-element.90.g_ref, f32[8,128]{1,0:T(8,128)S(1)} %get-tuple-element.91.s0, ...), custom_call_target="tpu_custom_call" | custom-call | tf_op jit(solution)/shard_map/pallas_call | solution.py:41
  181.8 2.6 %shard_map.55 = (f32[288,1024]{1,0:T(8,128)S(1)}, f32[288,1024]{1,0:T(8,128)S(1)}, f32[8,128]{1,0:T(8,128)S(1)}) custom-call(s32[8]{0:T(128)S(1)} %stack.105.ids_ref, f32[288,1024]{1,0:T(8,128)S(1)} %get-tuple-element.92.x_ref, f32[288,1024]{1,0:T(8,128)S(1)} %get-tuple-element.93.g_ref, f32[8,128]{1,0:T(8,128)S(1)} %get-tuple-element.94.s0, ...), custom_call_target="tpu_custom_call" | custom-call | tf_op jit(solution)/shard_map/pallas_call | solution.py:41
  188.8 5.1 %shard_map.56 = (f32[288,1024]{1,0:T(8,128)S(1)}, f32[64,1024]{1,0:T(8,128)S(1)}, f32[288,1024]{1,0:T(8,128)S(1)}, f32[8,128]{1,0:T(8,128)S(1)}) custom-call(s32[8]{0:T(128)S(1)} %stack.105.ids_ref, f32[288,1024]{1,0:T(8,128)S(1)} %get-tuple-element.95.x_ref, f32[288,1024]{1,0:T(8,128)S(1)} %get-tuple-element.96.g_ref, f32[8,128]{1,0:T(8,128)S(1)} %get-tuple-element.97.s0, ...), custom_call_target="tpu_custom_call" | custom-call | tf_op jit(solution)/shard_map/pallas_call | solution.py:41
  206.5 2.6 %shard_map.57 = (f32[288,1024]{1,0:T(8,128)S(1)}, f32[288,1024]{1,0:T(8,128)S(1)}, f32[8,128]{1,0:T(8,128)S(1)}) custom-call(s32[8]{0:T(128)S(1)} %stack.105.ids_ref, f32[288,1024]{1,0:T(8,128)S(1)} %get-tuple-element.99.x_ref, f32[288,1024]{1,0:T(8,128)S(1)} %get-tuple-element.100.g_ref, f32[8,128]{1,0:T(8,128)S(1)} %get-tuple-element.101.s0, ...), custom_call_target="tpu_custom_call" | custom-call | tf_op jit(solution)/shard_map/pallas_call | solution.py:41
  213.5 5.1 %shard_map.59 = (f32[288,1024]{1,0:T(8,128)S(1)}, f32[288,1024]{1,0:T(8,128)S(1)}, f32[8,128]{1,0:T(8,128)S(1)}) custom-call(s32[8]{0:T(128)S(1)} %stack.105.ids_ref, f32[288,1024]{1,0:T(8,128)S(1)} %get-tuple-element.102.x_ref, f32[288,1024]{1,0:T(8,128)S(1)} %get-tuple-element.103.g_ref, f32[8,128]{1,0:T(8,128)S(1)} %get-tuple-element.104.s0, ...), custom_call_target="tpu_custom_call" | custom-call | tf_op jit(solution)/shard_map/pallas_call | solution.py:41
  229.7 5.1 %shard_map.61 = (f32[288,1024]{1,0:T(8,128)S(1)}, f32[288,1024]{1,0:T(8,128)S(1)}, f32[8,128]{1,0:T(8,128)S(1)}) custom-call(s32[8]{0:T(128)S(1)} %stack.105.ids_ref, f32[288,1024]{1,0:T(8,128)S(1)} %get-tuple-element.113.x_ref, f32[288,1024]{1,0:T(8,128)S(1)} %get-tuple-element.114.g_ref, f32[8,128]{1,0:T(8,128)S(1)} %get-tuple-element.115.s0, ...), custom_call_target="tpu_custom_call" | custom-call | tf_op jit(solution)/shard_map/pallas_call | solution.py:41
  245.9 4.3 %shard_map.63 = (f32[288,1024]{1,0:T(8,128)}, f32[64,1024]{1,0:T(8,128)S(1)}) custom-call(s32[8]{0:T(128)S(1)} %stack.105.ids_ref, f32[288,1024]{1,0:T(8,128)S(1)} %get-tuple-element.119.x_ref, f32[288,1024]{1,0:T(8,128)S(1)} %get-tuple-element.120.g_ref, f32[8,128]{1,0:T(8,128)S(1)} %get-tuple-element.121.s0, f32[8,128]{1,0:T(8,128)S(1)} %collective-permute-done.73.s1, ...), custom_call_target="tpu_custom_call" | custom-call | tf_op jit(solution)/shard_map/pallas_call | solution.py:41
  (171 shorter events, 119.4 us)
Async XLA Ops:
  9.5 11.3 %collective-permute-start = (f32[64,1024]{1,0:T(8,128)S(1)}, f32[64,1024]{1,0:T(8,128)S(1)}, u32[]{:S(2)}, u32[]{:S(2)}) collective-permute-start(f32[64,1024]{1,0:T(8,128)S(1)} %copy-done.1), channel_id=1, source_target_pairs={{0,8},{2,10},{4,12},{6,14},{8,0},{10,2},{12,4},{14,6},{16,24},{18,... | collective-permute-start | bytes 786440 | tf_op jit(solution)/shard_map/ppermute | solution.py:70
  15.3 10.9 %collective-permute-start.7 = (f32[56,1024]{1,0:T(8,128)S(1)}, f32[56,1024]{1,0:T(8,128)S(1)}, u32[]{:S(2)}, u32[]{:S(2)}) collective-permute-start(f32[56,1024]{1,0:T(8,128)S(1)} %get-tuple-element.69), channel_id=1, source_target_pairs={{0,2},{1,3},{2,0},{3,1},{4,6},{5,7},{6,4},{7,5},{8,10},{9,11},{10,... | collective-permute-start | bytes 688136 | tf_op jit(solution)/shard_map/ppermute | solution.py:70
  17.3 11.6 %collective-permute-start.8 = (f32[56,1024]{1,0:T(8,128)S(1)}, f32[56,1024]{1,0:T(8,128)S(1)}, u32[]{:S(2)}, u32[]{:S(2)}) collective-permute-start(f32[56,1024]{1,0:T(8,128)S(1)} %get-tuple-element.70), channel_id=1, source_target_pairs={{0,4},{1,5},{2,6},{3,7},{4,0},{5,1},{6,2},{7,3},{8,12},{9,13},{10,... | collective-permute-start | bytes 688136 | tf_op jit(solution)/shard_map/ppermute | solution.py:70
  20.8 10.5 %collective-permute-start.9 = (f32[56,1024]{1,0:T(8,128)S(1)}, f32[56,1024]{1,0:T(8,128)S(1)}, u32[]{:S(2)}, u32[]{:S(2)}) collective-permute-start(f32[56,1024]{1,0:T(8,128)S(1)} %get-tuple-element.71), channel_id=1, source_target_pairs={{0,6},{1,7},{2,4},{3,5},{4,2},{5,3},{6,0},{7,1},{8,14},{9,15},{10,... | collective-permute-start | bytes 688136 | tf_op jit(solution)/shard_map/ppermute | solution.py:70
  20.9 36.5 %collective-permute-start.2 = (f32[2,64,1024]{2,1,0:T(8,128)S(1)}, f32[2,64,1024]{2,1,0:T(8,128)S(1)}, u32[]{:S(2)}, u32[]{:S(2)}) collective-permute-start(f32[2,64,1024]{2,1,0:T(8,128)S(1)} %maximum_select_fusion.1), channel_id=1, source_target_pairs={{0,32},{2,34},{4,36},{6,38},{8,40},{10,42},{12,44},{14,46},{16,48}... | collective-permute-start | bytes 1572872 | tf_op jit(solution)/shard_map/ppermute | solution.py:70
  23.6 36.0 %collective-permute-start.3 = (f32[2,64,1024]{2,1,0:T(8,128)S(1)}, f32[2,64,1024]{2,1,0:T(8,128)S(1)}, u32[]{:S(2)}, u32[]{:S(2)}) collective-permute-start(f32[2,64,1024]{2,1,0:T(8,128)S(1)} %maximum_select_fusion.1), channel_id=1, source_target_pairs={{0,16},{2,18},{4,20},{6,22},{8,24},{10,26},{12,28},{14,30},{16,0},... | collective-permute-start | bytes 1572872 | tf_op jit(solution)/shard_map/ppermute | solution.py:70
  32.1 10.7 %collective-permute-start.21 = (bf16[16,1024]{1,0:T(8,128)(2,1)S(1)}, bf16[16,1024]{1,0:T(8,128)(2,1)S(1)}, u32[]{:S(2)}, u32[]{:S(2)}) collective-permute-start(bf16[16,1024]{1,0:T(8,128)(2,1)S(1)} %get-tuple-element.80), channel_id=1, source_target_pairs={{0,4},{1,5},{2,6},{3,7},{4,0},{5,1},{6,2},{7,3},{8,12},{9,13},{10,... | collective-permute-start | bytes 98312 | tf_op jit(solution)/shard_map/ppermute | solution.py:70
  33.5 13.5 %collective-permute-start.22 = (bf16[16,1024]{1,0:T(8,128)(2,1)S(1)}, bf16[16,1024]{1,0:T(8,128)(2,1)S(1)}, u32[]{:S(2)}, u32[]{:S(2)}) collective-permute-start(bf16[16,1024]{1,0:T(8,128)(2,1)S(1)} %get-tuple-element.80), channel_id=1, source_target_pairs={{0,6},{1,7},{2,4},{3,5},{4,2},{5,3},{6,0},{7,1},{8,14},{9,15},{10,... | collective-permute-start | bytes 98312 | tf_op jit(solution)/shard_map/ppermute | solution.py:70
  36.8 24.1 %collective-permute-start.4 = (f32[2,64,1024]{2,1,0:T(8,128)S(1)}, f32[2,64,1024]{2,1,0:T(8,128)S(1)}, u32[]{:S(2)}, u32[]{:S(2)}) collective-permute-start(f32[2,64,1024]{2,1,0:T(8,128)S(1)} %maximum_select_fusion.1), channel_id=1, source_target_pairs={{0,48},{2,50},{4,52},{6,54},{8,56},{10,58},{12,60},{14,62},{16,32}... | collective-permute-start | bytes 1572872 | tf_op jit(solution)/shard_map/ppermute | solution.py:70
  42.8 8.4 %collective-permute-start.10 = (f32[2,16,1024]{2,1,0:T(8,128)S(1)}, f32[2,16,1024]{2,1,0:T(8,128)S(1)}, u32[]{:S(2)}, u32[]{:S(2)}) collective-permute-start(f32[2,16,1024]{2,1,0:T(8,128)S(1)} %get-tuple-element.105), channel_id=1, source_target_pairs={{0,8},{2,10},{4,12},{6,14},{8,0},{10,2},{12,4},{14,6},{16,24},{18,... | collective-permute-start | bytes 393224 | tf_op jit(solution)/shard_map/ppermute | solution.py:70
  47.0 6.6 %collective-permute-start.23 = (bf16[4,16,1024]{2,1,0:T(8,128)(2,1)S(1)}, bf16[4,16,1024]{2,1,0:T(8,128)(2,1)S(1)}, u32[]{:S(2)}, u32[]{:S(2)}) collective-permute-start(bf16[4,16,1024]{2,1,0:T(8,128)(2,1)S(1)} %pad_maximum_fusion.2), channel_id=1, source_target_pairs={{0,8},{1,9},{2,10},{3,11},{4,12},{5,13},{6,14},{7,15},{8,0},{9,1},... | collective-permute-start | bytes 393224 | tf_op jit(solution)/shard_map/ppermute | solution.py:70
  53.6 8.8 %collective-permute-start.25 = (bf16[4,16,1024]{2,1,0:T(8,128)(2,1)S(1)}, bf16[4,16,1024]{2,1,0:T(8,128)(2,1)S(1)}, u32[]{:S(2)}, u32[]{:S(2)}) collective-permute-start(bf16[4,16,1024]{2,1,0:T(8,128)(2,1)S(1)} %pad_maximum_fusion.2), channel_id=1, source_target_pairs={{0,72},{1,73},{2,74},{3,75},{4,76},{5,77},{6,78},{7,79},{8,64},{9,... | collective-permute-start | bytes 393224 | tf_op jit(solution)/shard_map/ppermute | solution.py:70
  56.1 11.6 %collective-permute-start.11 = (f32[2,2,16,1024]{3,2,1,0:T(8,128)S(1)}, f32[2,2,16,1024]{3,2,1,0:T(8,128)S(1)}, u32[]{:S(2)}, u32[]{:S(2)}) collective-permute-start(f32[2,2,16,1024]{3,2,1,0:T(8,128)S(1)} %maximum_select_fusion.4), channel_id=1, source_target_pairs={{0,32},{2,34},{4,36},{6,38},{8,40},{10,42},{12,44},{14,46},{16,48}... | collective-permute-start | bytes 786440 | tf_op jit(solution)/shard_map/ppermute | solution.py:70
  57.4 15.0 %collective-permute-start.12 = (f32[2,2,16,1024]{3,2,1,0:T(8,128)S(1)}, f32[2,2,16,1024]{3,2,1,0:T(8,128)S(1)}, u32[]{:S(2)}, u32[]{:S(2)}) collective-permute-start(f32[2,2,16,1024]{3,2,1,0:T(8,128)S(1)} %maximum_select_fusion.4), channel_id=1, source_target_pairs={{0,16},{2,18},{4,20},{6,22},{8,24},{10,26},{12,28},{14,30},{16,0},... | collective-permute-start | bytes 786440 | tf_op jit(solution)/shard_map/ppermute | solution.py:70
  59.6 12.8 %collective-permute-start.13 = (f32[2,2,16,1024]{3,2,1,0:T(8,128)S(1)}, f32[2,2,16,1024]{3,2,1,0:T(8,128)S(1)}, u32[]{:S(2)}, u32[]{:S(2)}) collective-permute-start(f32[2,2,16,1024]{3,2,1,0:T(8,128)S(1)} %maximum_select_fusion.4), channel_id=1, source_target_pairs={{0,48},{2,50},{4,52},{6,54},{8,56},{10,58},{12,60},{14,62},{16,32}... | collective-permute-start | bytes 786440 | tf_op jit(solution)/shard_map/ppermute | solution.py:70
  63.7 20.4 %collective-permute-start.26 = (bf16[16,16,1024]{2,1,0:T(8,128)(2,1)S(1)}, bf16[16,16,1024]{2,1,0:T(8,128)(2,1)S(1)}, u32[]{:S(2)}, u32[]{:S(2)}) collective-permute-start(bf16[16,16,1024]{2,1,0:T(8,128)(2,1)S(1)} %constant_dynamic-update-slice_fusion.y0), channel_id=1, source_target_pairs={{0,16},{1,17},{2,18},{3,19},{4,20},{5,21},{6,22},{7,23},{8,24},{9,... | collective-permute-start | bytes 1572872 | tf_op jit(solution)/shard_map/ppermute | solution.py:70
  67.6 20.6 %collective-permute-start.27 = (bf16[16,16,1024]{2,1,0:T(8,128)(2,1)S(1)}, bf16[16,16,1024]{2,1,0:T(8,128)(2,1)S(1)}, u32[]{:S(2)}, u32[]{:S(2)}) collective-permute-start(bf16[16,16,1024]{2,1,0:T(8,128)(2,1)S(1)} %constant_dynamic-update-slice_fusion.y0), channel_id=1, source_target_pairs={{0,32},{1,33},{2,34},{3,35},{4,36},{5,37},{6,38},{7,39},{8,40},{9,... | collective-permute-start | bytes 1572872 | tf_op jit(solution)/shard_map/ppermute | solution.py:70
  67.7 26.4 %collective-permute-start.28 = (bf16[16,16,1024]{2,1,0:T(8,128)(2,1)S(1)}, bf16[16,16,1024]{2,1,0:T(8,128)(2,1)S(1)}, u32[]{:S(2)}, u32[]{:S(2)}) collective-permute-start(bf16[16,16,1024]{2,1,0:T(8,128)(2,1)S(1)} %constant_dynamic-update-slice_fusion.y0), channel_id=1, source_target_pairs={{0,48},{1,49},{2,50},{3,51},{4,52},{5,53},{6,54},{7,55},{8,56},{9,... | collective-permute-start | bytes 1572872 | tf_op jit(solution)/shard_map/ppermute | solution.py:70
  94.9 56.9 %collective-permute-start.29 = (bf16[1024,1024]{1,0:T(8,128)(2,1)S(1)}, bf16[1024,1024]{1,0:T(8,128)(2,1)S(1)}, u32[]{:S(2)}, u32[]{:S(2)}) collective-permute-start(bf16[1024,1024]{1,0:T(8,128)(2,1)S(1)} %shard_map.50.mine_ref), channel_id=1, source_target_pairs={{0,1},{1,0},{2,3},{3,2},{4,5},{5,4},{6,7},{7,6},{8,9},{9,8},{10,11... | collective-permute-start | bytes 6291464 | tf_op jit(solution)/shard_map/ppermute | solution.py:70
  100.9 8.4 %collective-permute-start.55 = (f32[2,16,1024]{2,1,0:T(8,128)S(1)}, f32[2,16,1024]{2,1,0:T(8,128)S(1)}, u32[]{:S(2)}, u32[]{:S(2)}) collective-permute-start(f32[2,16,1024]{2,1,0:T(8,128)S(1)} %collective-permute-done.54), channel_id=1, source_target_pairs={{0,8},{2,10},{4,12},{6,14},{8,0},{10,2},{12,4},{14,6},{16,24},{18,... | collective-permute-start | bytes 393224 | tf_op jit(solution)/shard_map/ppermute | solution.py:70
  109.3 8.3 %collective-permute-start.57 = (f32[2,2,16,1024]{3,2,1,0:T(8,128)S(1)}, f32[2,2,16,1024]{3,2,1,0:T(8,128)S(1)}, u32[]{:S(2)}, u32[]{:S(2)}) collective-permute-start(f32[2,2,16,1024]{3,2,1,0:T(8,128)S(1)} %maximum_select_fusion.5), channel_id=1, source_target_pairs={{0,16},{2,18},{4,20},{6,22},{8,24},{10,26},{12,28},{14,30},{16,0},... | collective-permute-start | bytes 786440 | tf_op jit(solution)/shard_map/ppermute | solution.py:70
  111.2 6.3 %collective-permute-start.58 = (f32[2,2,16,1024]{3,2,1,0:T(8,128)S(1)}, f32[2,2,16,1024]{3,2,1,0:T(8,128)S(1)}, u32[]{:S(2)}, u32[]{:S(2)}) collective-permute-start(f32[2,2,16,1024]{3,2,1,0:T(8,128)S(1)} %maximum_select_fusion.5), channel_id=1, source_target_pairs={{0,48},{2,50},{4,52},{6,54},{8,56},{10,58},{12,60},{14,62},{16,32}... | collective-permute-start | bytes 786440 | tf_op jit(solution)/shard_map/ppermute | solution.py:70
  112.5 7.0 %collective-permute-start.56 = (f32[2,2,16,1024]{3,2,1,0:T(8,128)S(1)}, f32[2,2,16,1024]{3,2,1,0:T(8,128)S(1)}, u32[]{:S(2)}, u32[]{:S(2)}) collective-permute-start(f32[2,2,16,1024]{3,2,1,0:T(8,128)S(1)} %maximum_select_fusion.5), channel_id=1, source_target_pairs={{0,32},{2,34},{4,36},{6,38},{8,40},{10,42},{12,44},{14,46},{16,48}... | collective-permute-start | bytes 786440 | tf_op jit(solution)/shard_map/ppermute | solution.py:70
  113.8 12.1 %collective-permute-start.30 = (f32[4,2,16,1024]{3,2,1,0:T(8,128)S(1)}, f32[4,2,16,1024]{3,2,1,0:T(8,128)S(1)}, u32[]{:S(2)}, u32[]{:S(2)}) collective-permute-start(f32[4,2,16,1024]{3,2,1,0:T(8,128)S(1)} %maximum_select_fusion.2.z0), channel_id=1, source_target_pairs={{0,2},{1,3},{2,0},{3,1},{4,6},{5,7},{6,4},{7,5},{8,10},{9,11},{10,... | collective-permute-start | bytes 1572872 | tf_op jit(solution)/shard_map/ppermute | solution.py:70
  117.5 12.8 %collective-permute-start.31 = (f32[4,2,16,1024]{3,2,1,0:T(8,128)S(1)}, f32[4,2,16,1024]{3,2,1,0:T(8,128)S(1)}, u32[]{:S(2)}, u32[]{:S(2)}) collective-permute-start(f32[4,2,16,1024]{3,2,1,0:T(8,128)S(1)} %maximum_select_fusion.2.z0), channel_id=1, source_target_pairs={{0,4},{1,5},{2,6},{3,7},{4,0},{5,1},{6,2},{7,3},{8,12},{9,13},{10,... | collective-permute-start | bytes 1572872 | tf_op jit(solution)/shard_map/ppermute | solution.py:70
  117.5 19.8 %collective-permute-start.32 = (f32[4,2,16,1024]{3,2,1,0:T(8,128)S(1)}, f32[4,2,16,1024]{3,2,1,0:T(8,128)S(1)}, u32[]{:S(2)}, u32[]{:S(2)}) collective-permute-start(f32[4,2,16,1024]{3,2,1,0:T(8,128)S(1)} %maximum_select_fusion.2.z0), channel_id=1, source_target_pairs={{0,6},{1,7},{2,4},{3,5},{4,2},{5,3},{6,0},{7,1},{8,14},{9,15},{10,... | collective-permute-start | bytes 1572872 | tf_op jit(solution)/shard_map/ppermute | solution.py:70
  125.9 70.0 %collective-permute-start.59 = (f32[4,2,16,1024]{3,2,1,0:T(8,128)S(1)}, f32[4,2,16,1024]{3,2,1,0:T(8,128)S(1)}, u32[]{:S(2)}, u32[]{:S(2)}) collective-permute-start(f32[4,2,16,1024]{3,2,1,0:T(8,128)S(1)} %maximum_select_fusion.3.z0), channel_id=1, source_target_pairs={{0,2},{1,3},{2,0},{3,1},{4,6},{5,7},{6,4},{7,5},{8,10},{9,11},{10,... | collective-permute-start | bytes 1572872 | tf_op jit(solution)/shard_map/ppermute | solution.py:70
  125.9 70.0 %collective-permute-start.60 = (f32[4,2,16,1024]{3,2,1,0:T(8,128)S(1)}, f32[4,2,16,1024]{3,2,1,0:T(8,128)S(1)}, u32[]{:S(2)}, u32[]{:S(2)}) collective-permute-start(f32[4,2,16,1024]{3,2,1,0:T(8,128)S(1)} %maximum_select_fusion.3.z0), channel_id=1, source_target_pairs={{0,4},{1,5},{2,6},{3,7},{4,0},{5,1},{6,2},{7,3},{8,12},{9,13},{10,... | collective-permute-start | bytes 1572872 | tf_op jit(solution)/shard_map/ppermute | solution.py:70
  130.3 65.6 %collective-permute-start.61 = (f32[4,2,16,1024]{3,2,1,0:T(8,128)S(1)}, f32[4,2,16,1024]{3,2,1,0:T(8,128)S(1)}, u32[]{:S(2)}, u32[]{:S(2)}) collective-permute-start(f32[4,2,16,1024]{3,2,1,0:T(8,128)S(1)} %maximum_select_fusion.3.z0), channel_id=1, source_target_pairs={{0,6},{1,7},{2,4},{3,5},{4,2},{5,3},{6,0},{7,1},{8,14},{9,15},{10,... | collective-permute-start | bytes 1572872 | tf_op jit(solution)/shard_map/ppermute | solution.py:70
  193.8 58.4 %collective-permute-start.47 = (f32[64,1024]{1,0:T(8,128)S(1)}, f32[64,1024]{1,0:T(8,128)S(1)}, u32[]{:S(2)}, u32[]{:S(2)}) collective-permute-start(f32[64,1024]{1,0:T(8,128)S(1)} %get-tuple-element.98), channel_id=1, source_target_pairs={{0,1},{2,3},{4,5},{6,7},{8,9},{10,11},{12,13},{14,15},{16,17},{18,... | collective-permute-start | bytes 786440 | tf_op jit(solution)/shard_map/ppermute | solution.py:70
  196.7 16.8 %collective-permute-start.62 = (f32[2,16,1024]{2,1,0:T(8,128)S(1)}, f32[2,16,1024]{2,1,0:T(8,128)S(1)}, u32[]{:S(2)}, u32[]{:S(2)}) collective-permute-start(f32[2,16,1024]{2,1,0:T(8,128)S(1)} %get-tuple-element.107), channel_id=1, source_target_pairs={{0,1},{1,64},{2,3},{3,66},{4,5},{5,68},{6,7},{7,70},{8,9},{9,72},{... | collective-permute-start | bytes 393224 | tf_op jit(solution)/shard_map/ppermute | solution.py:70
  198.0 15.5 %collective-permute-start.63 = (f32[2,16,1024]{2,1,0:T(8,128)S(1)}, f32[2,16,1024]{2,1,0:T(8,128)S(1)}, u32[]{:S(2)}, u32[]{:S(2)}) collective-permute-start(f32[2,16,1024]{2,1,0:T(8,128)S(1)} %get-tuple-element.109), channel_id=1, source_target_pairs={{1,0},{3,2},{5,4},{7,6},{9,8},{11,10},{13,12},{15,14},{17,16},{19,... | collective-permute-start | bytes 393224 | tf_op jit(solution)/shard_map/ppermute | solution.py:70
  (47 other events, 160.2 us)

commit v7 on v6

--- a/solution.py
+++ b/solution.py
@@ -86,7 +86,7 @@
     return rule
 
 
-def gram_kernel(order_ref, ids_ref, a_ref, s0_ref, s1_ref, own_ref, send_ref, acc, level_ref):
+def gram_kernel(ids_ref, a_ref, s0_ref, s1_ref, own_ref, send_ref, acc, level_ref):
     n = pl.program_id(0)
     rows, det = s0_ref.shape
     my_rows = pl.ds(pl.multiple_of(ids_ref[1] * rows, rows), rows)
@@ -151,31 +151,31 @@
                     ref[k, 3 * part + half : 3 * part + 8, :] = cover[half:8]
 
 
-def gram_products(order, ids, projector, measured):
+def gram_products(ids, projector, measured):
     _, pixels, det = projector.shape
     rows = measured.shape[2]
     part = rows // QUARTERS
     shape = (QUARTERS, 3 * part + 8, pixels)
-    out = pl.BlockSpec(shape, lambda n, o, s: (0, 0, 0))
+    out = pl.BlockSpec(shape, lambda n, s: (0, 0, 0))
     projector = pltpu.with_memory_space_constraint(projector, pltpu.HBM)
     measured = pltpu.with_memory_space_constraint(measured, pltpu.HBM)
     return pl.pallas_call(
         gram_kernel,
         out_shape=(jax.ShapeDtypeStruct(shape, F32),) * 2,
         grid_spec=pltpu.PrefetchScalarGridSpec(
-            num_scalar_prefetch=2,
+            num_scalar_prefetch=1,
             grid=(2,),
             in_specs=[
-                pl.BlockSpec((None, pixels, det), lambda n, o, s: (o[n], 0, 0)),
-                pl.BlockSpec((None, None, rows, det), lambda n, o, s: (0, o[n], 0, 0)),
-                pl.BlockSpec((None, None, rows, det), lambda n, o, s: (1, o[n], 0, 0)),
+                pl.BlockSpec((None, pixels, det), lambda n, s: (s[8 + n], 0, 0)),
+                pl.BlockSpec((None, None, rows, det), lambda n, s: (0, s[8 + n], 0, 0)),
+                pl.BlockSpec((None, None, rows, det), lambda n, s: (1, s[8 + n], 0, 0)),
             ],
             out_specs=(out, out),
             scratch_shapes=[pltpu.VMEM((3 * rows + 16, pixels), F32), pltpu.VMEM((FRAMES, rows, RY), F32)],
         ),
         compiler_params=params(24),
         name="gram_products",
-    )(order, ids, projector, measured, measured)
+    )(ids, projector, measured, measured)
 
 
 def chip_sum_kernel(ids_ref, own_ref, got_ref, *outs):
@@ -345,6 +345,7 @@
     height = inner + 2 * HALO
     first = (2 * tm + c) * inner - HALO
     ids = jnp.stack([first, slab, z, c, keeper.astype(jnp.int32), y, h, tm])
+    ids = jnp.concatenate([ids, view_order])
 
     def pair_of(unit):
         across = move(unit, flip(dh=1), keeps)
@@ -364,7 +365,7 @@
         high = move(lax.slice_in_dim(array, 0, HALO, axis=dim), strip_step(-1))
         return jnp.concatenate([low, array, high], axis=dim)
 
-    own, send = gram_products(view_order, ids, projector, sinogram)
+    own, send = gram_products(ids, projector, sinogram)
     passed = move(send, flip(dc=1))
     warm_pair = pair_of(after(warm_volume, send))
     block = (own.shape[1:], F32)
@@ -394,20 +395,14 @@
 
     strip = strip_of(pair_of(b_unit))
     quarters = along_z(strip)
-    later = move(after(b_unit, strip), flip(dc=1), lambda d: not keeps(d))
-    later = along_z(strip_of(pair_of(later)))
 
     big = ((height, pixels), F32)
     small = ((8, RY), F32)
     flux = pltpu.VMEM((height, RY), F32)
 
     def everyone(sums):
-        return [
-            sums,
-            move(sums, flip(dc=1)),
-            move(sums, flip(dtm=1)),
-            move(sums, flip(dtm=1, dc=1)),
-        ]
+        flips = (flip(dc=1), flip(dtm=1), flip(dtm=1, dc=1))
+        return [sums] + [move(sums, f) for f in flips]
 
     x = widen(strip_of(after(warm_pair, terms[0])).reshape(inner, pixels), 0)
     x = after(x, strip)
@@ -438,6 +433,8 @@
                 )
                 other = move(mine, flip(dc=1))
                 b_wide[0] = b_rows(quarters)
+                later = move(after(b_unit, sums), flip(dc=1), lambda d: not keeps(d))
+                later = along_z(strip_of(pair_of(later)))
             if frame == 0 and sweep == 2:
                 b_wide[1] = b_rows([after(later[0], x)] + later[1:])
             last = sweep == SWEEPS - 1

time: 256 us -> 256 us (level)
  no operation moved by 1% of the time
where the time goes in v7:
time: 256 us; the launch traced here: 254 us
  starting transfers between devices  122 us (48%)
  waiting for transfers between devices  69.2 us (27%)
  Pallas kernels  60 us (23%)
    ppermute x77, starting transfers between devices, move(): return lax.ppermute(array, AXES, pairs)  122 us
    ppermute x77, waiting for transfers between devices, move(): return lax.ppermute(array, AXES, pairs)  69.2 us
    pallas_call x18, Pallas kernels, call(): pl.pallas_call(kernel, out_shape=tuple((pltpu.VMEM(shape, dtype) for shap...  51.3 us
    pallas_call x1, Pallas kernels, gram_products(): pl.pallas_call(gram_kernel, out_shape=(jax.ShapeDtypeStruct(shape, F32),)...  8.69 us
  transfers between devices with their start and end apart: 77, of which 42 were waited for; matrix products, arithmetic and copies ran while one was open for 0% of the time, Pallas kernels for 20%

profile of v7, /device:TPU:0, one launch (start us, length us, event | category | flops | bytes accessed | tf_op | source)
XLA Modules:
  0.0 254.2 jit_solution(13160842251949191669)
XLA Ops:
  0.7 8.7 %gram_products.1 = (f32[4,56,1024]{2,1,0:T(8,128)S(1)}, f32[4,56,1024]{2,1,0:T(8,128)S(1)}) custom-call(s32[10]{0:T(128)S(1)} %concatenate.28.ids_ref, bf16[2,1024,2560]{2,1,0:T(8,128)(2,1)} %a_ref.1, bf16[2,2,64,2560]{3,2,1,0:T(8,128)(2,1)} %s1_ref.1, bf16[2,2,64,2560]{3,2,1,0:T(8,128)(2,1)} %s1_ref.1), custom_call_target="tpu_custom_call" | custom-call | tf_op jit(solution)/shard_map/gram_products/pallas_call | solution.py:162
  9.5 5.0 %collective-permute-start = (f32[64,1024]{1,0:T(8,128)S(1)}, f32[64,1024]{1,0:T(8,128)S(1)}, u32[]{:S(2)}, u32[]{:S(2)}) collective-permute-start(f32[64,1024]{1,0:T(8,128)S(1)} %copy-done), channel_id=1, source_target_pairs={{0,8},{2,10},{4,12},{6,14},{8,0},{10,2},{12,4},{14,6},{16,24},{18,... | collective-permute-start | bytes 786440 | tf_op jit(solution)/shard_map/ppermute | solution.py:70
  17.2 3.6 %collective-permute-start.8 = (f32[56,1024]{1,0:T(8,128)S(1)}, f32[56,1024]{1,0:T(8,128)S(1)}, u32[]{:S(2)}, u32[]{:S(2)}) collective-permute-start(f32[56,1024]{1,0:T(8,128)S(1)} %get-tuple-element.70), channel_id=1, source_target_pairs={{0,4},{1,5},{2,6},{3,7},{4,0},{5,1},{6,2},{7,3},{8,12},{9,13},{10,... | collective-permute-start | bytes 688136 | tf_op jit(solution)/shard_map/ppermute | solution.py:70
  20.9 2.7 %collective-permute-start.2 = (f32[2,64,1024]{2,1,0:T(8,128)S(1)}, f32[2,64,1024]{2,1,0:T(8,128)S(1)}, u32[]{:S(2)}, u32[]{:S(2)}) collective-permute-start(f32[2,64,1024]{2,1,0:T(8,128)S(1)} %maximum_select_fusion.1), channel_id=1, source_target_pairs={{0,32},{2,34},{4,36},{6,38},{8,40},{10,42},{12,44},{14,46},{16,48}... | collective-permute-start | bytes 1572872 | tf_op jit(solution)/shard_map/ppermute | solution.py:70
  26.2 2.7 %collective-permute-done.8.a2 = f32[56,1024]{1,0:T(8,128)S(1)} collective-permute-done((f32[56,1024]{1,0:T(8,128)S(1)}, f32[56,1024]{1,0:T(8,128)S(1)}, u32[]{:S(2)}, u32[]{:S(2)}) %collective-permute-start.8) | collective-permute-done | bytes 229408 | tf_op jit(solution)/shard_map/ppermute | solution.py:70
  33.5 3.3 %collective-permute-start.22 = (bf16[16,1024]{1,0:T(8,128)(2,1)S(1)}, bf16[16,1024]{1,0:T(8,128)(2,1)S(1)}, u32[]{:S(2)}, u32[]{:S(2)}) collective-permute-start(bf16[16,1024]{1,0:T(8,128)(2,1)S(1)} %get-tuple-element.80), channel_id=1, source_target_pairs={{0,6},{1,7},{2,4},{3,5},{4,2},{5,3},{6,0},{7,1},{8,14},{9,15},{10,... | collective-permute-start | bytes 98312 | tf_op jit(solution)/shard_map/ppermute | solution.py:70
  36.8 6.0 %collective-permute-start.4 = (f32[2,64,1024]{2,1,0:T(8,128)S(1)}, f32[2,64,1024]{2,1,0:T(8,128)S(1)}, u32[]{:S(2)}, u32[]{:S(2)}) collective-permute-start(f32[2,64,1024]{2,1,0:T(8,128)S(1)} %maximum_select_fusion.1), channel_id=1, source_target_pairs={{0,48},{2,50},{4,52},{6,54},{8,56},{10,58},{12,60},{14,62},{16,32}... | collective-permute-start | bytes 1572872 | tf_op jit(solution)/shard_map/ppermute | solution.py:70
  42.7 4.2 %collective-permute-start.10 = (f32[2,16,1024]{2,1,0:T(8,128)S(1)}, f32[2,16,1024]{2,1,0:T(8,128)S(1)}, u32[]{:S(2)}, u32[]{:S(2)}) collective-permute-start(f32[2,16,1024]{2,1,0:T(8,128)S(1)} %get-tuple-element.105), channel_id=1, source_target_pairs={{0,8},{2,10},{4,12},{6,14},{8,0},{10,2},{12,4},{14,6},{16,24},{18,... | collective-permute-start | bytes 393224 | tf_op jit(solution)/shard_map/ppermute | solution.py:70
  48.3 2.8 %collective-permute-done.10 = f32[2,16,1024]{2,1,0:T(8,128)S(1)} collective-permute-done((f32[2,16,1024]{2,1,0:T(8,128)S(1)}, f32[2,16,1024]{2,1,0:T(8,128)S(1)}, u32[]{:S(2)}, u32[]{:S(2)}) %collective-permute-start.10) | collective-permute-done | bytes 131104 | tf_op jit(solution)/shard_map/ppermute | solution.py:70
  67.7 4.6 %collective-permute-start.28 = (bf16[16,16,1024]{2,1,0:T(8,128)(2,1)S(1)}, bf16[16,16,1024]{2,1,0:T(8,128)(2,1)S(1)}, u32[]{:S(2)}, u32[]{:S(2)}) collective-permute-start(bf16[16,16,1024]{2,1,0:T(8,128)(2,1)S(1)} %constant_dynamic-update-slice_fusion.y0), channel_id=1, source_target_pairs={{0,48},{1,49},{2,50},{3,51},{4,52},{5,53},{6,54},{7,55},{8,56},{9,... | collective-permute-start | bytes 1572872 | tf_op jit(solution)/shard_map/ppermute | solution.py:70
  74.9 2.7 %collective-permute-start.14 = (f32[8,128]{1,0:T(8,128)S(1)}, f32[8,128]{1,0:T(8,128)S(1)}, u32[]{:S(2)}, u32[]{:S(2)}) collective-permute-start(f32[8,128]{1,0:T(8,128)S(1)} %get-tuple-element.76.s0), channel_id=1, source_target_pairs={{0,1},{1,0},{2,3},{3,2},{4,5},{5,4},{6,7},{7,6},{8,9},{9,8},{10,11... | collective-permute-start | bytes 12296 | tf_op jit(solution)/shard_map/ppermute | solution.py:70
  81.5 2.6 %shard_map.49 = (f32[288,1024]{1,0:T(8,128)S(1)}, f32[288,1024]{1,0:T(8,128)S(1)}, f32[8,128]{1,0:T(8,128)S(1)}) custom-call(s32[10]{0:T(128)S(1)} %concatenate.28.ids_ref, f32[288,1024]{1,0:T(8,128)S(1)} %get-tuple-element.74.x_ref, f32[288,1024]{1,0:T(8,128)S(1)} %get-tuple-element.75.g_ref, f32[8,128]{1,0:T(8,128)S(1)} %get-tuple-element.76.s0, ...), custom_call_target="tpu_custom_call" | custom-call | tf_op jit(solution)/shard_map/pallas_call | solution.py:41
  84.2 4.1 %collective-permute-done.27.y2 = bf16[16,16,1024]{2,1,0:T(8,128)(2,1)S(1)} collective-permute-done((bf16[16,16,1024]{2,1,0:T(8,128)(2,1)S(1)}, bf16[16,16,1024]{2,1,0:T(8,128)(2,1)S(1)}, u32[]{:S(2)}, u32[]{:S(2)}) %collective-permute-start.27) | collective-permute-done | bytes 524320 | tf_op jit(solution)/shard_map/ppermute | solution.py:70
  88.2 5.9 %collective-permute-done.28.y3 = bf16[16,16,1024]{2,1,0:T(8,128)(2,1)S(1)} collective-permute-done((bf16[16,16,1024]{2,1,0:T(8,128)(2,1)S(1)}, bf16[16,16,1024]{2,1,0:T(8,128)(2,1)S(1)}, u32[]{:S(2)}, u32[]{:S(2)}) %collective-permute-start.28) | collective-permute-done | bytes 524320 | tf_op jit(solution)/shard_map/ppermute | solution.py:70
  100.9 4.4 %collective-permute-start.55 = (f32[2,16,1024]{2,1,0:T(8,128)S(1)}, f32[2,16,1024]{2,1,0:T(8,128)S(1)}, u32[]{:S(2)}, u32[]{:S(2)}) collective-permute-start(f32[2,16,1024]{2,1,0:T(8,128)S(1)} %collective-permute-done.54), channel_id=1, source_target_pairs={{0,8},{2,10},{4,12},{6,14},{8,0},{10,2},{12,4},{14,6},{16,24},{18,... | collective-permute-start | bytes 393224 | tf_op jit(solution)/shard_map/ppermute | solution.py:70
  105.3 3.9 %collective-permute-done.55 = f32[2,16,1024]{2,1,0:T(8,128)S(1)} collective-permute-done((f32[2,16,1024]{2,1,0:T(8,128)S(1)}, f32[2,16,1024]{2,1,0:T(8,128)S(1)}, u32[]{:S(2)}, u32[]{:S(2)}) %collective-permute-start.55) | collective-permute-done | bytes 131104 | tf_op jit(solution)/shard_map/ppermute | solution.py:70
  113.9 3.6 %collective-permute-done.57 = f32[2,2,16,1024]{3,2,1,0:T(8,128)S(1)} collective-permute-done((f32[2,2,16,1024]{3,2,1,0:T(8,128)S(1)}, f32[2,2,16,1024]{3,2,1,0:T(8,128)S(1)}, u32[]{:S(2)}, u32[]{:S(2)}) %collective-permute-start.57) | collective-permute-done | bytes 262176 | tf_op jit(solution)/shard_map/ppermute | solution.py:70
  122.3 3.6 %collective-permute-done.18.s2 = f32[8,128]{1,0:T(8,128)S(1)} collective-permute-done((f32[8,128]{1,0:T(8,128)S(1)}, f32[8,128]{1,0:T(8,128)S(1)}, u32[]{:S(2)}, u32[]{:S(2)}) %collective-permute-start.18) | collective-permute-done | bytes 4128 | tf_op jit(solution)/shard_map/ppermute | solution.py:70
  125.9 4.4 %collective-permute-start.60 = (f32[4,2,16,1024]{3,2,1,0:T(8,128)S(1)}, f32[4,2,16,1024]{3,2,1,0:T(8,128)S(1)}, u32[]{:S(2)}, u32[]{:S(2)}) collective-permute-start(f32[4,2,16,1024]{3,2,1,0:T(8,128)S(1)} %maximum_select_fusion.3.z0), channel_id=1, source_target_pairs={{0,4},{1,5},{2,6},{3,7},{4,0},{5,1},{6,2},{7,3},{8,12},{9,13},{10,... | collective-permute-start | bytes 1572872 | tf_op jit(solution)/shard_map/ppermute | solution.py:70
  130.3 4.8 %collective-permute-start.61 = (f32[4,2,16,1024]{3,2,1,0:T(8,128)S(1)}, f32[4,2,16,1024]{3,2,1,0:T(8,128)S(1)}, u32[]{:S(2)}, u32[]{:S(2)}) collective-permute-start(f32[4,2,16,1024]{3,2,1,0:T(8,128)S(1)} %maximum_select_fusion.3.z0), channel_id=1, source_target_pairs={{0,6},{1,7},{2,4},{3,5},{4,2},{5,3},{6,0},{7,1},{8,14},{9,15},{10,... | collective-permute-start | bytes 1572872 | tf_op jit(solution)/shard_map/ppermute | solution.py:70
  137.4 4.1 %collective-permute-start.19 = (f32[8,128]{1,0:T(8,128)S(1)}, f32[8,128]{1,0:T(8,128)S(1)}, u32[]{:S(2)}, u32[]{:S(2)}) collective-permute-start(f32[8,128]{1,0:T(8,128)S(1)} %get-tuple-element.79.s0), channel_id=1, source_target_pairs={{0,65},{1,64},{2,67},{3,66},{4,69},{5,68},{6,71},{7,70},{8,73},{9,... | collective-permute-start | bytes 12296 | tf_op jit(solution)/shard_map/ppermute | solution.py:70
  142.8 4.3 %collective-permute-start.33 = (f32[2,16,1024]{2,1,0:T(8,128)S(1)}, f32[2,16,1024]{2,1,0:T(8,128)S(1)}, u32[]{:S(2)}, u32[]{:S(2)}) collective-permute-start(f32[2,16,1024]{2,1,0:T(8,128)S(1)} %get-tuple-element.82), channel_id=1, source_target_pairs={{0,1},{1,64},{2,3},{3,66},{4,5},{5,68},{6,7},{7,70},{8,9},{9,72},{... | collective-permute-start | bytes 393224 | tf_op jit(solution)/shard_map/ppermute | solution.py:70
  151.8 5.1 %shard_map.52 = (f32[288,1024]{1,0:T(8,128)S(1)}, f32[288,1024]{1,0:T(8,128)S(1)}, f32[8,128]{1,0:T(8,128)S(1)}) custom-call(s32[10]{0:T(128)S(1)} %concatenate.28.ids_ref, f32[288,1024]{1,0:T(8,128)S(1)} %get-tuple-element.77.x_ref, f32[288,1024]{1,0:T(8,128)S(1)} %get-tuple-element.78.g_ref, f32[8,128]{1,0:T(8,128)S(1)} %get-tuple-element.79.s0, ...), custom_call_target="tpu_custom_call" | custom-call | tf_op jit(solution)/shard_map/pallas_call | solution.py:41
  156.8 4.6 %collective-permute-start.35 = (f32[8,128]{1,0:T(8,128)S(1)}, f32[8,128]{1,0:T(8,128)S(1)}, u32[]{:S(2)}, u32[]{:S(2)}) collective-permute-start(f32[8,128]{1,0:T(8,128)S(1)} %get-tuple-element.88.s0), channel_id=1, source_target_pairs={{0,1},{1,0},{2,3},{3,2},{4,5},{5,4},{6,7},{7,6},{8,9},{9,8},{10,11... | collective-permute-start | bytes 12296 | tf_op jit(solution)/shard_map/ppermute | solution.py:70
  165.3 2.6 %shard_map.53 = (f32[288,1024]{1,0:T(8,128)S(1)}, f32[288,1024]{1,0:T(8,128)S(1)}, f32[8,128]{1,0:T(8,128)S(1)}) custom-call(s32[10]{0:T(128)S(1)} %concatenate.28.ids_ref, f32[288,1024]{1,0:T(8,128)S(1)} %get-tuple-element.86.x_ref, f32[288,1024]{1,0:T(8,128)S(1)} %get-tuple-element.87.g_ref, f32[8,128]{1,0:T(8,128)S(1)} %get-tuple-element.88.s0, ...), custom_call_target="tpu_custom_call" | custom-call | tf_op jit(solution)/shard_map/pallas_call | solution.py:41
  172.4 5.1 %shard_map.54 = (f32[288,1024]{1,0:T(8,128)S(1)}, f32[288,1024]{1,0:T(8,128)S(1)}, f32[8,128]{1,0:T(8,128)S(1)}) custom-call(s32[10]{0:T(128)S(1)} %concatenate.28.ids_ref, f32[288,1024]{1,0:T(8,128)S(1)} %get-tuple-element.89.x_ref, f32[288,1024]{1,0:T(8,128)S(1)} %get-tuple-element.90.g_ref, f32[8,128]{1,0:T(8,128)S(1)} %get-tuple-element.91.s0, ...), custom_call_target="tpu_custom_call" | custom-call | tf_op jit(solution)/shard_map/pallas_call | solution.py:41
  181.8 2.6 %shard_map.55 = (f32[288,1024]{1,0:T(8,128)S(1)}, f32[288,1024]{1,0:T(8,128)S(1)}, f32[8,128]{1,0:T(8,128)S(1)}) custom-call(s32[10]{0:T(128)S(1)} %concatenate.28.ids_ref, f32[288,1024]{1,0:T(8,128)S(1)} %get-tuple-element.92.x_ref, f32[288,1024]{1,0:T(8,128)S(1)} %get-tuple-element.93.g_ref, f32[8,128]{1,0:T(8,128)S(1)} %get-tuple-element.94.s0, ...), custom_call_target="tpu_custom_call" | custom-call | tf_op jit(solution)/shard_map/pallas_call | solution.py:41
  188.7 5.1 %shard_map.56 = (f32[288,1024]{1,0:T(8,128)S(1)}, f32[64,1024]{1,0:T(8,128)S(1)}, f32[288,1024]{1,0:T(8,128)S(1)}, f32[8,128]{1,0:T(8,128)S(1)}) custom-call(s32[10]{0:T(128)S(1)} %concatenate.28.ids_ref, f32[288,1024]{1,0:T(8,128)S(1)} %get-tuple-element.95.x_ref, f32[288,1024]{1,0:T(8,128)S(1)} %get-tuple-element.96.g_ref, ...), custom_call_target="tpu_custom_call" | custom-call | tf_op jit(solution)/shard_map/pallas_call | solution.py:41
  206.4 2.6 %shard_map.57 = (f32[288,1024]{1,0:T(8,128)S(1)}, f32[288,1024]{1,0:T(8,128)S(1)}, f32[8,128]{1,0:T(8,128)S(1)}) custom-call(s32[10]{0:T(128)S(1)} %concatenate.28.ids_ref, f32[288,1024]{1,0:T(8,128)S(1)} %get-tuple-element.99.x_ref, f32[288,1024]{1,0:T(8,128)S(1)} %get-tuple-element.100.g_ref, f32[8,128]{1,0:T(8,128)S(1)} %get-tuple-element.101.s0, ...), custom_call_target="tpu_custom_call" | custom-call | tf_op jit(solution)/shard_map/pallas_call | solution.py:41
  213.5 5.1 %shard_map.59 = (f32[288,1024]{1,0:T(8,128)S(1)}, f32[288,1024]{1,0:T(8,128)S(1)}, f32[8,128]{1,0:T(8,128)S(1)}) custom-call(s32[10]{0:T(128)S(1)} %concatenate.28.ids_ref, f32[288,1024]{1,0:T(8,128)S(1)} %get-tuple-element.102.x_ref, f32[288,1024]{1,0:T(8,128)S(1)} %get-tuple-element.103.g_ref, f32[8,128]{1,0:T(8,128)S(1)} %get-tuple-element.104.s0, ...), custom_call_target="tpu_custom_call" | custom-call | tf_op jit(solution)/shard_map/pallas_call | solution.py:41
  229.7 5.1 %shard_map.61 = (f32[288,1024]{1,0:T(8,128)S(1)}, f32[288,1024]{1,0:T(8,128)S(1)}, f32[8,128]{1,0:T(8,128)S(1)}) custom-call(s32[10]{0:T(128)S(1)} %concatenate.28.ids_ref, f32[288,1024]{1,0:T(8,128)S(1)} %get-tuple-element.113.x_ref, f32[288,1024]{1,0:T(8,128)S(1)} %get-tuple-element.114.g_ref, f32[8,128]{1,0:T(8,128)S(1)} %get-tuple-element.115.s0, ...), custom_call_target="tpu_custom_call" | custom-call | tf_op jit(solution)/shard_map/pallas_call | solution.py:41
  245.8 4.3 %shard_map.63 = (f32[288,1024]{1,0:T(8,128)}, f32[64,1024]{1,0:T(8,128)S(1)}) custom-call(s32[10]{0:T(128)S(1)} %concatenate.28.ids_ref, f32[288,1024]{1,0:T(8,128)S(1)} %get-tuple-element.119.x_ref, f32[288,1024]{1,0:T(8,128)S(1)} %get-tuple-element.120.g_ref, f32[8,128]{1,0:T(8,128)S(1)} %get-tuple-element.121.s0, ...), custom_call_target="tpu_custom_call" | custom-call | tf_op jit(solution)/shard_map/pallas_call | solution.py:41
  (169 shorter events, 119.4 us)
Async XLA Ops:
  9.5 11.3 %collective-permute-start = (f32[64,1024]{1,0:T(8,128)S(1)}, f32[64,1024]{1,0:T(8,128)S(1)}, u32[]{:S(2)}, u32[]{:S(2)}) collective-permute-start(f32[64,1024]{1,0:T(8,128)S(1)} %copy-done), channel_id=1, source_target_pairs={{0,8},{2,10},{4,12},{6,14},{8,0},{10,2},{12,4},{14,6},{16,24},{18,... | collective-permute-start | bytes 786440 | tf_op jit(solution)/shard_map/ppermute | solution.py:70
  15.2 10.9 %collective-permute-start.7 = (f32[56,1024]{1,0:T(8,128)S(1)}, f32[56,1024]{1,0:T(8,128)S(1)}, u32[]{:S(2)}, u32[]{:S(2)}) collective-permute-start(f32[56,1024]{1,0:T(8,128)S(1)} %get-tuple-element.69), channel_id=1, source_target_pairs={{0,2},{1,3},{2,0},{3,1},{4,6},{5,7},{6,4},{7,5},{8,10},{9,11},{10,... | collective-permute-start | bytes 688136 | tf_op jit(solution)/shard_map/ppermute | solution.py:70
  17.2 11.6 %collective-permute-start.8 = (f32[56,1024]{1,0:T(8,128)S(1)}, f32[56,1024]{1,0:T(8,128)S(1)}, u32[]{:S(2)}, u32[]{:S(2)}) collective-permute-start(f32[56,1024]{1,0:T(8,128)S(1)} %get-tuple-element.70), channel_id=1, source_target_pairs={{0,4},{1,5},{2,6},{3,7},{4,0},{5,1},{6,2},{7,3},{8,12},{9,13},{10,... | collective-permute-start | bytes 688136 | tf_op jit(solution)/shard_map/ppermute | solution.py:70
  20.8 10.5 %collective-permute-start.9 = (f32[56,1024]{1,0:T(8,128)S(1)}, f32[56,1024]{1,0:T(8,128)S(1)}, u32[]{:S(2)}, u32[]{:S(2)}) collective-permute-start(f32[56,1024]{1,0:T(8,128)S(1)} %get-tuple-element.71), channel_id=1, source_target_pairs={{0,6},{1,7},{2,4},{3,5},{4,2},{5,3},{6,0},{7,1},{8,14},{9,15},{10,... | collective-permute-start | bytes 688136 | tf_op jit(solution)/shard_map/ppermute | solution.py:70
  20.9 36.5 %collective-permute-start.2 = (f32[2,64,1024]{2,1,0:T(8,128)S(1)}, f32[2,64,1024]{2,1,0:T(8,128)S(1)}, u32[]{:S(2)}, u32[]{:S(2)}) collective-permute-start(f32[2,64,1024]{2,1,0:T(8,128)S(1)} %maximum_select_fusion.1), channel_id=1, source_target_pairs={{0,32},{2,34},{4,36},{6,38},{8,40},{10,42},{12,44},{14,46},{16,48}... | collective-permute-start | bytes 1572872 | tf_op jit(solution)/shard_map/ppermute | solution.py:70
  23.6 36.0 %collective-permute-start.3 = (f32[2,64,1024]{2,1,0:T(8,128)S(1)}, f32[2,64,1024]{2,1,0:T(8,128)S(1)}, u32[]{:S(2)}, u32[]{:S(2)}) collective-permute-start(f32[2,64,1024]{2,1,0:T(8,128)S(1)} %maximum_select_fusion.1), channel_id=1, source_target_pairs={{0,16},{2,18},{4,20},{6,22},{8,24},{10,26},{12,28},{14,30},{16,0},... | collective-permute-start | bytes 1572872 | tf_op jit(solution)/shard_map/ppermute | solution.py:70
  32.1 10.7 %collective-permute-start.21 = (bf16[16,1024]{1,0:T(8,128)(2,1)S(1)}, bf16[16,1024]{1,0:T(8,128)(2,1)S(1)}, u32[]{:S(2)}, u32[]{:S(2)}) collective-permute-start(bf16[16,1024]{1,0:T(8,128)(2,1)S(1)} %get-tuple-element.80), channel_id=1, source_target_pairs={{0,4},{1,5},{2,6},{3,7},{4,0},{5,1},{6,2},{7,3},{8,12},{9,13},{10,... | collective-permute-start | bytes 98312 | tf_op jit(solution)/shard_map/ppermute | solution.py:70
  33.5 13.5 %collective-permute-start.22 = (bf16[16,1024]{1,0:T(8,128)(2,1)S(1)}, bf16[16,1024]{1,0:T(8,128)(2,1)S(1)}, u32[]{:S(2)}, u32[]{:S(2)}) collective-permute-start(bf16[16,1024]{1,0:T(8,128)(2,1)S(1)} %get-tuple-element.80), channel_id=1, source_target_pairs={{0,6},{1,7},{2,4},{3,5},{4,2},{5,3},{6,0},{7,1},{8,14},{9,15},{10,... | collective-permute-start | bytes 98312 | tf_op jit(solution)/shard_map/ppermute | solution.py:70
  36.8 24.1 %collective-permute-start.4 = (f32[2,64,1024]{2,1,0:T(8,128)S(1)}, f32[2,64,1024]{2,1,0:T(8,128)S(1)}, u32[]{:S(2)}, u32[]{:S(2)}) collective-permute-start(f32[2,64,1024]{2,1,0:T(8,128)S(1)} %maximum_select_fusion.1), channel_id=1, source_target_pairs={{0,48},{2,50},{4,52},{6,54},{8,56},{10,58},{12,60},{14,62},{16,32}... | collective-permute-start | bytes 1572872 | tf_op jit(solution)/shard_map/ppermute | solution.py:70
  42.7 8.4 %collective-permute-start.10 = (f32[2,16,1024]{2,1,0:T(8,128)S(1)}, f32[2,16,1024]{2,1,0:T(8,128)S(1)}, u32[]{:S(2)}, u32[]{:S(2)}) collective-permute-start(f32[2,16,1024]{2,1,0:T(8,128)S(1)} %get-tuple-element.105), channel_id=1, source_target_pairs={{0,8},{2,10},{4,12},{6,14},{8,0},{10,2},{12,4},{14,6},{16,24},{18,... | collective-permute-start | bytes 393224 | tf_op jit(solution)/shard_map/ppermute | solution.py:70
  47.0 6.6 %collective-permute-start.23 = (bf16[4,16,1024]{2,1,0:T(8,128)(2,1)S(1)}, bf16[4,16,1024]{2,1,0:T(8,128)(2,1)S(1)}, u32[]{:S(2)}, u32[]{:S(2)}) collective-permute-start(bf16[4,16,1024]{2,1,0:T(8,128)(2,1)S(1)} %pad_maximum_fusion.2), channel_id=1, source_target_pairs={{0,8},{1,9},{2,10},{3,11},{4,12},{5,13},{6,14},{7,15},{8,0},{9,1},... | collective-permute-start | bytes 393224 | tf_op jit(solution)/shard_map/ppermute | solution.py:70
  53.6 8.8 %collective-permute-start.25 = (bf16[4,16,1024]{2,1,0:T(8,128)(2,1)S(1)}, bf16[4,16,1024]{2,1,0:T(8,128)(2,1)S(1)}, u32[]{:S(2)}, u32[]{:S(2)}) collective-permute-start(bf16[4,16,1024]{2,1,0:T(8,128)(2,1)S(1)} %pad_maximum_fusion.2), channel_id=1, source_target_pairs={{0,72},{1,73},{2,74},{3,75},{4,76},{5,77},{6,78},{7,79},{8,64},{9,... | collective-permute-start | bytes 393224 | tf_op jit(solution)/shard_map/ppermute | solution.py:70
  56.1 11.6 %collective-permute-start.11 = (f32[2,2,16,1024]{3,2,1,0:T(8,128)S(1)}, f32[2,2,16,1024]{3,2,1,0:T(8,128)S(1)}, u32[]{:S(2)}, u32[]{:S(2)}) collective-permute-start(f32[2,2,16,1024]{3,2,1,0:T(8,128)S(1)} %maximum_select_fusion.4), channel_id=1, source_target_pairs={{0,32},{2,34},{4,36},{6,38},{8,40},{10,42},{12,44},{14,46},{16,48}... | collective-permute-start | bytes 786440 | tf_op jit(solution)/shard_map/ppermute | solution.py:70
  57.4 15.0 %collective-permute-start.12 = (f32[2,2,16,1024]{3,2,1,0:T(8,128)S(1)}, f32[2,2,16,1024]{3,2,1,0:T(8,128)S(1)}, u32[]{:S(2)}, u32[]{:S(2)}) collective-permute-start(f32[2,2,16,1024]{3,2,1,0:T(8,128)S(1)} %maximum_select_fusion.4), channel_id=1, source_target_pairs={{0,16},{2,18},{4,20},{6,22},{8,24},{10,26},{12,28},{14,30},{16,0},... | collective-permute-start | bytes 786440 | tf_op jit(solution)/shard_map/ppermute | solution.py:70
  59.6 12.8 %collective-permute-start.13 = (f32[2,2,16,1024]{3,2,1,0:T(8,128)S(1)}, f32[2,2,16,1024]{3,2,1,0:T(8,128)S(1)}, u32[]{:S(2)}, u32[]{:S(2)}) collective-permute-start(f32[2,2,16,1024]{3,2,1,0:T(8,128)S(1)} %maximum_select_fusion.4), channel_id=1, source_target_pairs={{0,48},{2,50},{4,52},{6,54},{8,56},{10,58},{12,60},{14,62},{16,32}... | collective-permute-start | bytes 786440 | tf_op jit(solution)/shard_map/ppermute | solution.py:70
  63.7 20.4 %collective-permute-start.26 = (bf16[16,16,1024]{2,1,0:T(8,128)(2,1)S(1)}, bf16[16,16,1024]{2,1,0:T(8,128)(2,1)S(1)}, u32[]{:S(2)}, u32[]{:S(2)}) collective-permute-start(bf16[16,16,1024]{2,1,0:T(8,128)(2,1)S(1)} %constant_dynamic-update-slice_fusion.y0), channel_id=1, source_target_pairs={{0,16},{1,17},{2,18},{3,19},{4,20},{5,21},{6,22},{7,23},{8,24},{9,... | collective-permute-start | bytes 1572872 | tf_op jit(solution)/shard_map/ppermute | solution.py:70
  67.6 20.6 %collective-permute-start.27 = (bf16[16,16,1024]{2,1,0:T(8,128)(2,1)S(1)}, bf16[16,16,1024]{2,1,0:T(8,128)(2,1)S(1)}, u32[]{:S(2)}, u32[]{:S(2)}) collective-permute-start(bf16[16,16,1024]{2,1,0:T(8,128)(2,1)S(1)} %constant_dynamic-update-slice_fusion.y0), channel_id=1, source_target_pairs={{0,32},{1,33},{2,34},{3,35},{4,36},{5,37},{6,38},{7,39},{8,40},{9,... | collective-permute-start | bytes 1572872 | tf_op jit(solution)/shard_map/ppermute | solution.py:70
  67.7 26.4 %collective-permute-start.28 = (bf16[16,16,1024]{2,1,0:T(8,128)(2,1)S(1)}, bf16[16,16,1024]{2,1,0:T(8,128)(2,1)S(1)}, u32[]{:S(2)}, u32[]{:S(2)}) collective-permute-start(bf16[16,16,1024]{2,1,0:T(8,128)(2,1)S(1)} %constant_dynamic-update-slice_fusion.y0), channel_id=1, source_target_pairs={{0,48},{1,49},{2,50},{3,51},{4,52},{5,53},{6,54},{7,55},{8,56},{9,... | collective-permute-start | bytes 1572872 | tf_op jit(solution)/shard_map/ppermute | solution.py:70
  94.9 56.9 %collective-permute-start.29 = (bf16[1024,1024]{1,0:T(8,128)(2,1)S(1)}, bf16[1024,1024]{1,0:T(8,128)(2,1)S(1)}, u32[]{:S(2)}, u32[]{:S(2)}) collective-permute-start(bf16[1024,1024]{1,0:T(8,128)(2,1)S(1)} %shard_map.50.mine_ref), channel_id=1, source_target_pairs={{0,1},{1,0},{2,3},{3,2},{4,5},{5,4},{6,7},{7,6},{8,9},{9,8},{10,11... | collective-permute-start | bytes 6291464 | tf_op jit(solution)/shard_map/ppermute | solution.py:70
  100.9 8.4 %collective-permute-start.55 = (f32[2,16,1024]{2,1,0:T(8,128)S(1)}, f32[2,16,1024]{2,1,0:T(8,128)S(1)}, u32[]{:S(2)}, u32[]{:S(2)}) collective-permute-start(f32[2,16,1024]{2,1,0:T(8,128)S(1)} %collective-permute-done.54), channel_id=1, source_target_pairs={{0,8},{2,10},{4,12},{6,14},{8,0},{10,2},{12,4},{14,6},{16,24},{18,... | collective-permute-start | bytes 393224 | tf_op jit(solution)/shard_map/ppermute | solution.py:70
  109.2 8.3 %collective-permute-start.57 = (f32[2,2,16,1024]{3,2,1,0:T(8,128)S(1)}, f32[2,2,16,1024]{3,2,1,0:T(8,128)S(1)}, u32[]{:S(2)}, u32[]{:S(2)}) collective-permute-start(f32[2,2,16,1024]{3,2,1,0:T(8,128)S(1)} %maximum_select_fusion.5), channel_id=1, source_target_pairs={{0,16},{2,18},{4,20},{6,22},{8,24},{10,26},{12,28},{14,30},{16,0},... | collective-permute-start | bytes 786440 | tf_op jit(solution)/shard_map/ppermute | solution.py:70
  111.2 6.3 %collective-permute-start.58 = (f32[2,2,16,1024]{3,2,1,0:T(8,128)S(1)}, f32[2,2,16,1024]{3,2,1,0:T(8,128)S(1)}, u32[]{:S(2)}, u32[]{:S(2)}) collective-permute-start(f32[2,2,16,1024]{3,2,1,0:T(8,128)S(1)} %maximum_select_fusion.5), channel_id=1, source_target_pairs={{0,48},{2,50},{4,52},{6,54},{8,56},{10,58},{12,60},{14,62},{16,32}... | collective-permute-start | bytes 786440 | tf_op jit(solution)/shard_map/ppermute | solution.py:70
  112.5 7.0 %collective-permute-start.56 = (f32[2,2,16,1024]{3,2,1,0:T(8,128)S(1)}, f32[2,2,16,1024]{3,2,1,0:T(8,128)S(1)}, u32[]{:S(2)}, u32[]{:S(2)}) collective-permute-start(f32[2,2,16,1024]{3,2,1,0:T(8,128)S(1)} %maximum_select_fusion.5), channel_id=1, source_target_pairs={{0,32},{2,34},{4,36},{6,38},{8,40},{10,42},{12,44},{14,46},{16,48}... | collective-permute-start | bytes 786440 | tf_op jit(solution)/shard_map/ppermute | solution.py:70
  113.8 12.1 %collective-permute-start.30 = (f32[4,2,16,1024]{3,2,1,0:T(8,128)S(1)}, f32[4,2,16,1024]{3,2,1,0:T(8,128)S(1)}, u32[]{:S(2)}, u32[]{:S(2)}) collective-permute-start(f32[4,2,16,1024]{3,2,1,0:T(8,128)S(1)} %maximum_select_fusion.2.z0), channel_id=1, source_target_pairs={{0,2},{1,3},{2,0},{3,1},{4,6},{5,7},{6,4},{7,5},{8,10},{9,11},{10,... | collective-permute-start | bytes 1572872 | tf_op jit(solution)/shard_map/ppermute | solution.py:70
  117.5 12.8 %collective-permute-start.31 = (f32[4,2,16,1024]{3,2,1,0:T(8,128)S(1)}, f32[4,2,16,1024]{3,2,1,0:T(8,128)S(1)}, u32[]{:S(2)}, u32[]{:S(2)}) collective-permute-start(f32[4,2,16,1024]{3,2,1,0:T(8,128)S(1)} %maximum_select_fusion.2.z0), channel_id=1, source_target_pairs={{0,4},{1,5},{2,6},{3,7},{4,0},{5,1},{6,2},{7,3},{8,12},{9,13},{10,... | collective-permute-start | bytes 1572872 | tf_op jit(solution)/shard_map/ppermute | solution.py:70
  117.5 19.8 %collective-permute-start.32 = (f32[4,2,16,1024]{3,2,1,0:T(8,128)S(1)}, f32[4,2,16,1024]{3,2,1,0:T(8,128)S(1)}, u32[]{:S(2)}, u32[]{:S(2)}) collective-permute-start(f32[4,2,16,1024]{3,2,1,0:T(8,128)S(1)} %maximum_select_fusion.2.z0), channel_id=1, source_target_pairs={{0,6},{1,7},{2,4},{3,5},{4,2},{5,3},{6,0},{7,1},{8,14},{9,15},{10,... | collective-permute-start | bytes 1572872 | tf_op jit(solution)/shard_map/ppermute | solution.py:70
  125.9 70.0 %collective-permute-start.59 = (f32[4,2,16,1024]{3,2,1,0:T(8,128)S(1)}, f32[4,2,16,1024]{3,2,1,0:T(8,128)S(1)}, u32[]{:S(2)}, u32[]{:S(2)}) collective-permute-start(f32[4,2,16,1024]{3,2,1,0:T(8,128)S(1)} %maximum_select_fusion.3.z0), channel_id=1, source_target_pairs={{0,2},{1,3},{2,0},{3,1},{4,6},{5,7},{6,4},{7,5},{8,10},{9,11},{10,... | collective-permute-start | bytes 1572872 | tf_op jit(solution)/shard_map/ppermute | solution.py:70
  125.9 70.0 %collective-permute-start.60 = (f32[4,2,16,1024]{3,2,1,0:T(8,128)S(1)}, f32[4,2,16,1024]{3,2,1,0:T(8,128)S(1)}, u32[]{:S(2)}, u32[]{:S(2)}) collective-permute-start(f32[4,2,16,1024]{3,2,1,0:T(8,128)S(1)} %maximum_select_fusion.3.z0), channel_id=1, source_target_pairs={{0,4},{1,5},{2,6},{3,7},{4,0},{5,1},{6,2},{7,3},{8,12},{9,13},{10,... | collective-permute-start | bytes 1572872 | tf_op jit(solution)/shard_map/ppermute | solution.py:70
  130.3 65.6 %collective-permute-start.61 = (f32[4,2,16,1024]{3,2,1,0:T(8,128)S(1)}, f32[4,2,16,1024]{3,2,1,0:T(8,128)S(1)}, u32[]{:S(2)}, u32[]{:S(2)}) collective-permute-start(f32[4,2,16,1024]{3,2,1,0:T(8,128)S(1)} %maximum_select_fusion.3.z0), channel_id=1, source_target_pairs={{0,6},{1,7},{2,4},{3,5},{4,2},{5,3},{6,0},{7,1},{8,14},{9,15},{10,... | collective-permute-start | bytes 1572872 | tf_op jit(solution)/shard_map/ppermute | solution.py:70
  193.8 58.4 %collective-permute-start.47 = (f32[64,1024]{1,0:T(8,128)S(1)}, f32[64,1024]{1,0:T(8,128)S(1)}, u32[]{:S(2)}, u32[]{:S(2)}) collective-permute-start(f32[64,1024]{1,0:T(8,128)S(1)} %get-tuple-element.98), channel_id=1, source_target_pairs={{0,1},{2,3},{4,5},{6,7},{8,9},{10,11},{12,13},{14,15},{16,17},{18,... | collective-permute-start | bytes 786440 | tf_op jit(solution)/shard_map/ppermute | solution.py:70
  196.7 16.8 %collective-permute-start.62 = (f32[2,16,1024]{2,1,0:T(8,128)S(1)}, f32[2,16,1024]{2,1,0:T(8,128)S(1)}, u32[]{:S(2)}, u32[]{:S(2)}) collective-permute-start(f32[2,16,1024]{2,1,0:T(8,128)S(1)} %get-tuple-element.107), channel_id=1, source_target_pairs={{0,1},{1,64},{2,3},{3,66},{4,5},{5,68},{6,7},{7,70},{8,9},{9,72},{... | collective-permute-start | bytes 393224 | tf_op jit(solution)/shard_map/ppermute | solution.py:70
  198.0 15.5 %collective-permute-start.63 = (f32[2,16,1024]{2,1,0:T(8,128)S(1)}, f32[2,16,1024]{2,1,0:T(8,128)S(1)}, u32[]{:S(2)}, u32[]{:S(2)}) collective-permute-start(f32[2,16,1024]{2,1,0:T(8,128)S(1)} %get-tuple-element.109), channel_id=1, source_target_pairs={{1,0},{3,2},{5,4},{7,6},{9,8},{11,10},{13,12},{15,14},{17,16},{19,... | collective-permute-start | bytes 393224 | tf_op jit(solution)/shard_map/ppermute | solution.py:70
  (46 other events, 159.6 us)
